TPU v7x, 128 devices: a whole 4x4x4 slice. The times are simulated.
128 devices in a mesh: row: 16 (over y, z_lo, core), col: 8 (over x, z_hi).
Axes of the slice: x: 4, y: 4, z: 4 (z_hi: 2, z_lo: 2; z = z_hi * 2 + z_lo), core: 2. Of those that a mesh axis runs over, the one named last changes fastest.
Arguments:
- patches: bfloat16 [128, 128, 1280], P('row', 'col'), may hold values from -6 to 6
- norm_gain: float32 [1280], replicated, may hold values from 0.1 to 1.9
- query_weight: bfloat16 [1280, 1280], P(None, 'col'), may hold values from -12 to 12
- key_weight: bfloat16 [1280, 1280], P(None, 'col'), may hold values from -0.15625 to 0.15625
- value_weight: bfloat16 [1280, 1280], P(None, 'col'), may hold values from -0.15625 to 0.15625
- out_weight: bfloat16 [1280, 1280], replicated, may hold values from -0.15625 to 0.15625
- merge_gain: float32 [1280], replicated, may hold values from 0.1 to 1.9
- up_weight: bfloat16 [5120, 5120], P(None, 'col'), may hold values from -0.078125 to 0.078125
- up_bias: float32 [5120], P('col'), may hold values from -3 to 3
- down_weight: bfloat16 [5120, 8192], P('col'), may hold values from -0.078125 to 0.078125
- down_bias: float32 [8192], replicated, may hold values from -3 to 3
Outputs:
- merged_tokens: bfloat16 [4096, 8192], P(('row', 'col'))
All inputs are finite; a program needn't handle non-finite values.
Results may differ from a plain program's by a relative error of at most 0.018.
The roundings to bfloat16 on the way count: a program that leaves them out, or rounds other values in their place, can miss the bound.
Values may be sent and summed in bfloat16 or wider, within the bound.
No kernel may reach another device: no remote copies, remote signals or barrier semaphores. Data moves between devices by JAX's collectives and lax.ppermute only.
A program may use at most 128 MiB of HBM per device.

v0:
```python
import functools
import math

import jax
import jax.numpy as jnp
import numpy as np
from jax import lax
from jax.experimental import pallas as pl
from jax.experimental.pallas import tpu as pltpu
from jax.sharding import Mesh
from jax.sharding import PartitionSpec as P


HEAD_DIM = 80
EPSILON = 1e-06
AXES = ("y", "zl", "c", "x", "zh")
SIZES = (4, 2, 2, 4, 2)
BF = jnp.bfloat16
F32 = jnp.float32
QUERY_BLOCK = 512
LIMIT = 2.0**64


def pairs(move):
    result = []
    for place in np.ndindex(*SIZES):
        there = dict(zip(AXES, place))
        there.update(move(there))
        target = tuple(there[a] % n for a, n in zip(AXES, SIZES))
        result.append(
            (int(np.ravel_multi_index(place, SIZES)), int(np.ravel_multi_index(target, SIZES)))
        )
    return result


def shift(axis, step):
    return pairs(lambda d: {axis: d[axis] + step})


def send(value, perm):
    return lax.ppermute(value, AXES, perm)


def vmem():
    return pl.BlockSpec(memory_space=pltpu.VMEM)


def smem():
    return pl.BlockSpec(memory_space=pltpu.SMEM)


def call(kernel, outs, ins, scratch=(), flops=0, nbytes=0, exps=0):
    specs = [smem() if k == "s" else vmem() for k, _ in ins]
    return pl.pallas_call(
        kernel,
        out_shape=outs,
        in_specs=specs,
        out_specs=jax.tree.map(lambda _: vmem(), outs),
        scratch_shapes=list(scratch),
        cost_estimate=pl.CostEstimate(flops=flops, bytes_accessed=nbytes, transcendentals=exps),
        compiler_params=pltpu.CompilerParams(vmem_limit_bytes=58 * 2**20),
    )(*[a for _, a in ins])


def norm(values, gain):
    center = values - jnp.mean(values, axis=-1, keepdims=True)
    spread = jnp.mean(center * center, axis=-1, keepdims=True)
    return center * lax.rsqrt(spread + EPSILON) * gain


def project_kernel(c_ref, *refs):
    tiles, rest = refs[:9], refs[9:]
    gain_ref, wq, wk, wv, cos_ref, sin_ref, q_out, kv_out, other_out = rest
    mine = pl.multiple_of(c_ref[0] * HEAD_DIM, 16)
    others = pl.multiple_of((1 - c_ref[0]) * HEAD_DIM, 16)
    weight = jnp.concatenate(
        [w[pl.ds(o, HEAD_DIM), :] for o in (mine, others) for w in (wq, wk, wv)], axis=0
    )
    half = HEAD_DIM // 2
    scale = math.log2(math.e) / math.sqrt(HEAD_DIM)
    groups = [tiles[0:2], tiles[2:4], tiles[4:6], tiles[6:9]]
    for g, group in enumerate(groups):
        rows = jnp.concatenate([t[...] for t in group], axis=0).astype(F32)
        rows = norm(rows, gain_ref[...]).astype(BF)
        mapped = lax.dot_general(
            weight, rows, (((1,), (1,)), ((), ())), preferred_element_type=F32
        )
        at = slice(g * 256, (g + 1) * 256)
        cos, sin = cos_ref[:, at], sin_ref[:, at]

        def turn(u):
            first, second = u[:half], u[half:]
            return jnp.concatenate([first * cos - second * sin, second * cos + first * sin], axis=0)

        part = [mapped[k * HEAD_DIM : (k + 1) * HEAD_DIM] for k in range(6)]
        q_out[:, at] = (turn(part[0]) * scale).astype(BF)
        kv_out[:HEAD_DIM, at] = turn(part[1]).astype(BF)
        kv_out[HEAD_DIM:, at] = part[2].astype(BF)
        other_out[:HEAD_DIM, at] = (turn(part[3]) * scale).astype(BF)
        other_out[HEAD_DIM : 2 * HEAD_DIM, at] = turn(part[4]).astype(BF)
        other_out[2 * HEAD_DIM :, at] = part[5].astype(BF)


def split_rows(m):
    hi = m.astype(BF)
    rest = m - hi.astype(F32)
    mid = rest.astype(BF)
    low = (rest - mid.astype(F32)).astype(BF)
    pad = jnp.zeros((13, m.shape[1]), BF)
    return jnp.concatenate([-hi, -mid, -low, pad], axis=0)


def attend_chunks(chunks, q_ref, m_ref, o_ref, k_all, v_all, flag):
    keys = k_all.shape[0]
    queries = q_ref.shape[1]
    step = keys if keys <= 2048 else max(d for d in (2048, 1536, 1024) if keys % d == 0)
    turns = queries // (2 * QUERY_BLOCK)
    at = 0
    for ref in chunks:
        n = ref.shape[1]
        ones = jnp.ones((16, n), BF)
        k_all[at : at + n, :] = jnp.concatenate([ref[-2 * HEAD_DIM : -HEAD_DIM, :], ones], axis=0).T
        v_all[:, at : at + n] = jnp.concatenate([ref[-HEAD_DIM:, :], ones], axis=0)
        at += n
    flag[0] = 1

    def attempt(tries, carry):
        @pl.when(flag[0] == 1)
        def _():
            o_ref[...] = jnp.zeros_like(o_ref)

            def block(t, carry):
                rows = pl.ds(pl.multiple_of((t // turns) * step, step), step)
                for i in range(2):
                    col = (t % turns) * (2 * QUERY_BLOCK) + i * QUERY_BLOCK
                    cols = pl.ds(pl.multiple_of(col, QUERY_BLOCK), QUERY_BLOCK)
                    s = jnp.dot(k_all[rows, :], q_ref[:, cols], preferred_element_type=F32)
                    p = jnp.exp2(s).astype(BF)
                    o_ref[:, cols] += jnp.dot(v_all[:, rows], p, preferred_element_type=F32)
                return carry

            lax.fori_loop(0, keys // step * turns, block, 0)
            mass = o_ref[HEAD_DIM : HEAD_DIM + 8, :]
            bad = jnp.max(jnp.where(mass < LIMIT, 0.0, 1.0)) > 0.0
            flag[0] = jnp.where(jnp.logical_and(bad, tries == 0), 1, 0)

            @pl.when(flag[0] == 1)
            def _():
                m_ref[1:2, :] = jnp.zeros((1, queries), F32)

                def top_block(t, carry):
                    rows = pl.ds(pl.multiple_of((t // 8) * 512, 512), 512)
                    cols = pl.ds(pl.multiple_of((t % 8) * 256, 256), 256)
                    s = jnp.dot(k_all[rows, :], q_ref[:, cols], preferred_element_type=F32)
                    m_ref[1:2, cols] = jnp.maximum(
                        m_ref[1:2, cols], jnp.max(s, axis=0, keepdims=True)
                    )
                    return carry

                lax.fori_loop(0, keys // 512 * (queries // 256), top_block, 0)
                fresh = m_ref[0:1, :] + m_ref[1:2, :]
                m_ref[0:1, :] = fresh
                q_ref[HEAD_DIM:, :] = split_rows(fresh)

        return carry

    lax.fori_loop(0, 2, attempt, 0)


def first_kernel(own_q, swapped, kv_ref, q_out, start_out, m_ref, o_ref, q_ref, k_all, v_all, flag):
    n = own_q.shape[1]
    q_ref[:HEAD_DIM, :n] = own_q[...]
    q_ref[:HEAD_DIM, n:] = swapped[:HEAD_DIM, :]
    some = kv_ref[:HEAD_DIM, :512].T

    def start(i, carry):
        cols = pl.ds(pl.multiple_of(i * QUERY_BLOCK, QUERY_BLOCK), QUERY_BLOCK)
        s = jnp.dot(some, q_ref[:HEAD_DIM, cols], preferred_element_type=F32)
        m_ref[:, cols] = jnp.broadcast_to(jnp.max(s, axis=0, keepdims=True), (8, QUERY_BLOCK))
        return carry

    lax.fori_loop(0, 2 * n // QUERY_BLOCK, start, 0)
    q_ref[HEAD_DIM:, :] = split_rows(m_ref[0:1, :])
    q_out[...] = q_ref[...]
    start_out[...] = m_ref[...]
    attend_chunks([kv_ref], q_ref, m_ref, o_ref, k_all, v_all, flag)


def next_kernel(count, *refs):
    chunks, rest = refs[:count], refs[count:]
    q_in, m_in, m_ref, o_ref, q_ref, k_all, v_all, flag = rest
    q_ref[...] = q_in[...]
    m_ref[...] = m_in[...]
    attend_chunks(chunks, q_ref, m_ref, o_ref, k_all, v_all, flag)


def last_kernel(count, done, place, *refs):
    chunks, rest = refs[:count], refs[count:]
    q_in, m_in = rest[:2]
    tops, sums = rest[2 : 2 + done], rest[2 + done : 2 + 2 * done]
    own_ref, swap_ref, q_ref, m_ref, o_ref, k_all, v_all, flag = rest[2 + 2 * done :]
    q_ref[...] = q_in[...]
    m_ref[...] = m_in[...]
    attend_chunks(chunks, q_ref, m_ref, o_ref, k_all, v_all, flag)
    top = m_ref[0:1, :]
    for t in tops:
        top = jnp.maximum(top, t[0:1, :])
    total = o_ref[...] * jnp.exp2(m_ref[0:1, :] - top)
    for t, o in zip(tops, sums):
        total = total + o[...] * jnp.exp2(t[0:1, :] - top)
    half = total.shape[1] // 2
    for out_ref, lower in ((own_ref, 0), (swap_ref, half)):
        for s in range(half // 128):
            cols = slice(lower + s * 128, lower + (s + 1) * 128)
            mass = total[HEAD_DIM : HEAD_DIM + 1, cols]
            target = pl.ds(pl.multiple_of(place[s] * 128, 128), 128)
            out_ref[:, target] = (total[:HEAD_DIM, cols] / mass).astype(BF)


def merge_kernel(col_ref, c_ref, *refs):
    pieces, tiles, rest = refs[:9], refs[9:18], refs[18:]
    out_weight, gain_ref, up_weight, bias_ref = rest[:4]
    hidden_a, hidden_b, att_all, token_all, mixed_all, merged = rest[4:]
    starts = [0, 0, 0, 0, 0, 0, 0, 0, 80]
    slots = [0, 1, 2, 3, 4, 5, 6, 7, 7]
    c, x, zh = c_ref[0], c_ref[1], c_ref[2]
    for piece, tile, slot, lower in zip(pieces, tiles, slots, starts):
        for part in range(piece.shape[0] // 80):
            odd = (lower + part * 80) // 80
            spot = col_ref[slot] * 160 + (c if odd == 0 else 1 - c) * 80
            att_all[pl.ds(pl.multiple_of(spot, 16), 80), :] = piece[part * 80 : (part + 1) * 80, :]
        row = slot * 128 + (64 if lower else 0)
        token_all[row : row + tile.shape[0], :] = tile[...]
    width = out_weight.shape[1]

    def project(i, carry):
        spot = pl.ds(pl.multiple_of(i * 256, 256), 256)
        lhs = att_all[:, spot].T
        mixed_all[spot, :] = jnp.dot(lhs, out_weight[...], preferred_element_type=F32)
        return carry

    lax.fori_loop(0, 4, project, 0)
    r = lax.broadcasted_iota(jnp.int32, (128, 128), 0)
    t = lax.broadcasted_iota(jnp.int32, (128, 128), 1)
    a, b, u, w = r >> 6, (r >> 5) & 1, (r >> 3) & 3, r & 7
    pick = ((2 * u + a) * 16 + 2 * w + b == t).astype(BF)

    def settle(s, carry):
        spot = pl.ds(pl.multiple_of(col_ref[s] * 128, 128), 128)
        own = pl.ds(pl.multiple_of(s * 128, 128), 128)
        residual = token_all[own, :].astype(F32) + mixed_all[spot, :]
        normed = norm(residual, gain_ref[...]).astype(BF)
        ordered = jnp.dot(pick, normed, preferred_element_type=F32).astype(BF)
        for q in range(4):
            merged[q, pl.ds(pl.multiple_of(s * 32, 32), 32), :] = ordered[q * 32 : (q + 1) * 32]
        return carry

    lax.fori_loop(0, 8, settle, 0)
    z = bias_ref[...]
    for q in range(4):
        z = z + jnp.dot(
            merged[q], up_weight[q * width : (q + 1) * width, :], preferred_element_type=F32
        )
    hidden = (0.5 * z * (1.0 + lax.erf(z * (1.0 / math.sqrt(2.0))))).astype(BF)
    n = hidden.shape[0]
    rows = lax.broadcasted_iota(jnp.int32, (n, n), 0)
    lane = lax.broadcasted_iota(jnp.int32, (1, n), 1)
    col = jnp.zeros((1, n), jnp.int32)
    for s in range(8):
        col = jnp.where((lane >> 5) == s, col_ref[s], col)
    raster = ((lane >> 3) & 3) * 64 + col * 8 + (lane & 7)
    owner = raster >> 5
    ahead = ((owner >> 1) - x) & 3
    other_half = (owner & 1) ^ zh
    place_a = ahead * 64 + other_half * 32 + (raster & 31)
    place_b = other_half * 128 + ahead * 32 + (raster & 31)
    for place, out in ((place_a, hidden_a), (place_b, hidden_b)):
        out[...] = jnp.dot(
            (rows == place).astype(BF), hidden, preferred_element_type=F32
        ).astype(BF)


def spread(own, axis, across, dim, extras=()):
    forward, backward = shift(axis, 1), shift(axis, -1)
    half = own.shape[dim] // 2
    plus, minus, mirror = send(own, forward), send(own, backward), send(own, across)
    plus, minus, mirror, extras = lax.optimization_barrier((plus, minus, mirror, extras))
    two = send(plus, forward)
    mirror_plus = send(plus, across)
    mirror_minus = send(mirror, backward)
    far_low = send(lax.slice_in_dim(mirror_plus, 0, half, axis=dim), forward)
    far_high = send(lax.slice_in_dim(two, half, 2 * half, axis=dim), across)
    return [own, plus, minus, mirror, two, mirror_plus, mirror_minus, far_low, far_high], extras


def shards(
    patches,
    norm_gain,
    query_weight,
    key_weight,
    value_weight,
    out_weight,
    merge_gain,
    up_weight,
    up_bias,
    down_weight,
    down_bias,
):
    band_height, tile_width, model_width = patches.shape
    tile = band_height * tile_width
    band = tile * 8
    y, zl, c = lax.axis_index("y"), lax.axis_index("zl"), lax.axis_index("c")
    x, zh = lax.axis_index("x"), lax.axis_index("zh")
    row_index = (y * 2 + zl) * 2 + c
    sds = jax.ShapeDtypeStruct

    slot_x = jnp.stack([x, x - 1, x + 1, x, x + 2, x - 1, x + 1, x + 2]) % 4
    slot_z = jnp.stack([zh, zh, zh, 1 - zh, zh, 1 - zh, 1 - zh, 1 - zh])
    slot_col = (slot_x * 2 + slot_z).astype(jnp.int32)
    local = np.arange(tile)
    row_coord = (row_index * band_height + jnp.tile(local // tile_width, 8)).astype(F32)
    col_coord = (
        (slot_col[:, None] * tile_width + (local % tile_width)[None, :]).astype(F32).reshape(-1)
    )
    frequency = 1.0 / 10000.0 ** (
        jnp.arange(HEAD_DIM // 4, dtype=F32) * 2.0 / (HEAD_DIM // 2)
    )
    angles = jnp.concatenate(
        [frequency[:, None] * row_coord[None, :], frequency[:, None] * col_coord[None, :]], axis=0
    )
    cos, sin = jnp.cos(angles), jnp.sin(angles)

    mirror_x = pairs(lambda d: {"zh": 1 - d["zh"]})
    tokens = patches.reshape(tile, model_width)
    gains = [v.reshape(1, -1) for v in (norm_gain, merge_gain, up_bias)]
    tiles, (cos, sin, gains) = spread(tokens, "x", mirror_x, 0, (cos, sin, gains))
    q_own, kv_own, other = call(
        project_kernel,
        (sds((HEAD_DIM, band), BF), sds((2 * HEAD_DIM, band), BF), sds((3 * HEAD_DIM, band), BF)),
        [("s", c.reshape(1).astype(jnp.int32))]
        + [("v", t) for t in tiles]
        + [("v", gains[0])]
        + [("v", query_weight.T), ("v", key_weight.T), ("v", value_weight.T), ("v", cos), ("v", sin)],
        flops=2 * band * model_width * 480,
    )
    n = 2 * band
    swap = pairs(lambda d: {"c": 1 - d["c"]})
    mirror_y = pairs(lambda d: {"zl": 1 - d["zl"]})
    swapped = send(other, swap)
    kv = jnp.concatenate([kv_own, swapped[HEAD_DIM:]], axis=1)
    chunks, _ = spread(kv, "y", mirror_y, 1)
    groups = (chunks[1:4], chunks[4:7], chunks[7:])
    q_shape, m_shape, o_shape = sds((96, n), BF), sds((8, n), F32), sds((96, n), F32)

    def scratch(keys):
        return [
            pltpu.VMEM((96, n), BF),
            pltpu.VMEM((keys, 96), BF),
            pltpu.VMEM((96, keys), BF),
            pltpu.SMEM((1,), jnp.int32),
        ]

    work = lambda keys: dict(flops=2 * n * keys * 512, exps=n * keys, nbytes=4 * n * 96)
    q, start, top, part = call(
        first_kernel,
        (q_shape, m_shape, m_shape, o_shape),
        [("v", q_own), ("v", swapped), ("v", kv)],
        scratch(n),
        **work(n),
    )
    tops, parts = [top], [part]
    for chunks in groups[:-1]:
        keys = sum(t.shape[1] for t in chunks)
        top, part = call(
            functools.partial(next_kernel, len(chunks)),
            (m_shape, o_shape),
            [("v", t) for t in chunks] + [("v", q), ("v", start)],
            scratch(keys),
            **work(keys),
        )
        tops.append(top)
        parts.append(part)
    final = scratch(n)
    half_shape = sds((HEAD_DIM, band), BF)
    attended, partner = call(
        functools.partial(last_kernel, 2, len(tops)),
        (half_shape, half_shape),
        [("s", slot_col)] + [("v", t) for t in (*groups[-1], q, start, *tops, *parts)],
        [final[0], pltpu.VMEM((8, n), F32), pltpu.VMEM((96, n), F32), *final[1:]],
        **work(n),
    )
    attended = jnp.concatenate([attended, send(partner, swap)], axis=0)
    pieces, _ = spread(attended, "x", mirror_x, 0)
    hidden_a, hidden_b = call(
        merge_kernel,
        (sds((256, up_weight.shape[1]), BF),) * 2,
        [("s", slot_col), ("s", jnp.stack([c, x, zh]).astype(jnp.int32))]
        + [("v", t) for t in (*pieces, *tiles)]
        + [
            ("v", out_weight),
            ("v", gains[1]),
            ("v", up_weight),
            ("v", gains[2]),
        ],
        [
            pltpu.VMEM((model_width, band), BF),
            pltpu.VMEM((band, model_width), BF),
            pltpu.VMEM((band, model_width), F32),
            pltpu.VMEM((4, 256, model_width), BF),
        ],
        flops=2 * 256 * 5120 * 640 + 2 * band * model_width * model_width,
    )
    return scatter_output(hidden_a, hidden_b, down_weight, down_bias, mirror_x)


def ring(block, rows):
    forward, backward = shift("x", 1), shift("x", -1)
    half = block.shape[1] // 2
    part = lambda k: block[k * rows : (k + 1) * rows]
    ahead, behind, far = part(1), part(3), part(2)
    from_behind = send(far[:, :half], forward)
    from_ahead = send(far[:, half:], backward)
    add = lambda p, q: (p.astype(F32) + q.astype(F32)).astype(BF)
    onward = jnp.concatenate([add(ahead[:, :half], from_behind), ahead[:, half:]], axis=1)
    back = jnp.concatenate([behind[:, :half], add(behind[:, half:], from_ahead)], axis=1)
    got_behind, got_ahead = send(onward, forward), send(back, backward)
    return part(0).astype(F32) + got_behind.astype(F32) + got_ahead.astype(F32)


def scatter_output(hidden_a, hidden_b, down_weight, down_bias, mirror):
    split = 4608
    part_b = jnp.dot(
        hidden_b, down_weight[:, split:], preferred_element_type=F32
    ).astype(BF)
    give_b, hidden_a = lax.optimization_barrier((part_b[128:], hidden_a))
    got_b = send(give_b, mirror)
    part_a = jnp.dot(
        hidden_a, down_weight[:, :split], preferred_element_type=F32
    ).astype(BF)
    total_a = ring(part_a, 64)
    got_a = send(total_a[32:].astype(BF), mirror)
    block_b = (part_b[:128].astype(F32) + got_b.astype(F32)).astype(BF)
    total_b = ring(block_b, 32)
    total_a = total_a[:32] + got_a.astype(F32)
    return (jnp.concatenate([total_a, total_b], axis=1) + down_bias[None, :]).astype(BF)


def solution(mesh):
    fine = Mesh(mesh.devices.reshape(SIZES), AXES)
    row, col = ("y", "zl", "c"), ("x", "zh")
    placed = (
        P(row, col, None),
        P(),
        P(None, col),
        P(None, col),
        P(None, col),
        P(),
        P(),
        P(None, col),
        P(col),
        P(col, None),
        P(),
    )

    return jax.shard_map(
        shards, mesh=fine, in_specs=placed, out_specs=P(row + col, None), check_vma=False
    )
```

profile of v0, /device:TPU:0, one launch (start us, length us, event | category | flops | bytes accessed | tf_op | source)
XLA Modules:
  0.0 295.1 jit_solution(13277059147448896570)
XLA Ops:
  0.0 4.0 %collective-permute-start.2 = (bf16[128,1280]{1,0:T(8,128)(2,1)}, bf16[128,1280]{1,0:T(8,128)(2,1)S(1)}, u32[]{:S(2)}, u32[]{:S(2)}) collective-permute-start(bf16[128,1280]{1,0:T(8,128)(2,1)} %bitcast.20), channel_id=1, source_target_pairs={{0,1},{1,0},{2,3},{3,2},{4,5},{5,4},{6,7},{7,6},{8,9},{9,8},{10,11... | collective-permute-start | bytes 983048 | tf_op jit(solution)/shard_map/ppermute | solution.py:41
  4.0 2.8 collective-permute-start.1
  14.1 2.9 collective-permute-done.refs_1_.refs_10_
  17.3 3.2 %collective-permute-start.5 = (bf16[128,1280]{1,0:T(8,128)(2,1)S(1)}, bf16[128,1280]{1,0:T(8,128)(2,1)S(1)}, u32[]{:S(2)}, u32[]{:S(2)}) collective-permute-start(bf16[128,1280]{1,0:T(8,128)(2,1)S(1)} %collective-permute-done.2.refs_3_.refs_12_), channel_id=1, source_target_pairs={{0,6},{1,7},{2,0},{3,1},{4,2},{5,3},{6,4},{7,5},{8,14},{9,15},{10,... | collective-permute-start | bytes 983048 | tf_op jit(solution)/shard_map/ppermute | solution.py:41
  20.6 6.0 %collective-permute-done.4.refs_5_.refs_14_ = bf16[128,1280]{1,0:T(8,128)(2,1)S(1)} collective-permute-done((bf16[128,1280]{1,0:T(8,128)(2,1)S(1)}, bf16[128,1280]{1,0:T(8,128)(2,1)S(1)}, u32[]{:S(2)}, u32[]{:S(2)}) %collective-permute-start.4) | collective-permute-done | bytes 327712 | tf_op jit(solution)/shard_map/ppermute | solution.py:41
  26.7 3.6 %collective-permute-start.7 = (bf16[64,1280]{1,0:T(8,128)(2,1)S(1)}, bf16[64,1280]{1,0:T(8,128)(2,1)S(1)}, u32[]{:S(2)}, u32[]{:S(2)}) collective-permute-start(bf16[64,1280]{1,0:T(8,128)(2,1)S(1)} %slice.128), channel_id=1, source_target_pairs={{0,1},{1,0},{2,3},{3,2},{4,5},{5,4},{6,7},{7,6},{8,9},{9,8},{10,11... | collective-permute-start | bytes 491528 | tf_op jit(solution)/shard_map/ppermute | solution.py:41
  30.3 2.9 collective-permute-done.6.refs_7_.refs_16_
  34.3 5.5 %shard_map.127 = (bf16[80,1024]{1,0:T(8,128)(2,1)}, bf16[160,1024]{1,0:T(8,128)(2,1)}, bf16[240,1024]{1,0:T(8,128)(2,1)}) custom-call(s32[1]{0:T(128)} %bitcast.6.c_ref, bf16[128,1280]{1,0:T(8,128)(2,1)} %bitcast.23, bf16[128,1280]{1,0:T(8,128)(2,1)} %copy-done.16, bf16[128,1280]{1,0:T(8,128)(2,1)} %copy-done.15, bf16[128,1280]{1,0:T(8,128)(2,1)} %copy-done.14, ...), custom_call_target="tpu_custom_call" | custom-call | flops 1258291200 | tf_op jit(solution)/shard_map/pallas_call | solution.py:54
  44.5 3.0 %collective-permute-start.10 = (bf16[160,2048]{1,0:T(8,128)(2,1)S(1)}, bf16[160,2048]{1,0:T(8,128)(2,1)S(1)}, u32[]{:S(2)}, u32[]{:S(2)}) collective-permute-start(bf16[160,2048]{1,0:T(8,128)(2,1)S(1)} %pad_maximum_fusion.kv_ref), channel_id=1, source_target_pairs={{0,96},{1,97},{2,98},{3,99},{4,100},{5,101},{6,102},{7,103},{8,104... | collective-permute-start | bytes 1966088 | tf_op jit(solution)/shard_map/ppermute | solution.py:41
  47.5 19.3 %shard_map.128 = (bf16[96,2048]{1,0:T(8,128)(2,1)}, f32[8,2048]{1,0:T(8,128)}, f32[8,2048]{1,0:T(8,128)}, f32[96,2048]{1,0:T(8,128)}) custom-call(bf16[80,1024]{1,0:T(8,128)(2,1)} %get-tuple-element.45.own_q, bf16[240,1024]{1,0:T(8,128)(2,1)} %copy-done.1, bf16[160,2048]{1,0:T(8,128)(2,1)} %copy-done), custom_call_target="tpu_custom_call" | custom-call | flops 4294967296 | bytes 786432 | tf_op jit(solution)/shard_map/pallas_call | solution.py:54
  68.2 2.7 collective-permute-start.16
  70.9 48.5 %shard_map.129 = (f32[8,2048]{1,0:T(8,128)}, f32[96,2048]{1,0:T(8,128)}) custom-call(bf16[160,2048]{1,0:T(8,128)(2,1)} %copy-done.11, bf16[160,2048]{1,0:T(8,128)(2,1)} %copy-done.12, bf16[160,2048]{1,0:T(8,128)(2,1)} %copy-done.10, bf16[96,2048]{1,0:T(8,128)(2,1)} %get-tuple-element.46.refs_3_.refs_2_, f32[8,2048]{1,0:T(8,128)} %get-tuple-element.47.refs_4_.refs_3_), custom_call_target="tpu_custom_call" | custom-call | flops 12884901888 | bytes 786432 | tf_op jit(solution)/shard_map/pallas_call | solution.py:54
  122.5 48.5 %shard_map.130 = (f32[8,2048]{1,0:T(8,128)}, f32[96,2048]{1,0:T(8,128)}) custom-call(bf16[160,2048]{1,0:T(8,128)(2,1)} %copy-done.2, bf16[160,2048]{1,0:T(8,128)(2,1)} %copy-done.3, bf16[160,2048]{1,0:T(8,128)(2,1)} %copy-done.13, bf16[96,2048]{1,0:T(8,128)(2,1)} %get-tuple-element.46.refs_3_.refs_2_, f32[8,2048]{1,0:T(8,128)} %get-tuple-element.47.refs_4_.refs_3_), custom_call_target="tpu_custom_call" | custom-call | flops 12884901888 | bytes 786432 | tf_op jit(solution)/shard_map/pallas_call | solution.py:54
  171.8 18.7 %shard_map.131 = (bf16[80,1024]{1,0:T(8,128)(2,1)}, bf16[80,1024]{1,0:T(8,128)(2,1)}) custom-call(s32[8]{0:T(128)} %get-tuple-element.68.place.col_ref, bf16[160,1024]{1,0:T(8,128)(2,1)} %copy-done.23, bf16[160,1024]{1,0:T(8,128)(2,1)} %copy-done.22, bf16[96,2048]{1,0:T(8,128)(2,1)} %get-tuple-element.46.refs_3_.refs_2_, ...), custom_call_target="tpu_custom_call" | custom-call | flops 4294967296 | bytes 786432 | tf_op jit(solution)/shard_map/pallas_call | solution.py:54
  192.1 4.2 %collective-permute-start.20 = (bf16[160,1024]{1,0:T(8,128)(2,1)S(1)}, bf16[160,1024]{1,0:T(8,128)(2,1)S(1)}, u32[]{:S(2)}, u32[]{:S(2)}) collective-permute-start(bf16[160,1024]{1,0:T(8,128)(2,1)S(1)} %constant_dynamic-update-slice_fusion.refs_0_), channel_id=1, source_target_pairs={{0,1},{1,0},{2,3},{3,2},{4,5},{5,4},{6,7},{7,6},{8,9},{9,8},{10,11... | collective-permute-start | bytes 983048 | tf_op jit(solution)/shard_map/ppermute | solution.py:41
  198.3 6.0 %collective-permute-done.20.refs_3_ = bf16[160,1024]{1,0:T(8,128)(2,1)S(1)} collective-permute-done((bf16[160,1024]{1,0:T(8,128)(2,1)S(1)}, bf16[160,1024]{1,0:T(8,128)(2,1)S(1)}, u32[]{:S(2)}, u32[]{:S(2)}) %collective-permute-start.20) | collective-permute-done | bytes 327712 | tf_op jit(solution)/shard_map/ppermute | solution.py:41
  207.9 3.0 %collective-permute-start.23 = (bf16[160,1024]{1,0:T(8,128)(2,1)S(1)}, bf16[160,1024]{1,0:T(8,128)(2,1)S(1)}, u32[]{:S(2)}, u32[]{:S(2)}) collective-permute-start(bf16[160,1024]{1,0:T(8,128)(2,1)S(1)} %collective-permute-done.20.refs_3_), channel_id=1, source_target_pairs={{0,6},{1,7},{2,0},{3,1},{4,2},{5,3},{6,4},{7,5},{8,14},{9,15},{10,... | collective-permute-start | bytes 983048 | tf_op jit(solution)/shard_map/ppermute | solution.py:41
  210.9 6.2 %collective-permute-done.22.refs_5_ = bf16[160,1024]{1,0:T(8,128)(2,1)S(1)} collective-permute-done((bf16[160,1024]{1,0:T(8,128)(2,1)S(1)}, bf16[160,1024]{1,0:T(8,128)(2,1)S(1)}, u32[]{:S(2)}, u32[]{:S(2)}) %collective-permute-start.22) | collective-permute-done | bytes 327712 | tf_op jit(solution)/shard_map/ppermute | solution.py:41
  217.5 2.9 collective-permute-start.25
  221.1 2.7 collective-permute-done.24.refs_7_
  225.4 17.2 %shard_map.132 = (bf16[256,640]{1,0:T(8,128)(2,1)}, bf16[256,640]{1,0:T(8,128)(2,1)}) custom-call(s32[8]{0:T(128)} %get-tuple-element.68.place.col_ref, s32[3]{0:T(128)} %pad_add_fusion.c_ref, bf16[160,1024]{1,0:T(8,128)(2,1)} %copy-done.8, bf16[160,1024]{1,0:T(8,128)(2,1)} %copy-done.20, bf16[160,1024]{1,0:T(8,128)(2,1)} %copy-done.19, ...), custom_call_target="tpu_custom_call" | custom-call | flops 5033164800 | tf_op jit(solution)/shard_map/pallas_call | solution.py:54
  242.6 4.0 %convolution_convert_fusion.1 = bf16[256,3584]{1,0:T(8,128)(2,1)S(1)} fusion(bf16[256,640]{1,0:T(8,128)(2,1)} %get-tuple-element.63, bf16[640,8192]{1,0:T(8,128)(2,1)} %param.22), kind=kOutput, calls=%fused_computation.2 | convolution fusion | flops 1175322624 | bytes 6750208 | tf_op jit(solution)/shard_map/dot_general | solution.py:432
  247.6 4.7 %convolution_convert_fusion = bf16[256,4608]{1,0:T(8,128)(2,1)S(1)} fusion(bf16[256,640]{1,0:T(8,128)(2,1)S(1)} %copy-done.28, bf16[640,8192]{1,0:T(8,128)(2,1)} %param.22), kind=kOutput, calls=%fused_computation | convolution fusion | flops 1511129088 | bytes 8585216 | tf_op jit(solution)/shard_map/dot_general | solution.py:437
  253.0 2.7 collective-permute-start.28
  255.7 2.6 collective-permute-start.31
  260.6 3.6 %collective-permute-start.29 = (bf16[64,4608]{1,0:T(8,128)(2,1)S(1)}, bf16[64,4608]{1,0:T(8,128)(2,1)S(1)}, u32[]{:S(2)}, u32[]{:S(2)}) collective-permute-start(bf16[64,4608]{1,0:T(8,128)(2,1)S(1)} %pad_maximum_fusion.2), channel_id=1, source_target_pairs={{0,6},{1,7},{2,0},{3,1},{4,2},{5,3},{6,4},{7,5},{8,14},{9,15},{10,... | collective-permute-start | bytes 1769480 | tf_op jit(solution)/shard_map/ppermute | solution.py:41
  264.3 11.5 %collective-permute-done.31 = bf16[128,3584]{1,0:T(8,128)(2,1)S(1)} collective-permute-done((bf16[128,3584]{1,0:T(8,128)(2,1)S(1)}, bf16[128,3584]{1,0:T(8,128)(2,1)S(1)}, u32[]{:S(2)}, u32[]{:S(2)}) %collective-permute-start.31) | collective-permute-done | bytes 917536 | tf_op jit(solution)/shard_map/ppermute | solution.py:41
  276.2 3.2 %collective-permute-start.34 = (bf16[32,1792]{1,0:T(8,128)(2,1)S(1)}, bf16[32,1792]{1,0:T(8,128)(2,1)S(1)}, u32[]{:S(2)}, u32[]{:S(2)}) collective-permute-start(bf16[32,1792]{1,0:T(8,128)(2,1)S(1)} %get-tuple-element.78), channel_id=1, source_target_pairs={{0,6},{1,7},{2,0},{3,1},{4,2},{5,3},{6,4},{7,5},{8,14},{9,15},{10,... | collective-permute-start | bytes 344072 | tf_op jit(solution)/shard_map/ppermute | solution.py:41
  279.7 2.7 collective-permute-start.30
  283.1 3.8 %collective-permute-start.35 = (bf16[32,3584]{1,0:T(8,128)(2,1)S(1)}, bf16[32,3584]{1,0:T(8,128)(2,1)S(1)}, u32[]{:S(2)}, u32[]{:S(2)}) collective-permute-start(bf16[32,3584]{1,0:T(8,128)(2,1)S(1)} %pad_maximum_fusion.4), channel_id=1, source_target_pairs={{0,6},{1,7},{2,0},{3,1},{4,2},{5,3},{6,4},{7,5},{8,14},{9,15},{10,... | collective-permute-start | bytes 688136 | tf_op jit(solution)/shard_map/ppermute | solution.py:41
  288.1 2.3 collective-permute-done.35
  290.4 3.8 %collective-permute-done.33 = bf16[32,3584]{1,0:T(8,128)(2,1)S(1)} collective-permute-done((bf16[32,3584]{1,0:T(8,128)(2,1)S(1)}, bf16[32,3584]{1,0:T(8,128)(2,1)S(1)}, u32[]{:S(2)}, u32[]{:S(2)}) %collective-permute-start.33) | collective-permute-done | bytes 229408 | tf_op jit(solution)/shard_map/ppermute | solution.py:41
  (144 shorter events, 36.0 us)
Async XLA Ops:
  0.0 14.1 %collective-permute-start.2 = (bf16[128,1280]{1,0:T(8,128)(2,1)}, bf16[128,1280]{1,0:T(8,128)(2,1)S(1)}, u32[]{:S(2)}, u32[]{:S(2)}) collective-permute-start(bf16[128,1280]{1,0:T(8,128)(2,1)} %bitcast.20), channel_id=1, source_target_pairs={{0,1},{1,0},{2,3},{3,2},{4,5},{5,4},{6,7},{7,6},{8,9},{9,8},{10,11... | collective-permute-start | bytes 983048 | tf_op jit(solution)/shard_map/ppermute | solution.py:41
  4.0 10.1 %collective-permute-start.1 = (bf16[128,1280]{1,0:T(8,128)(2,1)}, bf16[128,1280]{1,0:T(8,128)(2,1)S(1)}, u32[]{:S(2)}, u32[]{:S(2)}) collective-permute-start(bf16[128,1280]{1,0:T(8,128)(2,1)} %bitcast.21), channel_id=1, source_target_pairs={{0,6},{1,7},{2,0},{3,1},{4,2},{5,3},{6,4},{7,5},{8,14},{9,15},{10,... | collective-permute-start | bytes 983048 | tf_op jit(solution)/shard_map/ppermute | solution.py:41
  6.7 10.3 %collective-permute-start = (bf16[128,1280]{1,0:T(8,128)(2,1)}, bf16[128,1280]{1,0:T(8,128)(2,1)S(1)}, u32[]{:S(2)}, u32[]{:S(2)}) collective-permute-start(bf16[128,1280]{1,0:T(8,128)(2,1)} %bitcast.22), channel_id=1, source_target_pairs={{0,2},{1,3},{2,4},{3,5},{4,6},{5,7},{6,0},{7,1},{8,10},{9,11},{10,... | collective-permute-start | bytes 983048 | tf_op jit(solution)/shard_map/ppermute | solution.py:41
  17.1 9.5 %collective-permute-start.4 = (bf16[128,1280]{1,0:T(8,128)(2,1)S(1)}, bf16[128,1280]{1,0:T(8,128)(2,1)S(1)}, u32[]{:S(2)}, u32[]{:S(2)}) collective-permute-start(bf16[128,1280]{1,0:T(8,128)(2,1)S(1)} %collective-permute-done.refs_1_.refs_10_), channel_id=1, source_target_pairs={{0,1},{1,0},{2,3},{3,2},{4,5},{5,4},{6,7},{7,6},{8,9},{9,8},{10,11... | collective-permute-start | bytes 983048 | tf_op jit(solution)/shard_map/ppermute | solution.py:41
  17.3 9.4 %collective-permute-start.3 = (bf16[128,1280]{1,0:T(8,128)(2,1)S(1)}, bf16[128,1280]{1,0:T(8,128)(2,1)S(1)}, u32[]{:S(2)}, u32[]{:S(2)}) collective-permute-start(bf16[128,1280]{1,0:T(8,128)(2,1)S(1)} %collective-permute-done.refs_1_.refs_10_), channel_id=1, source_target_pairs={{0,2},{1,3},{2,4},{3,5},{4,6},{5,7},{6,0},{7,1},{8,10},{9,11},{10,... | collective-permute-start | bytes 983048 | tf_op jit(solution)/shard_map/ppermute | solution.py:41
  17.3 13.0 %collective-permute-start.5 = (bf16[128,1280]{1,0:T(8,128)(2,1)S(1)}, bf16[128,1280]{1,0:T(8,128)(2,1)S(1)}, u32[]{:S(2)}, u32[]{:S(2)}) collective-permute-start(bf16[128,1280]{1,0:T(8,128)(2,1)S(1)} %collective-permute-done.2.refs_3_.refs_12_), channel_id=1, source_target_pairs={{0,6},{1,7},{2,0},{3,1},{4,2},{5,3},{6,4},{7,5},{8,14},{9,15},{10,... | collective-permute-start | bytes 983048 | tf_op jit(solution)/shard_map/ppermute | solution.py:41
  26.6 6.6 %collective-permute-start.6 = (bf16[64,1280]{1,0:T(8,128)(2,1)S(1)}, bf16[64,1280]{1,0:T(8,128)(2,1)S(1)}, u32[]{:S(2)}, u32[]{:S(2)}) collective-permute-start(bf16[64,1280]{1,0:T(8,128)(2,1)S(1)} %slice.127), channel_id=1, source_target_pairs={{0,2},{1,3},{2,4},{3,5},{4,6},{5,7},{6,0},{7,1},{8,10},{9,11},{10,... | collective-permute-start | bytes 491528 | tf_op jit(solution)/shard_map/ppermute | solution.py:41
  26.7 6.9 %collective-permute-start.7 = (bf16[64,1280]{1,0:T(8,128)(2,1)S(1)}, bf16[64,1280]{1,0:T(8,128)(2,1)S(1)}, u32[]{:S(2)}, u32[]{:S(2)}) collective-permute-start(bf16[64,1280]{1,0:T(8,128)(2,1)S(1)} %slice.128), channel_id=1, source_target_pairs={{0,1},{1,0},{2,3},{3,2},{4,5},{5,4},{6,7},{7,6},{8,9},{9,8},{10,11... | collective-permute-start | bytes 491528 | tf_op jit(solution)/shard_map/ppermute | solution.py:41
  43.1 23.7 %collective-permute-start.11 = (bf16[160,2048]{1,0:T(8,128)(2,1)S(1)}, bf16[160,2048]{1,0:T(8,128)(2,1)S(1)}, u32[]{:S(2)}, u32[]{:S(2)}) collective-permute-start(bf16[160,2048]{1,0:T(8,128)(2,1)S(1)} %pad_maximum_fusion.kv_ref), channel_id=1, source_target_pairs={{0,16},{1,17},{2,18},{3,19},{4,20},{5,21},{6,22},{7,23},{8,24},{9,... | collective-permute-start | bytes 1966088 | tf_op jit(solution)/shard_map/ppermute | solution.py:41
  44.5 22.3 %collective-permute-start.10 = (bf16[160,2048]{1,0:T(8,128)(2,1)S(1)}, bf16[160,2048]{1,0:T(8,128)(2,1)S(1)}, u32[]{:S(2)}, u32[]{:S(2)}) collective-permute-start(bf16[160,2048]{1,0:T(8,128)(2,1)S(1)} %pad_maximum_fusion.kv_ref), channel_id=1, source_target_pairs={{0,96},{1,97},{2,98},{3,99},{4,100},{5,101},{6,102},{7,103},{8,104... | collective-permute-start | bytes 1966088 | tf_op jit(solution)/shard_map/ppermute | solution.py:41
  47.5 19.3 %collective-permute-start.9 = (bf16[160,2048]{1,0:T(8,128)(2,1)S(1)}, bf16[160,2048]{1,0:T(8,128)(2,1)S(1)}, u32[]{:S(2)}, u32[]{:S(2)}) collective-permute-start(bf16[160,2048]{1,0:T(8,128)(2,1)S(1)} %pad_maximum_fusion.kv_ref), channel_id=1, source_target_pairs={{0,32},{1,33},{2,34},{3,35},{4,36},{5,37},{6,38},{7,39},{8,40},{9,... | collective-permute-start | bytes 1966088 | tf_op jit(solution)/shard_map/ppermute | solution.py:41
  66.8 52.6 %collective-permute-start.14 = (bf16[160,2048]{1,0:T(8,128)(2,1)S(1)}, bf16[160,2048]{1,0:T(8,128)(2,1)S(1)}, u32[]{:S(2)}, u32[]{:S(2)}) collective-permute-start(bf16[160,2048]{1,0:T(8,128)(2,1)S(1)} %collective-permute-done.9.refs_0_), channel_id=1, source_target_pairs={{0,32},{1,33},{2,34},{3,35},{4,36},{5,37},{6,38},{7,39},{8,40},{9,... | collective-permute-start | bytes 1966088 | tf_op jit(solution)/shard_map/ppermute | solution.py:41
  67.4 53.4 %collective-permute-start.12 = (bf16[160,2048]{1,0:T(8,128)(2,1)S(1)}, bf16[160,2048]{1,0:T(8,128)(2,1)S(1)}, u32[]{:S(2)}, u32[]{:S(2)}) collective-permute-start(bf16[160,2048]{1,0:T(8,128)(2,1)S(1)} %collective-permute-done.9.refs_0_), channel_id=1, source_target_pairs={{0,16},{1,17},{2,18},{3,19},{4,20},{5,21},{6,22},{7,23},{8,24},{9,... | collective-permute-start | bytes 1966088 | tf_op jit(solution)/shard_map/ppermute | solution.py:41
  68.2 52.7 %collective-permute-start.16 = (bf16[160,2048]{1,0:T(8,128)(2,1)S(1)}, bf16[160,2048]{1,0:T(8,128)(2,1)S(1)}, u32[]{:S(2)}, u32[]{:S(2)}) collective-permute-start(bf16[160,2048]{1,0:T(8,128)(2,1)S(1)} %collective-permute-done.11.refs_2_), channel_id=1, source_target_pairs={{0,96},{1,97},{2,98},{3,99},{4,100},{5,101},{6,102},{7,103},{8,104... | collective-permute-start | bytes 1966088 | tf_op jit(solution)/shard_map/ppermute | solution.py:41
  119.5 51.5 %collective-permute-start.15 = (bf16[160,1024]{1,0:T(8,128)(2,1)S(1)}, bf16[160,1024]{1,0:T(8,128)(2,1)S(1)}, u32[]{:S(2)}, u32[]{:S(2)}) collective-permute-start(bf16[160,1024]{1,0:T(8,128)(2,1)S(1)} %slice.131), channel_id=1, source_target_pairs={{0,16},{1,17},{2,18},{3,19},{4,20},{5,21},{6,22},{7,23},{8,24},{9,... | collective-permute-start | bytes 983048 | tf_op jit(solution)/shard_map/ppermute | solution.py:41
  120.9 50.1 %collective-permute-start.13 = (bf16[160,1024]{1,0:T(8,128)(2,1)S(1)}, bf16[160,1024]{1,0:T(8,128)(2,1)S(1)}, u32[]{:S(2)}, u32[]{:S(2)}) collective-permute-start(bf16[160,1024]{1,0:T(8,128)(2,1)S(1)} %slice.130), channel_id=1, source_target_pairs={{0,32},{1,33},{2,34},{3,35},{4,36},{5,37},{6,38},{7,39},{8,40},{9,... | collective-permute-start | bytes 983048 | tf_op jit(solution)/shard_map/ppermute | solution.py:41
  192.1 12.2 %collective-permute-start.20 = (bf16[160,1024]{1,0:T(8,128)(2,1)S(1)}, bf16[160,1024]{1,0:T(8,128)(2,1)S(1)}, u32[]{:S(2)}, u32[]{:S(2)}) collective-permute-start(bf16[160,1024]{1,0:T(8,128)(2,1)S(1)} %constant_dynamic-update-slice_fusion.refs_0_), channel_id=1, source_target_pairs={{0,1},{1,0},{2,3},{3,2},{4,5},{5,4},{6,7},{7,6},{8,9},{9,8},{10,11... | collective-permute-start | bytes 983048 | tf_op jit(solution)/shard_map/ppermute | solution.py:41
  196.3 9.5 %collective-permute-start.19 = (bf16[160,1024]{1,0:T(8,128)(2,1)S(1)}, bf16[160,1024]{1,0:T(8,128)(2,1)S(1)}, u32[]{:S(2)}, u32[]{:S(2)}) collective-permute-start(bf16[160,1024]{1,0:T(8,128)(2,1)S(1)} %constant_dynamic-update-slice_fusion.refs_0_), channel_id=1, source_target_pairs={{0,6},{1,7},{2,0},{3,1},{4,2},{5,3},{6,4},{7,5},{8,14},{9,15},{10,... | collective-permute-start | bytes 983048 | tf_op jit(solution)/shard_map/ppermute | solution.py:41
  196.3 10.7 %collective-permute-start.18 = (bf16[160,1024]{1,0:T(8,128)(2,1)S(1)}, bf16[160,1024]{1,0:T(8,128)(2,1)S(1)}, u32[]{:S(2)}, u32[]{:S(2)}) collective-permute-start(bf16[160,1024]{1,0:T(8,128)(2,1)S(1)} %constant_dynamic-update-slice_fusion.refs_0_), channel_id=1, source_target_pairs={{0,2},{1,3},{2,4},{3,5},{4,6},{5,7},{6,0},{7,1},{8,10},{9,11},{10,... | collective-permute-start | bytes 983048 | tf_op jit(solution)/shard_map/ppermute | solution.py:41
  207.0 10.1 %collective-permute-start.22 = (bf16[160,1024]{1,0:T(8,128)(2,1)S(1)}, bf16[160,1024]{1,0:T(8,128)(2,1)S(1)}, u32[]{:S(2)}, u32[]{:S(2)}) collective-permute-start(bf16[160,1024]{1,0:T(8,128)(2,1)S(1)} %collective-permute-done.18.refs_1_), channel_id=1, source_target_pairs={{0,1},{1,0},{2,3},{3,2},{4,5},{5,4},{6,7},{7,6},{8,9},{9,8},{10,11... | collective-permute-start | bytes 983048 | tf_op jit(solution)/shard_map/ppermute | solution.py:41
  207.7 9.8 %collective-permute-start.21 = (bf16[160,1024]{1,0:T(8,128)(2,1)S(1)}, bf16[160,1024]{1,0:T(8,128)(2,1)S(1)}, u32[]{:S(2)}, u32[]{:S(2)}) collective-permute-start(bf16[160,1024]{1,0:T(8,128)(2,1)S(1)} %collective-permute-done.18.refs_1_), channel_id=1, source_target_pairs={{0,2},{1,3},{2,4},{3,5},{4,6},{5,7},{6,0},{7,1},{8,10},{9,11},{10,... | collective-permute-start | bytes 983048 | tf_op jit(solution)/shard_map/ppermute | solution.py:41
  207.9 13.2 %collective-permute-start.23 = (bf16[160,1024]{1,0:T(8,128)(2,1)S(1)}, bf16[160,1024]{1,0:T(8,128)(2,1)S(1)}, u32[]{:S(2)}, u32[]{:S(2)}) collective-permute-start(bf16[160,1024]{1,0:T(8,128)(2,1)S(1)} %collective-permute-done.20.refs_3_), channel_id=1, source_target_pairs={{0,6},{1,7},{2,0},{3,1},{4,2},{5,3},{6,4},{7,5},{8,14},{9,15},{10,... | collective-permute-start | bytes 983048 | tf_op jit(solution)/shard_map/ppermute | solution.py:41
  217.5 7.1 %collective-permute-start.25 = (bf16[80,1024]{1,0:T(8,128)(2,1)S(1)}, bf16[80,1024]{1,0:T(8,128)(2,1)S(1)}, u32[]{:S(2)}, u32[]{:S(2)}) collective-permute-start(bf16[80,1024]{1,0:T(8,128)(2,1)S(1)} %slice.133), channel_id=1, source_target_pairs={{0,1},{1,0},{2,3},{3,2},{4,5},{5,4},{6,7},{7,6},{8,9},{9,8},{10,11... | collective-permute-start | bytes 491528 | tf_op jit(solution)/shard_map/ppermute | solution.py:41
  252.4 8.0 %collective-permute-start.26 = (bf16[64,2304]{1,0:T(8,128)(2,1)S(1)}, bf16[64,2304]{1,0:T(8,128)(2,1)S(1)}, u32[]{:S(2)}, u32[]{:S(2)}) collective-permute-start(bf16[64,2304]{1,0:T(8,128)(2,1)S(1)} %get-tuple-element.71), channel_id=1, source_target_pairs={{0,2},{1,3},{2,4},{3,5},{4,6},{5,7},{6,0},{7,1},{8,10},{9,11},{10,... | collective-permute-start | bytes 884744 | tf_op jit(solution)/shard_map/ppermute | solution.py:41
  253.0 7.4 %collective-permute-start.28 = (bf16[64,2304]{1,0:T(8,128)(2,1)S(1)}, bf16[64,2304]{1,0:T(8,128)(2,1)S(1)}, u32[]{:S(2)}, u32[]{:S(2)}) collective-permute-start(bf16[64,2304]{1,0:T(8,128)(2,1)S(1)} %get-tuple-element.72), channel_id=1, source_target_pairs={{0,6},{1,7},{2,0},{3,1},{4,2},{5,3},{6,4},{7,5},{8,14},{9,15},{10,... | collective-permute-start | bytes 884744 | tf_op jit(solution)/shard_map/ppermute | solution.py:41
  255.7 20.2 %collective-permute-start.31 = (bf16[128,3584]{1,0:T(8,128)(2,1)S(1)}, bf16[128,3584]{1,0:T(8,128)(2,1)S(1)}, u32[]{:S(2)}, u32[]{:S(2)}) collective-permute-start(bf16[128,3584]{1,0:T(8,128)(2,1)S(1)} %slice.134), channel_id=1, source_target_pairs={{0,1},{1,0},{2,3},{3,2},{4,5},{5,4},{6,7},{7,6},{8,9},{9,8},{10,11... | collective-permute-start | bytes 2752520 | tf_op jit(solution)/shard_map/ppermute | solution.py:41
  260.6 18.9 %collective-permute-start.29 = (bf16[64,4608]{1,0:T(8,128)(2,1)S(1)}, bf16[64,4608]{1,0:T(8,128)(2,1)S(1)}, u32[]{:S(2)}, u32[]{:S(2)}) collective-permute-start(bf16[64,4608]{1,0:T(8,128)(2,1)S(1)} %pad_maximum_fusion.2), channel_id=1, source_target_pairs={{0,6},{1,7},{2,0},{3,1},{4,2},{5,3},{6,4},{7,5},{8,14},{9,15},{10,... | collective-permute-start | bytes 1769480 | tf_op jit(solution)/shard_map/ppermute | solution.py:41
  264.3 15.2 %collective-permute-start.27 = (bf16[64,4608]{1,0:T(8,128)(2,1)S(1)}, bf16[64,4608]{1,0:T(8,128)(2,1)S(1)}, u32[]{:S(2)}, u32[]{:S(2)}) collective-permute-start(bf16[64,4608]{1,0:T(8,128)(2,1)S(1)} %pad_maximum_fusion.1), channel_id=1, source_target_pairs={{0,2},{1,3},{2,4},{3,5},{4,6},{5,7},{6,0},{7,1},{8,10},{9,11},{10,... | collective-permute-start | bytes 1769480 | tf_op jit(solution)/shard_map/ppermute | solution.py:41
  276.2 6.8 %collective-permute-start.34 = (bf16[32,1792]{1,0:T(8,128)(2,1)S(1)}, bf16[32,1792]{1,0:T(8,128)(2,1)S(1)}, u32[]{:S(2)}, u32[]{:S(2)}) collective-permute-start(bf16[32,1792]{1,0:T(8,128)(2,1)S(1)} %get-tuple-element.78), channel_id=1, source_target_pairs={{0,6},{1,7},{2,0},{3,1},{4,2},{5,3},{6,4},{7,5},{8,14},{9,15},{10,... | collective-permute-start | bytes 344072 | tf_op jit(solution)/shard_map/ppermute | solution.py:41
  279.7 8.3 %collective-permute-start.30 = (bf16[32,4608]{1,0:T(8,128)(2,1)S(1)}, bf16[32,4608]{1,0:T(8,128)(2,1)S(1)}, u32[]{:S(2)}, u32[]{:S(2)}) collective-permute-start(bf16[32,4608]{1,0:T(8,128)(2,1)S(1)} %slice.165), channel_id=1, source_target_pairs={{0,1},{1,0},{2,3},{3,2},{4,5},{5,4},{6,7},{7,6},{8,9},{9,8},{10,11... | collective-permute-start | bytes 884744 | tf_op jit(solution)/shard_map/ppermute | solution.py:41
  283.1 7.3 %collective-permute-start.35 = (bf16[32,3584]{1,0:T(8,128)(2,1)S(1)}, bf16[32,3584]{1,0:T(8,128)(2,1)S(1)}, u32[]{:S(2)}, u32[]{:S(2)}) collective-permute-start(bf16[32,3584]{1,0:T(8,128)(2,1)S(1)} %pad_maximum_fusion.4), channel_id=1, source_target_pairs={{0,6},{1,7},{2,0},{3,1},{4,2},{5,3},{6,4},{7,5},{8,14},{9,15},{10,... | collective-permute-start | bytes 688136 | tf_op jit(solution)/shard_map/ppermute | solution.py:41
  286.8 7.3 %collective-permute-start.33 = (bf16[32,3584]{1,0:T(8,128)(2,1)S(1)}, bf16[32,3584]{1,0:T(8,128)(2,1)S(1)}, u32[]{:S(2)}, u32[]{:S(2)}) collective-permute-start(bf16[32,3584]{1,0:T(8,128)(2,1)S(1)} %pad_maximum_fusion.3), channel_id=1, source_target_pairs={{0,2},{1,3},{2,4},{3,5},{4,6},{5,7},{6,0},{7,1},{8,10},{9,11},{10,... | collective-permute-start | bytes 688136 | tf_op jit(solution)/shard_map/ppermute | solution.py:41
  (33 other events, 239.6 us)
where the time goes:
time: 296 us; the launch traced here: 295 us
  Pallas kernels  158 us (53%)
  starting transfers between devices  56.6 us (19%)
  waiting for transfers between devices  55 us (19%)
  local copies, waits for them, and re-layouts  9.9 us (3%)
  matrix products  8.71 us (3%)
  other arithmetic  6.88 us (2%)
    pallas_call x6, Pallas kernels, call(): pl.pallas_call(kernel, out_shape=outs, in_specs=specs, out_specs=jax.tree...  158 us
    ppermute x36, starting transfers between devices, send(): return lax.ppermute(value, AXES, perm)  56.6 us
    ppermute x36, waiting for transfers between devices, send(): return lax.ppermute(value, AXES, perm)  55 us
  transfers between devices with their start and end apart: 36, of which 18 were waited for; matrix products, arithmetic and copies ran while one was open for 3% of the time, Pallas kernels for 39%

commit v1 on v0

--- a/solution.py
+++ b/solution.py
@@ -49,7 +49,7 @@
     return pl.BlockSpec(memory_space=pltpu.SMEM)
 
 
-def call(kernel, outs, ins, scratch=(), flops=0, nbytes=0, exps=0):
+def call(kernel, outs, ins, scratch=(), flops=0, nbytes=0, exps=0, grant=8):
     specs = [smem() if k == "s" else vmem() for k, _ in ins]
     return pl.pallas_call(
         kernel,
@@ -58,7 +58,7 @@
         out_specs=jax.tree.map(lambda _: vmem(), outs),
         scratch_shapes=list(scratch),
         cost_estimate=pl.CostEstimate(flops=flops, bytes_accessed=nbytes, transcendentals=exps),
-        compiler_params=pltpu.CompilerParams(vmem_limit_bytes=58 * 2**20),
+        compiler_params=pltpu.CompilerParams(vmem_limit_bytes=grant * 2**20),
     )(*[a for _, a in ins])
 
 
@@ -234,28 +234,31 @@
     width = out_weight.shape[1]
 
     def project(i, carry):
-        spot = pl.ds(pl.multiple_of(i * 256, 256), 256)
+        spot = pl.ds(pl.multiple_of(i * 512, 512), 512)
         lhs = att_all[:, spot].T
         mixed_all[spot, :] = jnp.dot(lhs, out_weight[...], preferred_element_type=F32)
         return carry
 
-    lax.fori_loop(0, 4, project, 0)
+    lax.fori_loop(0, 2, project, 0)
     r = lax.broadcasted_iota(jnp.int32, (128, 128), 0)
     t = lax.broadcasted_iota(jnp.int32, (128, 128), 1)
     a, b, u, w = r >> 6, (r >> 5) & 1, (r >> 3) & 3, r & 7
     pick = ((2 * u + a) * 16 + 2 * w + b == t).astype(BF)
 
-    def settle(s, carry):
-        spot = pl.ds(pl.multiple_of(col_ref[s] * 128, 128), 128)
-        own = pl.ds(pl.multiple_of(s * 128, 128), 128)
-        residual = token_all[own, :].astype(F32) + mixed_all[spot, :]
-        normed = norm(residual, gain_ref[...]).astype(BF)
-        ordered = jnp.dot(pick, normed, preferred_element_type=F32).astype(BF)
-        for q in range(4):
-            merged[q, pl.ds(pl.multiple_of(s * 32, 32), 32), :] = ordered[q * 32 : (q + 1) * 32]
+    def settle(turn, carry):
+        for k in range(4):
+            s = turn * 4 + k
+            spot = pl.ds(pl.multiple_of(col_ref[s] * 128, 128), 128)
+            own = pl.ds(pl.multiple_of(s * 128, 128), 128)
+            residual = token_all[own, :].astype(F32) + mixed_all[spot, :]
+            normed = norm(residual, gain_ref[...]).astype(BF)
+            ordered = jnp.dot(pick, normed, preferred_element_type=F32).astype(BF)
+            rows = pl.ds(pl.multiple_of(s * 32, 32), 32)
+            for q in range(4):
+                merged[q, rows, :] = ordered[q * 32 : (q + 1) * 32]
         return carry
 
-    lax.fori_loop(0, 8, settle, 0)
+    lax.fori_loop(0, 2, settle, 0)
     z = bias_ref[...]
     for q in range(4):
         z = z + jnp.dot(
@@ -409,6 +412,7 @@
             pltpu.VMEM((4, 256, model_width), BF),
         ],
         flops=2 * 256 * 5120 * 640 + 2 * band * model_width * model_width,
+        grant=18,
     )
     return scatter_output(hidden_a, hidden_b, down_weight, down_bias, mirror_x)
 

time: 296 us -> 269 us (0.909)
  Pallas kernels: 158 us -> 138 us
  waiting for transfers between devices: 55 us -> 60.2 us
  matrix products: 8.71 us -> 3.59 us
  local copies, waits for them, and re-layouts: 9.9 us -> 6.63 us
    pallas_call x6, Pallas kernels: 158 us -> 138 us  [call(): pl.pallas_call(kernel, out_shape=outs, in_specs=specs, out_specs=jax.tree...]
    ppermute x36, waiting for transfers between devices: 55 us -> 60.2 us  [send(): return lax.ppermute(value, AXES, perm)]
  transfers between devices with their start and end apart: 36 -> 36, of which waited for: 18 -> 24; matrix products, arithmetic and copies ran while one was open for 3% -> 2% of each run, Pallas kernels for 39% -> 40%
where the time goes in v1:
time: 269 us
  Pallas kernels  138 us (51%)
  waiting for transfers between devices  60.2 us (22%)
  starting transfers between devices  56.2 us (21%)
  local copies, waits for them, and re-layouts  6.63 us (2%)
  other arithmetic  4.03 us (1%)
  matrix products  3.59 us (1%)
    pallas_call x6, Pallas kernels, call(): pl.pallas_call(kernel, out_shape=outs, in_specs=specs, out_specs=jax.tree...  138 us
    ppermute x36, waiting for transfers between devices, send(): return lax.ppermute(value, AXES, perm)  60.2 us
    ppermute x36, starting transfers between devices, send(): return lax.ppermute(value, AXES, perm)  56.2 us
  transfers between devices with their start and end apart: 36, of which 24 were waited for; matrix products, arithmetic and copies ran while one was open for 2% of the time, Pallas kernels for 40%

profile of v1, /device:TPU:0, one launch (start us, length us, event | category | flops | bytes accessed | tf_op | source)
XLA Modules:
  0.0 268.7 jit_solution(11045040874540964981)
XLA Ops:
  0.0 4.0 %collective-permute-start.2 = (bf16[128,1280]{1,0:T(8,128)(2,1)}, bf16[128,1280]{1,0:T(8,128)(2,1)S(1)}, u32[]{:S(2)}, u32[]{:S(2)}) collective-permute-start(bf16[128,1280]{1,0:T(8,128)(2,1)} %bitcast.22), channel_id=1, source_target_pairs={{0,1},{1,0},{2,3},{3,2},{4,5},{5,4},{6,7},{7,6},{8,9},{9,8},{10,11... | collective-permute-start | bytes 983048 | tf_op jit(solution)/shard_map/ppermute | solution.py:41
  4.0 2.8 %collective-permute-start.1 = (bf16[128,1280]{1,0:T(8,128)(2,1)}, bf16[128,1280]{1,0:T(8,128)(2,1)S(1)}, u32[]{:S(2)}, u32[]{:S(2)}) collective-permute-start(bf16[128,1280]{1,0:T(8,128)(2,1)} %bitcast.23), channel_id=1, source_target_pairs={{0,6},{1,7},{2,0},{3,1},{4,2},{5,3},{6,4},{7,5},{8,14},{9,15},{10,... | collective-permute-start | bytes 983048 | tf_op jit(solution)/shard_map/ppermute | solution.py:41
  13.8 3.3 %collective-permute-done.refs_1_.refs_10_ = bf16[128,1280]{1,0:T(8,128)(2,1)S(1)} collective-permute-done((bf16[128,1280]{1,0:T(8,128)(2,1)}, bf16[128,1280]{1,0:T(8,128)(2,1)S(1)}, u32[]{:S(2)}, u32[]{:S(2)}) %collective-permute-start) | collective-permute-done | bytes 327712 | tf_op jit(solution)/shard_map/ppermute | solution.py:41
  17.3 3.2 %collective-permute-start.5 = (bf16[128,1280]{1,0:T(8,128)(2,1)S(1)}, bf16[128,1280]{1,0:T(8,128)(2,1)S(1)}, u32[]{:S(2)}, u32[]{:S(2)}) collective-permute-start(bf16[128,1280]{1,0:T(8,128)(2,1)S(1)} %collective-permute-done.2.refs_3_.refs_12_), channel_id=1, source_target_pairs={{0,6},{1,7},{2,0},{3,1},{4,2},{5,3},{6,4},{7,5},{8,14},{9,15},{10,... | collective-permute-start | bytes 983048 | tf_op jit(solution)/shard_map/ppermute | solution.py:41
  20.6 6.0 %collective-permute-done.4.refs_5_.refs_14_ = bf16[128,1280]{1,0:T(8,128)(2,1)S(1)} collective-permute-done((bf16[128,1280]{1,0:T(8,128)(2,1)S(1)}, bf16[128,1280]{1,0:T(8,128)(2,1)S(1)}, u32[]{:S(2)}, u32[]{:S(2)}) %collective-permute-start.4) | collective-permute-done | bytes 327712 | tf_op jit(solution)/shard_map/ppermute | solution.py:41
  26.7 3.6 %collective-permute-start.7 = (bf16[64,1280]{1,0:T(8,128)(2,1)S(1)}, bf16[64,1280]{1,0:T(8,128)(2,1)S(1)}, u32[]{:S(2)}, u32[]{:S(2)}) collective-permute-start(bf16[64,1280]{1,0:T(8,128)(2,1)S(1)} %slice.128), channel_id=1, source_target_pairs={{0,1},{1,0},{2,3},{3,2},{4,5},{5,4},{6,7},{7,6},{8,9},{9,8},{10,11... | collective-permute-start | bytes 491528 | tf_op jit(solution)/shard_map/ppermute | solution.py:41
  30.3 2.9 %collective-permute-done.6.refs_7_.refs_16_ = bf16[64,1280]{1,0:T(8,128)(2,1)S(1)} collective-permute-done((bf16[64,1280]{1,0:T(8,128)(2,1)S(1)}, bf16[64,1280]{1,0:T(8,128)(2,1)S(1)}, u32[]{:S(2)}, u32[]{:S(2)}) %collective-permute-start.6) | collective-permute-done | bytes 163872 | tf_op jit(solution)/shard_map/ppermute | solution.py:41
  37.6 2.6 shard_map.127
  43.6 3.0 %collective-permute-start.10 = (bf16[160,2048]{1,0:T(8,128)(2,1)S(1)}, bf16[160,2048]{1,0:T(8,128)(2,1)S(1)}, u32[]{:S(2)}, u32[]{:S(2)}) collective-permute-start(bf16[160,2048]{1,0:T(8,128)(2,1)S(1)} %pad_maximum_fusion.kv_ref), channel_id=1, source_target_pairs={{0,96},{1,97},{2,98},{3,99},{4,100},{5,101},{6,102},{7,103},{8,104... | collective-permute-start | bytes 1966088 | tf_op jit(solution)/shard_map/ppermute | solution.py:41
  46.6 16.9 %shard_map.128 = (bf16[96,2048]{1,0:T(8,128)(2,1)S(1)}, f32[8,2048]{1,0:T(8,128)S(1)}, f32[8,2048]{1,0:T(8,128)S(1)}, f32[96,2048]{1,0:T(8,128)S(1)}) custom-call(bf16[80,1024]{1,0:T(8,128)(2,1)S(1)} %get-tuple-element.45.own_q, bf16[240,1024]{1,0:T(8,128)(2,1)S(1)} %collective-permute-done.8.swapped, bf16[160,2048]{1,0:T(8,128)(2,1)S(1)} %pad_maximum_fusion.kv_ref), custom_call_target="tpu_custom_call" | custom-call | flops 4294967296 | bytes 786432 | tf_op jit(solution)/shard_map/pallas_call | solution.py:54
  64.9 3.1 %collective-permute-start.16 = (bf16[160,2048]{1,0:T(8,128)(2,1)S(1)}, bf16[160,2048]{1,0:T(8,128)(2,1)S(1)}, u32[]{:S(2)}, u32[]{:S(2)}) collective-permute-start(bf16[160,2048]{1,0:T(8,128)(2,1)S(1)} %collective-permute-done.11.refs_2_), channel_id=1, source_target_pairs={{0,96},{1,97},{2,98},{3,99},{4,100},{5,101},{6,102},{7,103},{8,104... | collective-permute-start | bytes 1966088 | tf_op jit(solution)/shard_map/ppermute | solution.py:41
  68.0 45.9 %shard_map.129 = (f32[8,2048]{1,0:T(8,128)S(1)}, f32[96,2048]{1,0:T(8,128)S(1)}) custom-call(bf16[160,2048]{1,0:T(8,128)(2,1)S(1)} %collective-permute-done.9.refs_0_, bf16[160,2048]{1,0:T(8,128)(2,1)S(1)} %collective-permute-done.10.refs_1_, bf16[160,2048]{1,0:T(8,128)(2,1)S(1)} %collective-permute-done.11.refs_2_, ...), custom_call_target="tpu_custom_call" | custom-call | flops 12884901888 | bytes 786432 | tf_op jit(solution)/shard_map/pallas_call | solution.py:54
  115.5 46.0 %shard_map.130 = (f32[8,2048]{1,0:T(8,128)S(1)}, f32[96,2048]{1,0:T(8,128)S(1)}) custom-call(bf16[160,2048]{1,0:T(8,128)(2,1)S(1)} %collective-permute-done.14.refs_0_, bf16[160,2048]{1,0:T(8,128)(2,1)S(1)} %collective-permute-done.12.refs_1_, bf16[160,2048]{1,0:T(8,128)(2,1)S(1)} %collective-permute-done.16.refs_2_, ...), custom_call_target="tpu_custom_call" | custom-call | flops 12884901888 | bytes 786432 | tf_op jit(solution)/shard_map/pallas_call | solution.py:54
  161.5 16.5 %shard_map.131 = (bf16[80,1024]{1,0:T(8,128)(2,1)S(1)}, bf16[80,1024]{1,0:T(8,128)(2,1)S(1)}) custom-call(s32[8]{0:T(128)S(1)} %get-tuple-element.68.place.col_ref, bf16[160,1024]{1,0:T(8,128)(2,1)S(1)} %collective-permute-done.13.refs_0_, bf16[160,1024]{1,0:T(8,128)(2,1)S(1)} %collective-permute-done.15.refs_1_, ...), custom_call_target="tpu_custom_call" | custom-call | flops 4294967296 | bytes 786432 | tf_op jit(solution)/shard_map/pallas_call | solution.py:54
  179.5 4.2 %collective-permute-start.20 = (bf16[160,1024]{1,0:T(8,128)(2,1)S(1)}, bf16[160,1024]{1,0:T(8,128)(2,1)S(1)}, u32[]{:S(2)}, u32[]{:S(2)}) collective-permute-start(bf16[160,1024]{1,0:T(8,128)(2,1)S(1)} %constant_dynamic-update-slice_fusion.refs_0_), channel_id=1, source_target_pairs={{0,1},{1,0},{2,3},{3,2},{4,5},{5,4},{6,7},{7,6},{8,9},{9,8},{10,11... | collective-permute-start | bytes 983048 | tf_op jit(solution)/shard_map/ppermute | solution.py:41
  183.7 2.0 collective-permute-start.18
  185.7 6.0 %collective-permute-done.20.refs_3_ = bf16[160,1024]{1,0:T(8,128)(2,1)S(1)} collective-permute-done((bf16[160,1024]{1,0:T(8,128)(2,1)S(1)}, bf16[160,1024]{1,0:T(8,128)(2,1)S(1)}, u32[]{:S(2)}, u32[]{:S(2)}) %collective-permute-start.20) | collective-permute-done | bytes 327712 | tf_op jit(solution)/shard_map/ppermute | solution.py:41
  194.4 2.1 collective-permute-start.22
  196.4 3.2 %collective-permute-start.23 = (bf16[160,1024]{1,0:T(8,128)(2,1)S(1)}, bf16[160,1024]{1,0:T(8,128)(2,1)S(1)}, u32[]{:S(2)}, u32[]{:S(2)}) collective-permute-start(bf16[160,1024]{1,0:T(8,128)(2,1)S(1)} %collective-permute-done.20.refs_3_), channel_id=1, source_target_pairs={{0,6},{1,7},{2,0},{3,1},{4,2},{5,3},{6,4},{7,5},{8,14},{9,15},{10,... | collective-permute-start | bytes 983048 | tf_op jit(solution)/shard_map/ppermute | solution.py:41
  199.7 4.8 %collective-permute-done.22.refs_5_ = bf16[160,1024]{1,0:T(8,128)(2,1)S(1)} collective-permute-done((bf16[160,1024]{1,0:T(8,128)(2,1)S(1)}, bf16[160,1024]{1,0:T(8,128)(2,1)S(1)}, u32[]{:S(2)}, u32[]{:S(2)}) %collective-permute-start.22) | collective-permute-done | bytes 327712 | tf_op jit(solution)/shard_map/ppermute | solution.py:41
  205.7 2.0 collective-permute-start.25
  207.8 3.3 %collective-permute-done.24.refs_7_ = bf16[80,1024]{1,0:T(8,128)(2,1)S(1)} collective-permute-done((bf16[80,1024]{1,0:T(8,128)(2,1)S(1)}, bf16[80,1024]{1,0:T(8,128)(2,1)S(1)}, u32[]{:S(2)}, u32[]{:S(2)}) %collective-permute-start.24) | collective-permute-done | bytes 163872 | tf_op jit(solution)/shard_map/ppermute | solution.py:41
  212.9 9.8 %shard_map.132 = (bf16[256,640]{1,0:T(8,128)(2,1)S(1)}, bf16[256,640]{1,0:T(8,128)(2,1)S(1)}) custom-call(s32[8]{0:T(128)S(1)} %get-tuple-element.68.place.col_ref, s32[3]{0:T(128)S(1)} %pad_add_fusion.c_ref, bf16[160,1024]{1,0:T(8,128)(2,1)S(1)} %constant_dynamic-update-slice_fusion.refs_0_, bf16[160,1024]{1,0:T(8,128)(2,1)S(1)} %collective-permute-done.18.refs_1_, ...), custom_call_target="tpu_custom_call" | custom-call | flops 5033164800 | tf_op jit(solution)/shard_map/pallas_call | solution.py:54
  226.5 3.2 %collective-permute-start.28 = (bf16[64,2304]{1,0:T(8,128)(2,1)S(1)}, bf16[64,2304]{1,0:T(8,128)(2,1)S(1)}, u32[]{:S(2)}, u32[]{:S(2)}) collective-permute-start(bf16[64,2304]{1,0:T(8,128)(2,1)S(1)} %get-tuple-element.72), channel_id=1, source_target_pairs={{0,6},{1,7},{2,0},{3,1},{4,2},{5,3},{6,4},{7,5},{8,14},{9,15},{10,... | collective-permute-start | bytes 884744 | tf_op jit(solution)/shard_map/ppermute | solution.py:41
  231.5 3.0 %collective-permute-done.26 = bf16[64,2304]{1,0:T(8,128)(2,1)S(1)} collective-permute-done((bf16[64,2304]{1,0:T(8,128)(2,1)S(1)}, bf16[64,2304]{1,0:T(8,128)(2,1)S(1)}, u32[]{:S(2)}, u32[]{:S(2)}) %collective-permute-start.26) | collective-permute-done | bytes 294944 | tf_op jit(solution)/shard_map/ppermute | solution.py:41
  235.1 3.8 %collective-permute-start.29 = (bf16[64,4608]{1,0:T(8,128)(2,1)S(1)}, bf16[64,4608]{1,0:T(8,128)(2,1)S(1)}, u32[]{:S(2)}, u32[]{:S(2)}) collective-permute-start(bf16[64,4608]{1,0:T(8,128)(2,1)S(1)} %pad_maximum_fusion.2), channel_id=1, source_target_pairs={{0,6},{1,7},{2,0},{3,1},{4,2},{5,3},{6,4},{7,5},{8,14},{9,15},{10,... | collective-permute-start | bytes 1769480 | tf_op jit(solution)/shard_map/ppermute | solution.py:41
  239.0 10.4 %collective-permute-done.31 = bf16[128,3584]{1,0:T(8,128)(2,1)S(1)} collective-permute-done((bf16[128,3584]{1,0:T(8,128)(2,1)S(1)}, bf16[128,3584]{1,0:T(8,128)(2,1)S(1)}, u32[]{:S(2)}, u32[]{:S(2)}) %collective-permute-start.31) | collective-permute-done | bytes 917536 | tf_op jit(solution)/shard_map/ppermute | solution.py:41
  249.8 3.2 %collective-permute-start.34 = (bf16[32,1792]{1,0:T(8,128)(2,1)S(1)}, bf16[32,1792]{1,0:T(8,128)(2,1)S(1)}, u32[]{:S(2)}, u32[]{:S(2)}) collective-permute-start(bf16[32,1792]{1,0:T(8,128)(2,1)S(1)} %get-tuple-element.78), channel_id=1, source_target_pairs={{0,6},{1,7},{2,0},{3,1},{4,2},{5,3},{6,4},{7,5},{8,14},{9,15},{10,... | collective-permute-start | bytes 344072 | tf_op jit(solution)/shard_map/ppermute | solution.py:41
  253.3 2.4 collective-permute-start.30
  256.7 3.8 %collective-permute-start.35 = (bf16[32,3584]{1,0:T(8,128)(2,1)S(1)}, bf16[32,3584]{1,0:T(8,128)(2,1)S(1)}, u32[]{:S(2)}, u32[]{:S(2)}) collective-permute-start(bf16[32,3584]{1,0:T(8,128)(2,1)S(1)} %pad_maximum_fusion.4), channel_id=1, source_target_pairs={{0,6},{1,7},{2,0},{3,1},{4,2},{5,3},{6,4},{7,5},{8,14},{9,15},{10,... | collective-permute-start | bytes 688136 | tf_op jit(solution)/shard_map/ppermute | solution.py:41
  261.6 2.3 collective-permute-done.35
  264.0 3.8 %collective-permute-done.33 = bf16[32,3584]{1,0:T(8,128)(2,1)S(1)} collective-permute-done((bf16[32,3584]{1,0:T(8,128)(2,1)S(1)}, bf16[32,3584]{1,0:T(8,128)(2,1)S(1)}, u32[]{:S(2)}, u32[]{:S(2)}) %collective-permute-start.33) | collective-permute-done | bytes 229408 | tf_op jit(solution)/shard_map/ppermute | solution.py:41
  (112 shorter events, 35.3 us)
Async XLA Ops:
  0.0 11.9 %collective-permute-start.2 = (bf16[128,1280]{1,0:T(8,128)(2,1)}, bf16[128,1280]{1,0:T(8,128)(2,1)S(1)}, u32[]{:S(2)}, u32[]{:S(2)}) collective-permute-start(bf16[128,1280]{1,0:T(8,128)(2,1)} %bitcast.22), channel_id=1, source_target_pairs={{0,1},{1,0},{2,3},{3,2},{4,5},{5,4},{6,7},{7,6},{8,9},{9,8},{10,11... | collective-permute-start | bytes 983048 | tf_op jit(solution)/shard_map/ppermute | solution.py:41
  4.0 9.8 %collective-permute-start.1 = (bf16[128,1280]{1,0:T(8,128)(2,1)}, bf16[128,1280]{1,0:T(8,128)(2,1)S(1)}, u32[]{:S(2)}, u32[]{:S(2)}) collective-permute-start(bf16[128,1280]{1,0:T(8,128)(2,1)} %bitcast.23), channel_id=1, source_target_pairs={{0,6},{1,7},{2,0},{3,1},{4,2},{5,3},{6,4},{7,5},{8,14},{9,15},{10,... | collective-permute-start | bytes 983048 | tf_op jit(solution)/shard_map/ppermute | solution.py:41
  6.7 10.3 %collective-permute-start = (bf16[128,1280]{1,0:T(8,128)(2,1)}, bf16[128,1280]{1,0:T(8,128)(2,1)S(1)}, u32[]{:S(2)}, u32[]{:S(2)}) collective-permute-start(bf16[128,1280]{1,0:T(8,128)(2,1)} %bitcast.24), channel_id=1, source_target_pairs={{0,2},{1,3},{2,4},{3,5},{4,6},{5,7},{6,0},{7,1},{8,10},{9,11},{10,... | collective-permute-start | bytes 983048 | tf_op jit(solution)/shard_map/ppermute | solution.py:41
  17.1 9.5 %collective-permute-start.4 = (bf16[128,1280]{1,0:T(8,128)(2,1)S(1)}, bf16[128,1280]{1,0:T(8,128)(2,1)S(1)}, u32[]{:S(2)}, u32[]{:S(2)}) collective-permute-start(bf16[128,1280]{1,0:T(8,128)(2,1)S(1)} %collective-permute-done.refs_1_.refs_10_), channel_id=1, source_target_pairs={{0,1},{1,0},{2,3},{3,2},{4,5},{5,4},{6,7},{7,6},{8,9},{9,8},{10,11... | collective-permute-start | bytes 983048 | tf_op jit(solution)/shard_map/ppermute | solution.py:41
  17.3 9.4 %collective-permute-start.3 = (bf16[128,1280]{1,0:T(8,128)(2,1)S(1)}, bf16[128,1280]{1,0:T(8,128)(2,1)S(1)}, u32[]{:S(2)}, u32[]{:S(2)}) collective-permute-start(bf16[128,1280]{1,0:T(8,128)(2,1)S(1)} %collective-permute-done.refs_1_.refs_10_), channel_id=1, source_target_pairs={{0,2},{1,3},{2,4},{3,5},{4,6},{5,7},{6,0},{7,1},{8,10},{9,11},{10,... | collective-permute-start | bytes 983048 | tf_op jit(solution)/shard_map/ppermute | solution.py:41
  17.3 13.0 %collective-permute-start.5 = (bf16[128,1280]{1,0:T(8,128)(2,1)S(1)}, bf16[128,1280]{1,0:T(8,128)(2,1)S(1)}, u32[]{:S(2)}, u32[]{:S(2)}) collective-permute-start(bf16[128,1280]{1,0:T(8,128)(2,1)S(1)} %collective-permute-done.2.refs_3_.refs_12_), channel_id=1, source_target_pairs={{0,6},{1,7},{2,0},{3,1},{4,2},{5,3},{6,4},{7,5},{8,14},{9,15},{10,... | collective-permute-start | bytes 983048 | tf_op jit(solution)/shard_map/ppermute | solution.py:41
  26.6 6.6 %collective-permute-start.6 = (bf16[64,1280]{1,0:T(8,128)(2,1)S(1)}, bf16[64,1280]{1,0:T(8,128)(2,1)S(1)}, u32[]{:S(2)}, u32[]{:S(2)}) collective-permute-start(bf16[64,1280]{1,0:T(8,128)(2,1)S(1)} %slice.127), channel_id=1, source_target_pairs={{0,2},{1,3},{2,4},{3,5},{4,6},{5,7},{6,0},{7,1},{8,10},{9,11},{10,... | collective-permute-start | bytes 491528 | tf_op jit(solution)/shard_map/ppermute | solution.py:41
  26.7 6.9 %collective-permute-start.7 = (bf16[64,1280]{1,0:T(8,128)(2,1)S(1)}, bf16[64,1280]{1,0:T(8,128)(2,1)S(1)}, u32[]{:S(2)}, u32[]{:S(2)}) collective-permute-start(bf16[64,1280]{1,0:T(8,128)(2,1)S(1)} %slice.128), channel_id=1, source_target_pairs={{0,1},{1,0},{2,3},{3,2},{4,5},{5,4},{6,7},{7,6},{8,9},{9,8},{10,11... | collective-permute-start | bytes 491528 | tf_op jit(solution)/shard_map/ppermute | solution.py:41
  42.2 21.2 %collective-permute-start.11 = (bf16[160,2048]{1,0:T(8,128)(2,1)S(1)}, bf16[160,2048]{1,0:T(8,128)(2,1)S(1)}, u32[]{:S(2)}, u32[]{:S(2)}) collective-permute-start(bf16[160,2048]{1,0:T(8,128)(2,1)S(1)} %pad_maximum_fusion.kv_ref), channel_id=1, source_target_pairs={{0,16},{1,17},{2,18},{3,19},{4,20},{5,21},{6,22},{7,23},{8,24},{9,... | collective-permute-start | bytes 1966088 | tf_op jit(solution)/shard_map/ppermute | solution.py:41
  43.6 19.9 %collective-permute-start.10 = (bf16[160,2048]{1,0:T(8,128)(2,1)S(1)}, bf16[160,2048]{1,0:T(8,128)(2,1)S(1)}, u32[]{:S(2)}, u32[]{:S(2)}) collective-permute-start(bf16[160,2048]{1,0:T(8,128)(2,1)S(1)} %pad_maximum_fusion.kv_ref), channel_id=1, source_target_pairs={{0,96},{1,97},{2,98},{3,99},{4,100},{5,101},{6,102},{7,103},{8,104... | collective-permute-start | bytes 1966088 | tf_op jit(solution)/shard_map/ppermute | solution.py:41
  46.6 17.4 %collective-permute-start.9 = (bf16[160,2048]{1,0:T(8,128)(2,1)S(1)}, bf16[160,2048]{1,0:T(8,128)(2,1)S(1)}, u32[]{:S(2)}, u32[]{:S(2)}) collective-permute-start(bf16[160,2048]{1,0:T(8,128)(2,1)S(1)} %pad_maximum_fusion.kv_ref), channel_id=1, source_target_pairs={{0,32},{1,33},{2,34},{3,35},{4,36},{5,37},{6,38},{7,39},{8,40},{9,... | collective-permute-start | bytes 1966088 | tf_op jit(solution)/shard_map/ppermute | solution.py:41
  64.0 49.9 %collective-permute-start.14 = (bf16[160,2048]{1,0:T(8,128)(2,1)S(1)}, bf16[160,2048]{1,0:T(8,128)(2,1)S(1)}, u32[]{:S(2)}, u32[]{:S(2)}) collective-permute-start(bf16[160,2048]{1,0:T(8,128)(2,1)S(1)} %collective-permute-done.9.refs_0_), channel_id=1, source_target_pairs={{0,32},{1,33},{2,34},{3,35},{4,36},{5,37},{6,38},{7,39},{8,40},{9,... | collective-permute-start | bytes 1966088 | tf_op jit(solution)/shard_map/ppermute | solution.py:41
  64.1 51.2 %collective-permute-start.12 = (bf16[160,2048]{1,0:T(8,128)(2,1)S(1)}, bf16[160,2048]{1,0:T(8,128)(2,1)S(1)}, u32[]{:S(2)}, u32[]{:S(2)}) collective-permute-start(bf16[160,2048]{1,0:T(8,128)(2,1)S(1)} %collective-permute-done.9.refs_0_), channel_id=1, source_target_pairs={{0,16},{1,17},{2,18},{3,19},{4,20},{5,21},{6,22},{7,23},{8,24},{9,... | collective-permute-start | bytes 1966088 | tf_op jit(solution)/shard_map/ppermute | solution.py:41
  64.9 50.6 %collective-permute-start.16 = (bf16[160,2048]{1,0:T(8,128)(2,1)S(1)}, bf16[160,2048]{1,0:T(8,128)(2,1)S(1)}, u32[]{:S(2)}, u32[]{:S(2)}) collective-permute-start(bf16[160,2048]{1,0:T(8,128)(2,1)S(1)} %collective-permute-done.11.refs_2_), channel_id=1, source_target_pairs={{0,96},{1,97},{2,98},{3,99},{4,100},{5,101},{6,102},{7,103},{8,104... | collective-permute-start | bytes 1966088 | tf_op jit(solution)/shard_map/ppermute | solution.py:41
  114.0 47.5 %collective-permute-start.15 = (bf16[160,1024]{1,0:T(8,128)(2,1)S(1)}, bf16[160,1024]{1,0:T(8,128)(2,1)S(1)}, u32[]{:S(2)}, u32[]{:S(2)}) collective-permute-start(bf16[160,1024]{1,0:T(8,128)(2,1)S(1)} %slice.131), channel_id=1, source_target_pairs={{0,16},{1,17},{2,18},{3,19},{4,20},{5,21},{6,22},{7,23},{8,24},{9,... | collective-permute-start | bytes 983048 | tf_op jit(solution)/shard_map/ppermute | solution.py:41
  115.4 46.1 %collective-permute-start.13 = (bf16[160,1024]{1,0:T(8,128)(2,1)S(1)}, bf16[160,1024]{1,0:T(8,128)(2,1)S(1)}, u32[]{:S(2)}, u32[]{:S(2)}) collective-permute-start(bf16[160,1024]{1,0:T(8,128)(2,1)S(1)} %slice.130), channel_id=1, source_target_pairs={{0,32},{1,33},{2,34},{3,35},{4,36},{5,37},{6,38},{7,39},{8,40},{9,... | collective-permute-start | bytes 983048 | tf_op jit(solution)/shard_map/ppermute | solution.py:41
  179.5 12.2 %collective-permute-start.20 = (bf16[160,1024]{1,0:T(8,128)(2,1)S(1)}, bf16[160,1024]{1,0:T(8,128)(2,1)S(1)}, u32[]{:S(2)}, u32[]{:S(2)}) collective-permute-start(bf16[160,1024]{1,0:T(8,128)(2,1)S(1)} %constant_dynamic-update-slice_fusion.refs_0_), channel_id=1, source_target_pairs={{0,1},{1,0},{2,3},{3,2},{4,5},{5,4},{6,7},{7,6},{8,9},{9,8},{10,11... | collective-permute-start | bytes 983048 | tf_op jit(solution)/shard_map/ppermute | solution.py:41
  183.7 9.5 %collective-permute-start.19 = (bf16[160,1024]{1,0:T(8,128)(2,1)S(1)}, bf16[160,1024]{1,0:T(8,128)(2,1)S(1)}, u32[]{:S(2)}, u32[]{:S(2)}) collective-permute-start(bf16[160,1024]{1,0:T(8,128)(2,1)S(1)} %constant_dynamic-update-slice_fusion.refs_0_), channel_id=1, source_target_pairs={{0,6},{1,7},{2,0},{3,1},{4,2},{5,3},{6,4},{7,5},{8,14},{9,15},{10,... | collective-permute-start | bytes 983048 | tf_op jit(solution)/shard_map/ppermute | solution.py:41
  183.7 10.7 %collective-permute-start.18 = (bf16[160,1024]{1,0:T(8,128)(2,1)S(1)}, bf16[160,1024]{1,0:T(8,128)(2,1)S(1)}, u32[]{:S(2)}, u32[]{:S(2)}) collective-permute-start(bf16[160,1024]{1,0:T(8,128)(2,1)S(1)} %constant_dynamic-update-slice_fusion.refs_0_), channel_id=1, source_target_pairs={{0,2},{1,3},{2,4},{3,5},{4,6},{5,7},{6,0},{7,1},{8,10},{9,11},{10,... | collective-permute-start | bytes 983048 | tf_op jit(solution)/shard_map/ppermute | solution.py:41
  194.4 10.1 %collective-permute-start.22 = (bf16[160,1024]{1,0:T(8,128)(2,1)S(1)}, bf16[160,1024]{1,0:T(8,128)(2,1)S(1)}, u32[]{:S(2)}, u32[]{:S(2)}) collective-permute-start(bf16[160,1024]{1,0:T(8,128)(2,1)S(1)} %collective-permute-done.18.refs_1_), channel_id=1, source_target_pairs={{0,1},{1,0},{2,3},{3,2},{4,5},{5,4},{6,7},{7,6},{8,9},{9,8},{10,11... | collective-permute-start | bytes 983048 | tf_op jit(solution)/shard_map/ppermute | solution.py:41
  196.4 9.3 %collective-permute-start.21 = (bf16[160,1024]{1,0:T(8,128)(2,1)S(1)}, bf16[160,1024]{1,0:T(8,128)(2,1)S(1)}, u32[]{:S(2)}, u32[]{:S(2)}) collective-permute-start(bf16[160,1024]{1,0:T(8,128)(2,1)S(1)} %collective-permute-done.18.refs_1_), channel_id=1, source_target_pairs={{0,2},{1,3},{2,4},{3,5},{4,6},{5,7},{6,0},{7,1},{8,10},{9,11},{10,... | collective-permute-start | bytes 983048 | tf_op jit(solution)/shard_map/ppermute | solution.py:41
  196.4 11.4 %collective-permute-start.23 = (bf16[160,1024]{1,0:T(8,128)(2,1)S(1)}, bf16[160,1024]{1,0:T(8,128)(2,1)S(1)}, u32[]{:S(2)}, u32[]{:S(2)}) collective-permute-start(bf16[160,1024]{1,0:T(8,128)(2,1)S(1)} %collective-permute-done.20.refs_3_), channel_id=1, source_target_pairs={{0,6},{1,7},{2,0},{3,1},{4,2},{5,3},{6,4},{7,5},{8,14},{9,15},{10,... | collective-permute-start | bytes 983048 | tf_op jit(solution)/shard_map/ppermute | solution.py:41
  205.7 7.1 %collective-permute-start.25 = (bf16[80,1024]{1,0:T(8,128)(2,1)S(1)}, bf16[80,1024]{1,0:T(8,128)(2,1)S(1)}, u32[]{:S(2)}, u32[]{:S(2)}) collective-permute-start(bf16[80,1024]{1,0:T(8,128)(2,1)S(1)} %slice.133), channel_id=1, source_target_pairs={{0,1},{1,0},{2,3},{3,2},{4,5},{5,4},{6,7},{7,6},{8,9},{9,8},{10,11... | collective-permute-start | bytes 491528 | tf_op jit(solution)/shard_map/ppermute | solution.py:41
  226.4 8.0 %collective-permute-start.26 = (bf16[64,2304]{1,0:T(8,128)(2,1)S(1)}, bf16[64,2304]{1,0:T(8,128)(2,1)S(1)}, u32[]{:S(2)}, u32[]{:S(2)}) collective-permute-start(bf16[64,2304]{1,0:T(8,128)(2,1)S(1)} %get-tuple-element.71), channel_id=1, source_target_pairs={{0,2},{1,3},{2,4},{3,5},{4,6},{5,7},{6,0},{7,1},{8,10},{9,11},{10,... | collective-permute-start | bytes 884744 | tf_op jit(solution)/shard_map/ppermute | solution.py:41
  226.5 8.4 %collective-permute-start.28 = (bf16[64,2304]{1,0:T(8,128)(2,1)S(1)}, bf16[64,2304]{1,0:T(8,128)(2,1)S(1)}, u32[]{:S(2)}, u32[]{:S(2)}) collective-permute-start(bf16[64,2304]{1,0:T(8,128)(2,1)S(1)} %get-tuple-element.72), channel_id=1, source_target_pairs={{0,6},{1,7},{2,0},{3,1},{4,2},{5,3},{6,4},{7,5},{8,14},{9,15},{10,... | collective-permute-start | bytes 884744 | tf_op jit(solution)/shard_map/ppermute | solution.py:41
  229.7 19.6 %collective-permute-start.31 = (bf16[128,3584]{1,0:T(8,128)(2,1)S(1)}, bf16[128,3584]{1,0:T(8,128)(2,1)S(1)}, u32[]{:S(2)}, u32[]{:S(2)}) collective-permute-start(bf16[128,3584]{1,0:T(8,128)(2,1)S(1)} %slice.134), channel_id=1, source_target_pairs={{0,1},{1,0},{2,3},{3,2},{4,5},{5,4},{6,7},{7,6},{8,9},{9,8},{10,11... | collective-permute-start | bytes 2752520 | tf_op jit(solution)/shard_map/ppermute | solution.py:41
  235.1 17.9 %collective-permute-start.29 = (bf16[64,4608]{1,0:T(8,128)(2,1)S(1)}, bf16[64,4608]{1,0:T(8,128)(2,1)S(1)}, u32[]{:S(2)}, u32[]{:S(2)}) collective-permute-start(bf16[64,4608]{1,0:T(8,128)(2,1)S(1)} %pad_maximum_fusion.2), channel_id=1, source_target_pairs={{0,6},{1,7},{2,0},{3,1},{4,2},{5,3},{6,4},{7,5},{8,14},{9,15},{10,... | collective-permute-start | bytes 1769480 | tf_op jit(solution)/shard_map/ppermute | solution.py:41
  238.9 14.1 %collective-permute-start.27 = (bf16[64,4608]{1,0:T(8,128)(2,1)S(1)}, bf16[64,4608]{1,0:T(8,128)(2,1)S(1)}, u32[]{:S(2)}, u32[]{:S(2)}) collective-permute-start(bf16[64,4608]{1,0:T(8,128)(2,1)S(1)} %pad_maximum_fusion.1), channel_id=1, source_target_pairs={{0,2},{1,3},{2,4},{3,5},{4,6},{5,7},{6,0},{7,1},{8,10},{9,11},{10,... | collective-permute-start | bytes 1769480 | tf_op jit(solution)/shard_map/ppermute | solution.py:41
  249.8 6.8 %collective-permute-start.34 = (bf16[32,1792]{1,0:T(8,128)(2,1)S(1)}, bf16[32,1792]{1,0:T(8,128)(2,1)S(1)}, u32[]{:S(2)}, u32[]{:S(2)}) collective-permute-start(bf16[32,1792]{1,0:T(8,128)(2,1)S(1)} %get-tuple-element.78), channel_id=1, source_target_pairs={{0,6},{1,7},{2,0},{3,1},{4,2},{5,3},{6,4},{7,5},{8,14},{9,15},{10,... | collective-permute-start | bytes 344072 | tf_op jit(solution)/shard_map/ppermute | solution.py:41
  253.3 8.3 %collective-permute-start.30 = (bf16[32,4608]{1,0:T(8,128)(2,1)S(1)}, bf16[32,4608]{1,0:T(8,128)(2,1)S(1)}, u32[]{:S(2)}, u32[]{:S(2)}) collective-permute-start(bf16[32,4608]{1,0:T(8,128)(2,1)S(1)} %slice.165), channel_id=1, source_target_pairs={{0,1},{1,0},{2,3},{3,2},{4,5},{5,4},{6,7},{7,6},{8,9},{9,8},{10,11... | collective-permute-start | bytes 884744 | tf_op jit(solution)/shard_map/ppermute | solution.py:41
  256.7 7.3 %collective-permute-start.35 = (bf16[32,3584]{1,0:T(8,128)(2,1)S(1)}, bf16[32,3584]{1,0:T(8,128)(2,1)S(1)}, u32[]{:S(2)}, u32[]{:S(2)}) collective-permute-start(bf16[32,3584]{1,0:T(8,128)(2,1)S(1)} %pad_maximum_fusion.4), channel_id=1, source_target_pairs={{0,6},{1,7},{2,0},{3,1},{4,2},{5,3},{6,4},{7,5},{8,14},{9,15},{10,... | collective-permute-start | bytes 688136 | tf_op jit(solution)/shard_map/ppermute | solution.py:41
  260.4 7.3 %collective-permute-start.33 = (bf16[32,3584]{1,0:T(8,128)(2,1)S(1)}, bf16[32,3584]{1,0:T(8,128)(2,1)S(1)}, u32[]{:S(2)}, u32[]{:S(2)}) collective-permute-start(bf16[32,3584]{1,0:T(8,128)(2,1)S(1)} %pad_maximum_fusion.3), channel_id=1, source_target_pairs={{0,2},{1,3},{2,4},{3,5},{4,6},{5,7},{6,0},{7,1},{8,10},{9,11},{10,... | collective-permute-start | bytes 688136 | tf_op jit(solution)/shard_map/ppermute | solution.py:41
  (16 other events, 422.9 us)

commit v2 on v1

--- a/solution.py
+++ b/solution.py
@@ -49,7 +49,7 @@
     return pl.BlockSpec(memory_space=pltpu.SMEM)
 
 
-def call(kernel, outs, ins, scratch=(), flops=0, nbytes=0, exps=0, grant=8):
+def call(kernel, outs, ins, scratch=(), flops=0, nbytes=0, exps=0, grant=8, alias=None):
     specs = [smem() if k == "s" else vmem() for k, _ in ins]
     return pl.pallas_call(
         kernel,
@@ -57,6 +57,7 @@
         in_specs=specs,
         out_specs=jax.tree.map(lambda _: vmem(), outs),
         scratch_shapes=list(scratch),
+        input_output_aliases=alias or {},
         cost_estimate=pl.CostEstimate(flops=flops, bytes_accessed=nbytes, transcendentals=exps),
         compiler_params=pltpu.CompilerParams(vmem_limit_bytes=grant * 2**20),
     )(*[a for _, a in ins])
@@ -68,9 +69,9 @@
     return center * lax.rsqrt(spread + EPSILON) * gain
 
 
-def project_kernel(c_ref, *refs):
-    tiles, rest = refs[:9], refs[9:]
-    gain_ref, wq, wk, wv, cos_ref, sin_ref, q_out, kv_out, other_out = rest
+def project_kernel(groups, at, c_ref, gain_ref, wq, wk, wv, cos_ref, sin_ref, *refs):
+    tiles = refs[: sum(groups)]
+    q_out, kv_out, other_out = refs[-3:]
     mine = pl.multiple_of(c_ref[0] * HEAD_DIM, 16)
     others = pl.multiple_of((1 - c_ref[0]) * HEAD_DIM, 16)
     weight = jnp.concatenate(
@@ -78,27 +79,28 @@
     )
     half = HEAD_DIM // 2
     scale = math.log2(math.e) / math.sqrt(HEAD_DIM)
-    groups = [tiles[0:2], tiles[2:4], tiles[4:6], tiles[6:9]]
-    for g, group in enumerate(groups):
+    for count in groups:
+        group, tiles = tiles[:count], tiles[count:]
         rows = jnp.concatenate([t[...] for t in group], axis=0).astype(F32)
         rows = norm(rows, gain_ref[...]).astype(BF)
+        span = slice(at, at + rows.shape[0])
+        at += rows.shape[0]
         mapped = lax.dot_general(
             weight, rows, (((1,), (1,)), ((), ())), preferred_element_type=F32
         )
-        at = slice(g * 256, (g + 1) * 256)
-        cos, sin = cos_ref[:, at], sin_ref[:, at]
+        cos, sin = cos_ref[:, span], sin_ref[:, span]
 
         def turn(u):
             first, second = u[:half], u[half:]
             return jnp.concatenate([first * cos - second * sin, second * cos + first * sin], axis=0)
 
         part = [mapped[k * HEAD_DIM : (k + 1) * HEAD_DIM] for k in range(6)]
-        q_out[:, at] = (turn(part[0]) * scale).astype(BF)
-        kv_out[:HEAD_DIM, at] = turn(part[1]).astype(BF)
-        kv_out[HEAD_DIM:, at] = part[2].astype(BF)
-        other_out[:HEAD_DIM, at] = (turn(part[3]) * scale).astype(BF)
-        other_out[HEAD_DIM : 2 * HEAD_DIM, at] = turn(part[4]).astype(BF)
-        other_out[2 * HEAD_DIM :, at] = part[5].astype(BF)
+        q_out[:, span] = (turn(part[0]) * scale).astype(BF)
+        kv_out[:HEAD_DIM, span] = turn(part[1]).astype(BF)
+        kv_out[HEAD_DIM:, span] = part[2].astype(BF)
+        other_out[:HEAD_DIM, span] = (turn(part[3]) * scale).astype(BF)
+        other_out[HEAD_DIM : 2 * HEAD_DIM, span] = turn(part[4]).astype(BF)
+        other_out[2 * HEAD_DIM :, span] = part[5].astype(BF)
 
 
 def split_rows(m):
@@ -217,29 +219,48 @@
             out_ref[:, target] = (total[:HEAD_DIM, cols] / mass).astype(BF)
 
 
-def merge_kernel(col_ref, c_ref, *refs):
-    pieces, tiles, rest = refs[:9], refs[9:18], refs[18:]
-    out_weight, gain_ref, up_weight, bias_ref = rest[:4]
-    hidden_a, hidden_b, att_all, token_all, mixed_all, merged = rest[4:]
-    starts = [0, 0, 0, 0, 0, 0, 0, 0, 80]
-    slots = [0, 1, 2, 3, 4, 5, 6, 7, 7]
-    c, x, zh = c_ref[0], c_ref[1], c_ref[2]
-    for piece, tile, slot, lower in zip(pieces, tiles, slots, starts):
-        for part in range(piece.shape[0] // 80):
-            odd = (lower + part * 80) // 80
-            spot = col_ref[slot] * 160 + (c if odd == 0 else 1 - c) * 80
-            att_all[pl.ds(pl.multiple_of(spot, 16), 80), :] = piece[part * 80 : (part + 1) * 80, :]
-        row = slot * 128 + (64 if lower else 0)
-        token_all[row : row + tile.shape[0], :] = tile[...]
+def add_heads(slots, pieces, col_ref, c, weight_ref, base_ref, out_ref):
+    rows = []
+    for slot in slots:
+        for head in (c, 1 - c):
+            spot = pl.multiple_of(col_ref[slot] * 160 + head * 80, 16)
+            rows.append(weight_ref[pl.ds(spot, 80), :])
+    weight = jnp.concatenate(rows, axis=0)
+
+    def block(i, carry):
+        spot = pl.ds(pl.multiple_of(i * 512, 512), 512)
+        lhs = jnp.concatenate([p[:, spot] for p in pieces], axis=0).T
+        out_ref[spot, :] = base_ref[spot, :] + jnp.dot(lhs, weight, preferred_element_type=F32)
+        return carry
+
+    lax.fori_loop(0, out_ref.shape[0] // 512, block, 0)
+
+
+def mix_first_kernel(col_ref, place_ref, weight_ref, *refs):
+    pieces, tiles, out_ref = refs[:4], refs[4:13], refs[13]
+    for slot in range(8):
+        row = col_ref[slot] * 128
+        if slot < 7:
+            spot = pl.ds(pl.multiple_of(row, 128), 128)
+            out_ref[spot, :] = tiles[slot][...].astype(F32)
+        else:
+            for k in range(2):
+                spot = pl.ds(pl.multiple_of(row + k * 64, 64), 64)
+                out_ref[spot, :] = tiles[7 + k][...].astype(F32)
+    add_heads((0, 1, 2, 3), pieces, col_ref, place_ref[0], weight_ref, out_ref, out_ref)
+
+
+def mix_next_kernel(col_ref, place_ref, weight_ref, *refs):
+    pieces, base_ref, out_ref = refs[:3], refs[3], refs[4]
+    add_heads((4, 5, 6), pieces, col_ref, place_ref[0], weight_ref, base_ref, out_ref)
+
+
+def merge_kernel(col_ref, place_ref, out_weight, *refs):
+    pieces, rest = refs[:2], refs[2:]
+    base_ref, gain_ref, up_weight, bias_ref, hidden_a, hidden_b, mixed_all, merged = rest
+    c, x, zh = place_ref[0], place_ref[1], place_ref[2]
     width = out_weight.shape[1]
-
-    def project(i, carry):
-        spot = pl.ds(pl.multiple_of(i * 512, 512), 512)
-        lhs = att_all[:, spot].T
-        mixed_all[spot, :] = jnp.dot(lhs, out_weight[...], preferred_element_type=F32)
-        return carry
-
-    lax.fori_loop(0, 2, project, 0)
+    add_heads((7,), pieces, col_ref, c, out_weight, base_ref, mixed_all)
     r = lax.broadcasted_iota(jnp.int32, (128, 128), 0)
     t = lax.broadcasted_iota(jnp.int32, (128, 128), 1)
     a, b, u, w = r >> 6, (r >> 5) & 1, (r >> 3) & 3, r & 7
@@ -249,9 +270,7 @@
         for k in range(4):
             s = turn * 4 + k
             spot = pl.ds(pl.multiple_of(col_ref[s] * 128, 128), 128)
-            own = pl.ds(pl.multiple_of(s * 128, 128), 128)
-            residual = token_all[own, :].astype(F32) + mixed_all[spot, :]
-            normed = norm(residual, gain_ref[...]).astype(BF)
+            normed = norm(mixed_all[spot, :], gain_ref[...]).astype(BF)
             ordered = jnp.dot(pick, normed, preferred_element_type=F32).astype(BF)
             rows = pl.ds(pl.multiple_of(s * 32, 32), 32)
             for q in range(4):
@@ -337,15 +356,28 @@
     tokens = patches.reshape(tile, model_width)
     gains = [v.reshape(1, -1) for v in (norm_gain, merge_gain, up_bias)]
     tiles, (cos, sin, gains) = spread(tokens, "x", mirror_x, 0, (cos, sin, gains))
-    q_own, kv_own, other = call(
-        project_kernel,
-        (sds((HEAD_DIM, band), BF), sds((2 * HEAD_DIM, band), BF), sds((3 * HEAD_DIM, band), BF)),
-        [("s", c.reshape(1).astype(jnp.int32))]
-        + [("v", t) for t in tiles]
-        + [("v", gains[0])]
-        + [("v", query_weight.T), ("v", key_weight.T), ("v", value_weight.T), ("v", cos), ("v", sin)],
-        flops=2 * band * model_width * 480,
-    )
+    shapes = (
+        sds((HEAD_DIM, band), BF),
+        sds((2 * HEAD_DIM, band), BF),
+        sds((3 * HEAD_DIM, band), BF),
+    )
+    fixed = [("s", c.reshape(1).astype(jnp.int32)), ("v", gains[0])]
+    fixed += [("v", w.T) for w in (query_weight, key_weight, value_weight)]
+    fixed += [("v", cos), ("v", sin)]
+    mapped = ()
+    for k, (groups, used) in enumerate(
+        (((2, 2), tiles[:4]), ((2, 1), tiles[4:7]), ((2,), tiles[7:]))
+    ):
+        first = (0, 4, 7)[k]
+        spot = len(fixed) + len(used)
+        mapped = call(
+            functools.partial(project_kernel, groups, first * tile),
+            shapes,
+            fixed + [("v", t) for t in used] + [("v", t) for t in mapped],
+            flops=2 * tile * (4, 3, 1)[k] * model_width * 480,
+            alias={spot + o: o for o in range(len(mapped))},
+        )
+    q_own, kv_own, other = mapped
     n = 2 * band
     swap = pairs(lambda d: {"c": 1 - d["c"]})
     mirror_y = pairs(lambda d: {"zl": 1 - d["zl"]})
@@ -394,24 +426,36 @@
     )
     attended = jnp.concatenate([attended, send(partner, swap)], axis=0)
     pieces, _ = spread(attended, "x", mirror_x, 0)
+    where = [
+        ("s", slot_col),
+        ("s", jnp.stack([c, x, zh]).astype(jnp.int32)),
+        ("v", out_weight),
+    ]
+    total = sds((band, model_width), F32)
+    total_flops = 2 * band * model_width * model_width
+    mixed = call(
+        mix_first_kernel,
+        total,
+        where + [("v", t) for t in (*pieces[:4], *tiles)],
+        flops=total_flops // 2,
+        grant=10,
+    )
+    mixed = call(
+        mix_next_kernel,
+        total,
+        where + [("v", t) for t in (*pieces[4:7], mixed)],
+        flops=3 * total_flops // 8,
+        grant=10,
+        alias={6: 0},
+    )
     hidden_a, hidden_b = call(
         merge_kernel,
         (sds((256, up_weight.shape[1]), BF),) * 2,
-        [("s", slot_col), ("s", jnp.stack([c, x, zh]).astype(jnp.int32))]
-        + [("v", t) for t in (*pieces, *tiles)]
-        + [
-            ("v", out_weight),
-            ("v", gains[1]),
-            ("v", up_weight),
-            ("v", gains[2]),
-        ],
-        [
-            pltpu.VMEM((model_width, band), BF),
-            pltpu.VMEM((band, model_width), BF),
-            pltpu.VMEM((band, model_width), F32),
-            pltpu.VMEM((4, 256, model_width), BF),
-        ],
-        flops=2 * 256 * 5120 * 640 + 2 * band * model_width * model_width,
+        where
+        + [("v", t) for t in (*pieces[7:], mixed, gains[1])]
+        + [("v", up_weight), ("v", gains[2])],
+        [pltpu.VMEM((band, model_width), F32), pltpu.VMEM((4, 256, model_width), BF)],
+        flops=2 * 256 * 5120 * 640 + total_flops // 8,
         grant=18,
     )
     return scatter_output(hidden_a, hidden_b, down_weight, down_bias, mirror_x)

time: 269 us -> 261 us (0.970)
  waiting for transfers between devices: 60.2 us -> 45.4 us
  Pallas kernels: 138 us -> 141 us
    ppermute x36, waiting for transfers between devices: 60.2 us -> 45.4 us  [send(): return lax.ppermute(value, AXES, perm)]
    pallas_call x6 -> x10, Pallas kernels: 138 us -> 141 us  [call(): pl.pallas_call(kernel, out_shape=outs, in_specs=specs, out_specs=jax.tree...]
  transfers between devices with their start and end apart: 36 -> 36, of which waited for: 24 -> 16; matrix products, arithmetic and copies ran while one was open for 2% -> 2% of each run, Pallas kernels for 40% -> 45%
where the time goes in v2:
time: 261 us; the launch traced here: 260 us
  Pallas kernels  141 us (54%)
  starting transfers between devices  58 us (22%)
  waiting for transfers between devices  45.4 us (17%)
  local copies, waits for them, and re-layouts  6.63 us (3%)
  other arithmetic  3.97 us (2%)
  matrix products  3.67 us (1%)
    pallas_call x10, Pallas kernels, call(): pl.pallas_call(kernel, out_shape=outs, in_specs=specs, out_specs=jax.tree...  141 us
    ppermute x36, starting transfers between devices, send(): return lax.ppermute(value, AXES, perm)  58 us
    ppermute x36, waiting for transfers between devices, send(): return lax.ppermute(value, AXES, perm)  45.4 us
  transfers between devices with their start and end apart: 36, of which 16 were waited for; matrix products, arithmetic and copies ran while one was open for 2% of the time, Pallas kernels for 45%

profile of v2, /device:TPU:0, one launch (start us, length us, event | category | flops | bytes accessed | tf_op | source)
XLA Modules:
  0.0 259.6 jit_solution(10547784938867743634)
XLA Ops:
  3.2 4.0 %collective-permute-start.2 = (bf16[128,1280]{1,0:T(8,128)(2,1)}, bf16[128,1280]{1,0:T(8,128)(2,1)S(1)}, u32[]{:S(2)}, u32[]{:S(2)}) collective-permute-start(bf16[128,1280]{1,0:T(8,128)(2,1)} %bitcast.30), channel_id=1, source_target_pairs={{0,1},{1,0},{2,3},{3,2},{4,5},{5,4},{6,7},{7,6},{8,9},{9,8},{10,11... | collective-permute-start | bytes 983048 | tf_op jit(solution)/shard_map/ppermute | solution.py:41
  11.6 3.0 %collective-permute-done.2.refs_3_.refs_7_ = bf16[128,1280]{1,0:T(8,128)(2,1)S(1)} collective-permute-done((bf16[128,1280]{1,0:T(8,128)(2,1)}, bf16[128,1280]{1,0:T(8,128)(2,1)S(1)}, u32[]{:S(2)}, u32[]{:S(2)}) %collective-permute-start.2) | collective-permute-done | bytes 327712 | tf_op jit(solution)/shard_map/ppermute | solution.py:41
  14.6 3.2 %collective-permute-start.3 = (bf16[128,1280]{1,0:T(8,128)(2,1)S(1)}, bf16[128,1280]{1,0:T(8,128)(2,1)S(1)}, u32[]{:S(2)}, u32[]{:S(2)}) collective-permute-start(bf16[128,1280]{1,0:T(8,128)(2,1)S(1)} %collective-permute-done.refs_1_.refs_5_), channel_id=1, source_target_pairs={{0,1},{1,0},{2,3},{3,2},{4,5},{5,4},{6,7},{7,6},{8,9},{9,8},{10,11... | collective-permute-start | bytes 983048 | tf_op jit(solution)/shard_map/ppermute | solution.py:41
  18.1 3.0 %collective-permute-start.7 = (bf16[128,1280]{1,0:T(8,128)(2,1)S(1)}, bf16[128,1280]{1,0:T(8,128)(2,1)S(1)}, u32[]{:S(2)}, u32[]{:S(2)}) collective-permute-start(bf16[128,1280]{1,0:T(8,128)(2,1)S(1)} %collective-permute-done.2.refs_3_.refs_7_), channel_id=1, source_target_pairs={{0,6},{1,7},{2,0},{3,1},{4,2},{5,3},{6,4},{7,5},{8,14},{9,15},{10,... | collective-permute-start | bytes 983048 | tf_op jit(solution)/shard_map/ppermute | solution.py:41
  21.1 3.4 %collective-permute-done.3.refs_1_.refs_9_ = bf16[128,1280]{1,0:T(8,128)(2,1)S(1)} collective-permute-done((bf16[128,1280]{1,0:T(8,128)(2,1)S(1)}, bf16[128,1280]{1,0:T(8,128)(2,1)S(1)}, u32[]{:S(2)}, u32[]{:S(2)}) %collective-permute-start.3) | collective-permute-done | bytes 327712 | tf_op jit(solution)/shard_map/ppermute | solution.py:41
  24.8 2.6 %collective-permute-done.5.refs_0_.refs_8_ = bf16[128,1280]{1,0:T(8,128)(2,1)S(1)} collective-permute-done((bf16[128,1280]{1,0:T(8,128)(2,1)S(1)}, bf16[128,1280]{1,0:T(8,128)(2,1)S(1)}, u32[]{:S(2)}, u32[]{:S(2)}) %collective-permute-start.5) | collective-permute-done | bytes 327712 | tf_op jit(solution)/shard_map/ppermute | solution.py:41
  35.5 1.9 collective-permute-done.8.swapped
  37.4 3.1 %collective-permute-start.10 = (bf16[160,2048]{1,0:T(8,128)(2,1)S(1)}, bf16[160,2048]{1,0:T(8,128)(2,1)S(1)}, u32[]{:S(2)}, u32[]{:S(2)}) collective-permute-start(bf16[160,2048]{1,0:T(8,128)(2,1)S(1)} %pad_maximum_fusion.kv_ref), channel_id=1, source_target_pairs={{0,96},{1,97},{2,98},{3,99},{4,100},{5,101},{6,102},{7,103},{8,104... | collective-permute-start | bytes 1966088 | tf_op jit(solution)/shard_map/ppermute | solution.py:41
  41.6 16.8 %shard_map.130 = (bf16[96,2048]{1,0:T(8,128)(2,1)S(1)}, f32[8,2048]{1,0:T(8,128)S(1)}, f32[8,2048]{1,0:T(8,128)S(1)}, f32[96,2048]{1,0:T(8,128)S(1)}) custom-call(bf16[80,1024]{1,0:T(8,128)(2,1)S(1)} %get-tuple-element.57.own_q, bf16[240,1024]{1,0:T(8,128)(2,1)S(1)} %collective-permute-done.8.swapped, bf16[160,2048]{1,0:T(8,128)(2,1)S(1)} %pad_maximum_fusion.kv_ref), custom_call_target="tpu_custom_call" | custom-call | flops 4294967296 | bytes 786432 | tf_op jit(solution)/shard_map/pallas_call | solution.py:54
  60.1 3.1 %collective-permute-start.16 = (bf16[160,2048]{1,0:T(8,128)(2,1)S(1)}, bf16[160,2048]{1,0:T(8,128)(2,1)S(1)}, u32[]{:S(2)}, u32[]{:S(2)}) collective-permute-start(bf16[160,2048]{1,0:T(8,128)(2,1)S(1)} %collective-permute-done.11.refs_2_), channel_id=1, source_target_pairs={{0,96},{1,97},{2,98},{3,99},{4,100},{5,101},{6,102},{7,103},{8,104... | collective-permute-start | bytes 1966088 | tf_op jit(solution)/shard_map/ppermute | solution.py:41
  63.2 45.9 %shard_map.131 = (f32[8,2048]{1,0:T(8,128)S(1)}, f32[96,2048]{1,0:T(8,128)S(1)}) custom-call(bf16[160,2048]{1,0:T(8,128)(2,1)S(1)} %collective-permute-done.9.refs_0_, bf16[160,2048]{1,0:T(8,128)(2,1)S(1)} %collective-permute-done.10.refs_1_, bf16[160,2048]{1,0:T(8,128)(2,1)S(1)} %collective-permute-done.11.refs_2_, ...), custom_call_target="tpu_custom_call" | custom-call | flops 12884901888 | bytes 786432 | tf_op jit(solution)/shard_map/pallas_call | solution.py:54
  110.4 45.9 %shard_map.132 = (f32[8,2048]{1,0:T(8,128)S(1)}, f32[96,2048]{1,0:T(8,128)S(1)}) custom-call(bf16[160,2048]{1,0:T(8,128)(2,1)S(1)} %collective-permute-done.14.refs_0_, bf16[160,2048]{1,0:T(8,128)(2,1)S(1)} %collective-permute-done.12.refs_1_, bf16[160,2048]{1,0:T(8,128)(2,1)S(1)} %collective-permute-done.16.refs_2_, ...), custom_call_target="tpu_custom_call" | custom-call | flops 12884901888 | bytes 786432 | tf_op jit(solution)/shard_map/pallas_call | solution.py:54
  156.4 16.5 %shard_map.133 = (bf16[80,1024]{1,0:T(8,128)(2,1)S(1)}, bf16[80,1024]{1,0:T(8,128)(2,1)S(1)}) custom-call(s32[8]{0:T(128)S(1)} %get-tuple-element.80.place.col_ref, bf16[160,1024]{1,0:T(8,128)(2,1)S(1)} %collective-permute-done.13.refs_0_, bf16[160,1024]{1,0:T(8,128)(2,1)S(1)} %collective-permute-done.15.refs_1_, ...), custom_call_target="tpu_custom_call" | custom-call | flops 4294967296 | bytes 786432 | tf_op jit(solution)/shard_map/pallas_call | solution.py:54
  177.6 4.1 %collective-permute-start.20 = (bf16[160,1024]{1,0:T(8,128)(2,1)S(1)}, bf16[160,1024]{1,0:T(8,128)(2,1)S(1)}, u32[]{:S(2)}, u32[]{:S(2)}) collective-permute-start(bf16[160,1024]{1,0:T(8,128)(2,1)S(1)} %constant_dynamic-update-slice_fusion.refs_0_), channel_id=1, source_target_pairs={{0,1},{1,0},{2,3},{3,2},{4,5},{5,4},{6,7},{7,6},{8,9},{9,8},{10,11... | collective-permute-start | bytes 983048 | tf_op jit(solution)/shard_map/ppermute | solution.py:41
  181.8 3.6 %collective-permute-done.18.refs_1_ = bf16[160,1024]{1,0:T(8,128)(2,1)S(1)} collective-permute-done((bf16[160,1024]{1,0:T(8,128)(2,1)S(1)}, bf16[160,1024]{1,0:T(8,128)(2,1)S(1)}, u32[]{:S(2)}, u32[]{:S(2)}) %collective-permute-start.18) | collective-permute-done | bytes 327712 | tf_op jit(solution)/shard_map/ppermute | solution.py:41
  185.4 3.8 %collective-permute-done.20.refs_3_ = bf16[160,1024]{1,0:T(8,128)(2,1)S(1)} collective-permute-done((bf16[160,1024]{1,0:T(8,128)(2,1)S(1)}, bf16[160,1024]{1,0:T(8,128)(2,1)S(1)}, u32[]{:S(2)}, u32[]{:S(2)}) %collective-permute-start.20) | collective-permute-done | bytes 327712 | tf_op jit(solution)/shard_map/ppermute | solution.py:41
  189.2 3.2 %collective-permute-start.21 = (bf16[160,1024]{1,0:T(8,128)(2,1)S(1)}, bf16[160,1024]{1,0:T(8,128)(2,1)S(1)}, u32[]{:S(2)}, u32[]{:S(2)}) collective-permute-start(bf16[160,1024]{1,0:T(8,128)(2,1)S(1)} %collective-permute-done.18.refs_1_), channel_id=1, source_target_pairs={{0,1},{1,0},{2,3},{3,2},{4,5},{5,4},{6,7},{7,6},{8,9},{9,8},{10,11... | collective-permute-start | bytes 983048 | tf_op jit(solution)/shard_map/ppermute | solution.py:41
  192.5 3.2 %collective-permute-start.25 = (bf16[160,1024]{1,0:T(8,128)(2,1)S(1)}, bf16[160,1024]{1,0:T(8,128)(2,1)S(1)}, u32[]{:S(2)}, u32[]{:S(2)}) collective-permute-start(bf16[160,1024]{1,0:T(8,128)(2,1)S(1)} %collective-permute-done.20.refs_3_), channel_id=1, source_target_pairs={{0,6},{1,7},{2,0},{3,1},{4,2},{5,3},{6,4},{7,5},{8,14},{9,15},{10,... | collective-permute-start | bytes 983048 | tf_op jit(solution)/shard_map/ppermute | solution.py:41
  195.8 3.6 %collective-permute-done.21.refs_1_ = bf16[160,1024]{1,0:T(8,128)(2,1)S(1)} collective-permute-done((bf16[160,1024]{1,0:T(8,128)(2,1)S(1)}, bf16[160,1024]{1,0:T(8,128)(2,1)S(1)}, u32[]{:S(2)}, u32[]{:S(2)}) %collective-permute-start.21) | collective-permute-done | bytes 327712 | tf_op jit(solution)/shard_map/ppermute | solution.py:41
  199.5 2.6 %collective-permute-done.23.refs_0_ = bf16[160,1024]{1,0:T(8,128)(2,1)S(1)} collective-permute-done((bf16[160,1024]{1,0:T(8,128)(2,1)S(1)}, bf16[160,1024]{1,0:T(8,128)(2,1)S(1)}, u32[]{:S(2)}, u32[]{:S(2)}) %collective-permute-start.23) | collective-permute-done | bytes 327712 | tf_op jit(solution)/shard_map/ppermute | solution.py:41
  202.8 3.5 %shard_map.134.refs_3_ = f32[1024,1280]{1,0:T(8,128)S(1)} custom-call(s32[8]{0:T(128)S(1)} %get-tuple-element.80.place.col_ref, s32[3]{0:T(128)S(1)} %pad_add_fusion.place_ref, bf16[1280,1280]{1,0:T(8,128)(2,1)S(1)} %copy-done, bf16[160,1024]{1,0:T(8,128)(2,1)S(1)} %constant_dynamic-update-slice_fusion.refs_0_, ...), custom_call_target="tpu_custom_call" | custom-call | flops 1677721600 | tf_op jit(solution)/shard_map/pallas_call | solution.py:54
  206.4 2.7 %shard_map.135.refs_2_ = f32[1024,1280]{1,0:T(8,128)S(1)} custom-call(s32[8]{0:T(128)S(1)} %get-tuple-element.80.place.col_ref, s32[3]{0:T(128)S(1)} %pad_add_fusion.place_ref, bf16[1280,1280]{1,0:T(8,128)(2,1)S(1)} %copy-done, bf16[160,1024]{1,0:T(8,128)(2,1)S(1)} %collective-permute-done.23.refs_0_, ...), custom_call_target="tpu_custom_call", output_to_operand_aliasing={{}: (6, {})} | custom-call | flops 1258291200 | tf_op jit(solution)/shard_map/pallas_call | solution.py:54
  209.2 6.5 %shard_map.136 = (bf16[256,640]{1,0:T(8,128)(2,1)S(1)}, bf16[256,640]{1,0:T(8,128)(2,1)S(1)}) custom-call(s32[8]{0:T(128)S(1)} %get-tuple-element.80.place.col_ref, s32[3]{0:T(128)S(1)} %pad_add_fusion.place_ref, bf16[1280,1280]{1,0:T(8,128)(2,1)S(1)} %copy-done, bf16[80,1024]{1,0:T(8,128)(2,1)S(1)} %collective-permute-done.22.refs_0_, ...), custom_call_target="tpu_custom_call" | custom-call | flops 2097152000 | tf_op jit(solution)/shard_map/pallas_call | solution.py:54
  217.5 2.0 convolution_convert_fusion
  219.7 3.2 %collective-permute-start.28 = (bf16[64,2304]{1,0:T(8,128)(2,1)S(1)}, bf16[64,2304]{1,0:T(8,128)(2,1)S(1)}, u32[]{:S(2)}, u32[]{:S(2)}) collective-permute-start(bf16[64,2304]{1,0:T(8,128)(2,1)S(1)} %get-tuple-element.84), channel_id=1, source_target_pairs={{0,6},{1,7},{2,0},{3,1},{4,2},{5,3},{6,4},{7,5},{8,14},{9,15},{10,... | collective-permute-start | bytes 884744 | tf_op jit(solution)/shard_map/ppermute | solution.py:41
  222.9 3.1 %collective-permute-start.31 = (bf16[128,3584]{1,0:T(8,128)(2,1)S(1)}, bf16[128,3584]{1,0:T(8,128)(2,1)S(1)}, u32[]{:S(2)}, u32[]{:S(2)}) collective-permute-start(bf16[128,3584]{1,0:T(8,128)(2,1)S(1)} %slice.134), channel_id=1, source_target_pairs={{0,1},{1,0},{2,3},{3,2},{4,5},{5,4},{6,7},{7,6},{8,9},{9,8},{10,11... | collective-permute-start | bytes 2752520 | tf_op jit(solution)/shard_map/ppermute | solution.py:41
  229.3 2.0 collective-permute-start.29
  231.3 12.4 %collective-permute-done.31 = bf16[128,3584]{1,0:T(8,128)(2,1)S(1)} collective-permute-done((bf16[128,3584]{1,0:T(8,128)(2,1)S(1)}, bf16[128,3584]{1,0:T(8,128)(2,1)S(1)}, u32[]{:S(2)}, u32[]{:S(2)}) %collective-permute-start.31) | collective-permute-done | bytes 917536 | tf_op jit(solution)/shard_map/ppermute | solution.py:41
  244.0 3.2 %collective-permute-start.34 = (bf16[32,1792]{1,0:T(8,128)(2,1)S(1)}, bf16[32,1792]{1,0:T(8,128)(2,1)S(1)}, u32[]{:S(2)}, u32[]{:S(2)}) collective-permute-start(bf16[32,1792]{1,0:T(8,128)(2,1)S(1)} %get-tuple-element.90), channel_id=1, source_target_pairs={{0,6},{1,7},{2,0},{3,1},{4,2},{5,3},{6,4},{7,5},{8,14},{9,15},{10,... | collective-permute-start | bytes 344072 | tf_op jit(solution)/shard_map/ppermute | solution.py:41
  247.5 2.6 collective-permute-start.30
  251.3 3.5 %collective-permute-start.35 = (bf16[32,3584]{1,0:T(8,128)(2,1)S(1)}, bf16[32,3584]{1,0:T(8,128)(2,1)S(1)}, u32[]{:S(2)}, u32[]{:S(2)}) collective-permute-start(bf16[32,3584]{1,0:T(8,128)(2,1)S(1)} %pad_maximum_fusion.4), channel_id=1, source_target_pairs={{0,6},{1,7},{2,0},{3,1},{4,2},{5,3},{6,4},{7,5},{8,14},{9,15},{10,... | collective-permute-start | bytes 688136 | tf_op jit(solution)/shard_map/ppermute | solution.py:41
  255.9 2.7 %collective-permute-done.33 = bf16[32,3584]{1,0:T(8,128)(2,1)S(1)} collective-permute-done((bf16[32,3584]{1,0:T(8,128)(2,1)S(1)}, bf16[32,3584]{1,0:T(8,128)(2,1)S(1)}, u32[]{:S(2)}, u32[]{:S(2)}) %collective-permute-start.33) | collective-permute-done | bytes 229408 | tf_op jit(solution)/shard_map/ppermute | solution.py:41
  (116 shorter events, 34.9 us)
Async XLA Ops:
  0.0 11.6 %collective-permute-start = (bf16[128,1280]{1,0:T(8,128)(2,1)}, bf16[128,1280]{1,0:T(8,128)(2,1)S(1)}, u32[]{:S(2)}, u32[]{:S(2)}) collective-permute-start(bf16[128,1280]{1,0:T(8,128)(2,1)} %bitcast.28), channel_id=1, source_target_pairs={{0,2},{1,3},{2,4},{3,5},{4,6},{5,7},{6,0},{7,1},{8,10},{9,11},{10,... | collective-permute-start | bytes 983048 | tf_op jit(solution)/shard_map/ppermute | solution.py:41
  1.6 10.0 %collective-permute-start.1 = (bf16[128,1280]{1,0:T(8,128)(2,1)}, bf16[128,1280]{1,0:T(8,128)(2,1)S(1)}, u32[]{:S(2)}, u32[]{:S(2)}) collective-permute-start(bf16[128,1280]{1,0:T(8,128)(2,1)} %bitcast.29), channel_id=1, source_target_pairs={{0,6},{1,7},{2,0},{3,1},{4,2},{5,3},{6,4},{7,5},{8,14},{9,15},{10,... | collective-permute-start | bytes 983048 | tf_op jit(solution)/shard_map/ppermute | solution.py:41
  3.2 11.4 %collective-permute-start.2 = (bf16[128,1280]{1,0:T(8,128)(2,1)}, bf16[128,1280]{1,0:T(8,128)(2,1)S(1)}, u32[]{:S(2)}, u32[]{:S(2)}) collective-permute-start(bf16[128,1280]{1,0:T(8,128)(2,1)} %bitcast.30), channel_id=1, source_target_pairs={{0,1},{1,0},{2,3},{3,2},{4,5},{5,4},{6,7},{7,6},{8,9},{9,8},{10,11... | collective-permute-start | bytes 983048 | tf_op jit(solution)/shard_map/ppermute | solution.py:41
  14.6 9.8 %collective-permute-start.3 = (bf16[128,1280]{1,0:T(8,128)(2,1)S(1)}, bf16[128,1280]{1,0:T(8,128)(2,1)S(1)}, u32[]{:S(2)}, u32[]{:S(2)}) collective-permute-start(bf16[128,1280]{1,0:T(8,128)(2,1)S(1)} %collective-permute-done.refs_1_.refs_5_), channel_id=1, source_target_pairs={{0,1},{1,0},{2,3},{3,2},{4,5},{5,4},{6,7},{7,6},{8,9},{9,8},{10,11... | collective-permute-start | bytes 983048 | tf_op jit(solution)/shard_map/ppermute | solution.py:41
  17.8 9.6 %collective-permute-start.5 = (bf16[128,1280]{1,0:T(8,128)(2,1)S(1)}, bf16[128,1280]{1,0:T(8,128)(2,1)S(1)}, u32[]{:S(2)}, u32[]{:S(2)}) collective-permute-start(bf16[128,1280]{1,0:T(8,128)(2,1)S(1)} %collective-permute-done.refs_1_.refs_5_), channel_id=1, source_target_pairs={{0,2},{1,3},{2,4},{3,5},{4,6},{5,7},{6,0},{7,1},{8,10},{9,11},{10,... | collective-permute-start | bytes 983048 | tf_op jit(solution)/shard_map/ppermute | solution.py:41
  18.1 15.2 %collective-permute-start.7 = (bf16[128,1280]{1,0:T(8,128)(2,1)S(1)}, bf16[128,1280]{1,0:T(8,128)(2,1)S(1)}, u32[]{:S(2)}, u32[]{:S(2)}) collective-permute-start(bf16[128,1280]{1,0:T(8,128)(2,1)S(1)} %collective-permute-done.2.refs_3_.refs_7_), channel_id=1, source_target_pairs={{0,6},{1,7},{2,0},{3,1},{4,2},{5,3},{6,4},{7,5},{8,14},{9,15},{10,... | collective-permute-start | bytes 983048 | tf_op jit(solution)/shard_map/ppermute | solution.py:41
  24.5 10.2 %collective-permute-start.4 = (bf16[64,1280]{1,0:T(8,128)(2,1)S(1)}, bf16[64,1280]{1,0:T(8,128)(2,1)S(1)}, u32[]{:S(2)}, u32[]{:S(2)}) collective-permute-start(bf16[64,1280]{1,0:T(8,128)(2,1)S(1)} %slice.127), channel_id=1, source_target_pairs={{0,2},{1,3},{2,4},{3,5},{4,6},{5,7},{6,0},{7,1},{8,10},{9,11},{10,... | collective-permute-start | bytes 491528 | tf_op jit(solution)/shard_map/ppermute | solution.py:41
  27.4 7.2 %collective-permute-start.6 = (bf16[64,1280]{1,0:T(8,128)(2,1)S(1)}, bf16[64,1280]{1,0:T(8,128)(2,1)S(1)}, u32[]{:S(2)}, u32[]{:S(2)}) collective-permute-start(bf16[64,1280]{1,0:T(8,128)(2,1)S(1)} %slice.128), channel_id=1, source_target_pairs={{0,1},{1,0},{2,3},{3,2},{4,5},{5,4},{6,7},{7,6},{8,9},{9,8},{10,11... | collective-permute-start | bytes 491528 | tf_op jit(solution)/shard_map/ppermute | solution.py:41
  37.4 21.0 %collective-permute-start.10 = (bf16[160,2048]{1,0:T(8,128)(2,1)S(1)}, bf16[160,2048]{1,0:T(8,128)(2,1)S(1)}, u32[]{:S(2)}, u32[]{:S(2)}) collective-permute-start(bf16[160,2048]{1,0:T(8,128)(2,1)S(1)} %pad_maximum_fusion.kv_ref), channel_id=1, source_target_pairs={{0,96},{1,97},{2,98},{3,99},{4,100},{5,101},{6,102},{7,103},{8,104... | collective-permute-start | bytes 1966088 | tf_op jit(solution)/shard_map/ppermute | solution.py:41
  40.5 17.9 %collective-permute-start.11 = (bf16[160,2048]{1,0:T(8,128)(2,1)S(1)}, bf16[160,2048]{1,0:T(8,128)(2,1)S(1)}, u32[]{:S(2)}, u32[]{:S(2)}) collective-permute-start(bf16[160,2048]{1,0:T(8,128)(2,1)S(1)} %pad_maximum_fusion.kv_ref), channel_id=1, source_target_pairs={{0,16},{1,17},{2,18},{3,19},{4,20},{5,21},{6,22},{7,23},{8,24},{9,... | collective-permute-start | bytes 1966088 | tf_op jit(solution)/shard_map/ppermute | solution.py:41
  41.6 17.4 %collective-permute-start.9 = (bf16[160,2048]{1,0:T(8,128)(2,1)S(1)}, bf16[160,2048]{1,0:T(8,128)(2,1)S(1)}, u32[]{:S(2)}, u32[]{:S(2)}) collective-permute-start(bf16[160,2048]{1,0:T(8,128)(2,1)S(1)} %pad_maximum_fusion.kv_ref), channel_id=1, source_target_pairs={{0,32},{1,33},{2,34},{3,35},{4,36},{5,37},{6,38},{7,39},{8,40},{9,... | collective-permute-start | bytes 1966088 | tf_op jit(solution)/shard_map/ppermute | solution.py:41
  59.0 50.1 %collective-permute-start.12 = (bf16[160,2048]{1,0:T(8,128)(2,1)S(1)}, bf16[160,2048]{1,0:T(8,128)(2,1)S(1)}, u32[]{:S(2)}, u32[]{:S(2)}) collective-permute-start(bf16[160,2048]{1,0:T(8,128)(2,1)S(1)} %collective-permute-done.9.refs_0_), channel_id=1, source_target_pairs={{0,16},{1,17},{2,18},{3,19},{4,20},{5,21},{6,22},{7,23},{8,24},{9,... | collective-permute-start | bytes 1966088 | tf_op jit(solution)/shard_map/ppermute | solution.py:41
  60.0 49.2 %collective-permute-start.14 = (bf16[160,2048]{1,0:T(8,128)(2,1)S(1)}, bf16[160,2048]{1,0:T(8,128)(2,1)S(1)}, u32[]{:S(2)}, u32[]{:S(2)}) collective-permute-start(bf16[160,2048]{1,0:T(8,128)(2,1)S(1)} %collective-permute-done.9.refs_0_), channel_id=1, source_target_pairs={{0,32},{1,33},{2,34},{3,35},{4,36},{5,37},{6,38},{7,39},{8,40},{9,... | collective-permute-start | bytes 1966088 | tf_op jit(solution)/shard_map/ppermute | solution.py:41
  60.1 50.3 %collective-permute-start.16 = (bf16[160,2048]{1,0:T(8,128)(2,1)S(1)}, bf16[160,2048]{1,0:T(8,128)(2,1)S(1)}, u32[]{:S(2)}, u32[]{:S(2)}) collective-permute-start(bf16[160,2048]{1,0:T(8,128)(2,1)S(1)} %collective-permute-done.11.refs_2_), channel_id=1, source_target_pairs={{0,96},{1,97},{2,98},{3,99},{4,100},{5,101},{6,102},{7,103},{8,104... | collective-permute-start | bytes 1966088 | tf_op jit(solution)/shard_map/ppermute | solution.py:41
  109.1 47.2 %collective-permute-start.13 = (bf16[160,1024]{1,0:T(8,128)(2,1)S(1)}, bf16[160,1024]{1,0:T(8,128)(2,1)S(1)}, u32[]{:S(2)}, u32[]{:S(2)}) collective-permute-start(bf16[160,1024]{1,0:T(8,128)(2,1)S(1)} %slice.130), channel_id=1, source_target_pairs={{0,32},{1,33},{2,34},{3,35},{4,36},{5,37},{6,38},{7,39},{8,40},{9,... | collective-permute-start | bytes 983048 | tf_op jit(solution)/shard_map/ppermute | solution.py:41
  109.3 47.1 %collective-permute-start.15 = (bf16[160,1024]{1,0:T(8,128)(2,1)S(1)}, bf16[160,1024]{1,0:T(8,128)(2,1)S(1)}, u32[]{:S(2)}, u32[]{:S(2)}) collective-permute-start(bf16[160,1024]{1,0:T(8,128)(2,1)S(1)} %slice.131), channel_id=1, source_target_pairs={{0,16},{1,17},{2,18},{3,19},{4,20},{5,21},{6,22},{7,23},{8,24},{9,... | collective-permute-start | bytes 983048 | tf_op jit(solution)/shard_map/ppermute | solution.py:41
  174.3 11.0 %collective-permute-start.18 = (bf16[160,1024]{1,0:T(8,128)(2,1)S(1)}, bf16[160,1024]{1,0:T(8,128)(2,1)S(1)}, u32[]{:S(2)}, u32[]{:S(2)}) collective-permute-start(bf16[160,1024]{1,0:T(8,128)(2,1)S(1)} %constant_dynamic-update-slice_fusion.refs_0_), channel_id=1, source_target_pairs={{0,2},{1,3},{2,4},{3,5},{4,6},{5,7},{6,0},{7,1},{8,10},{9,11},{10,... | collective-permute-start | bytes 983048 | tf_op jit(solution)/shard_map/ppermute | solution.py:41
  175.9 9.5 %collective-permute-start.19 = (bf16[160,1024]{1,0:T(8,128)(2,1)S(1)}, bf16[160,1024]{1,0:T(8,128)(2,1)S(1)}, u32[]{:S(2)}, u32[]{:S(2)}) collective-permute-start(bf16[160,1024]{1,0:T(8,128)(2,1)S(1)} %constant_dynamic-update-slice_fusion.refs_0_), channel_id=1, source_target_pairs={{0,6},{1,7},{2,0},{3,1},{4,2},{5,3},{6,4},{7,5},{8,14},{9,15},{10,... | collective-permute-start | bytes 983048 | tf_op jit(solution)/shard_map/ppermute | solution.py:41
  177.6 11.6 %collective-permute-start.20 = (bf16[160,1024]{1,0:T(8,128)(2,1)S(1)}, bf16[160,1024]{1,0:T(8,128)(2,1)S(1)}, u32[]{:S(2)}, u32[]{:S(2)}) collective-permute-start(bf16[160,1024]{1,0:T(8,128)(2,1)S(1)} %constant_dynamic-update-slice_fusion.refs_0_), channel_id=1, source_target_pairs={{0,1},{1,0},{2,3},{3,2},{4,5},{5,4},{6,7},{7,6},{8,9},{9,8},{10,11... | collective-permute-start | bytes 983048 | tf_op jit(solution)/shard_map/ppermute | solution.py:41
  189.2 10.1 %collective-permute-start.21 = (bf16[160,1024]{1,0:T(8,128)(2,1)S(1)}, bf16[160,1024]{1,0:T(8,128)(2,1)S(1)}, u32[]{:S(2)}, u32[]{:S(2)}) collective-permute-start(bf16[160,1024]{1,0:T(8,128)(2,1)S(1)} %collective-permute-done.18.refs_1_), channel_id=1, source_target_pairs={{0,1},{1,0},{2,3},{3,2},{4,5},{5,4},{6,7},{7,6},{8,9},{9,8},{10,11... | collective-permute-start | bytes 983048 | tf_op jit(solution)/shard_map/ppermute | solution.py:41
  192.5 9.6 %collective-permute-start.23 = (bf16[160,1024]{1,0:T(8,128)(2,1)S(1)}, bf16[160,1024]{1,0:T(8,128)(2,1)S(1)}, u32[]{:S(2)}, u32[]{:S(2)}) collective-permute-start(bf16[160,1024]{1,0:T(8,128)(2,1)S(1)} %collective-permute-done.18.refs_1_), channel_id=1, source_target_pairs={{0,2},{1,3},{2,4},{3,5},{4,6},{5,7},{6,0},{7,1},{8,10},{9,11},{10,... | collective-permute-start | bytes 983048 | tf_op jit(solution)/shard_map/ppermute | solution.py:41
  192.5 13.9 %collective-permute-start.25 = (bf16[160,1024]{1,0:T(8,128)(2,1)S(1)}, bf16[160,1024]{1,0:T(8,128)(2,1)S(1)}, u32[]{:S(2)}, u32[]{:S(2)}) collective-permute-start(bf16[160,1024]{1,0:T(8,128)(2,1)S(1)} %collective-permute-done.20.refs_3_), channel_id=1, source_target_pairs={{0,6},{1,7},{2,0},{3,1},{4,2},{5,3},{6,4},{7,5},{8,14},{9,15},{10,... | collective-permute-start | bytes 983048 | tf_op jit(solution)/shard_map/ppermute | solution.py:41
  199.4 9.7 %collective-permute-start.22 = (bf16[80,1024]{1,0:T(8,128)(2,1)S(1)}, bf16[80,1024]{1,0:T(8,128)(2,1)S(1)}, u32[]{:S(2)}, u32[]{:S(2)}) collective-permute-start(bf16[80,1024]{1,0:T(8,128)(2,1)S(1)} %slice.132), channel_id=1, source_target_pairs={{0,2},{1,3},{2,4},{3,5},{4,6},{5,7},{6,0},{7,1},{8,10},{9,11},{10,... | collective-permute-start | bytes 491528 | tf_op jit(solution)/shard_map/ppermute | solution.py:41
  202.1 7.1 %collective-permute-start.24 = (bf16[80,1024]{1,0:T(8,128)(2,1)S(1)}, bf16[80,1024]{1,0:T(8,128)(2,1)S(1)}, u32[]{:S(2)}, u32[]{:S(2)}) collective-permute-start(bf16[80,1024]{1,0:T(8,128)(2,1)S(1)} %slice.133), channel_id=1, source_target_pairs={{0,1},{1,0},{2,3},{3,2},{4,5},{5,4},{6,7},{7,6},{8,9},{9,8},{10,11... | collective-permute-start | bytes 491528 | tf_op jit(solution)/shard_map/ppermute | solution.py:41
  219.6 8.0 %collective-permute-start.26 = (bf16[64,2304]{1,0:T(8,128)(2,1)S(1)}, bf16[64,2304]{1,0:T(8,128)(2,1)S(1)}, u32[]{:S(2)}, u32[]{:S(2)}) collective-permute-start(bf16[64,2304]{1,0:T(8,128)(2,1)S(1)} %get-tuple-element.83), channel_id=1, source_target_pairs={{0,2},{1,3},{2,4},{3,5},{4,6},{5,7},{6,0},{7,1},{8,10},{9,11},{10,... | collective-permute-start | bytes 884744 | tf_op jit(solution)/shard_map/ppermute | solution.py:41
  219.7 7.9 %collective-permute-start.28 = (bf16[64,2304]{1,0:T(8,128)(2,1)S(1)}, bf16[64,2304]{1,0:T(8,128)(2,1)S(1)}, u32[]{:S(2)}, u32[]{:S(2)}) collective-permute-start(bf16[64,2304]{1,0:T(8,128)(2,1)S(1)} %get-tuple-element.84), channel_id=1, source_target_pairs={{0,6},{1,7},{2,0},{3,1},{4,2},{5,3},{6,4},{7,5},{8,14},{9,15},{10,... | collective-permute-start | bytes 884744 | tf_op jit(solution)/shard_map/ppermute | solution.py:41
  222.9 20.8 %collective-permute-start.31 = (bf16[128,3584]{1,0:T(8,128)(2,1)S(1)}, bf16[128,3584]{1,0:T(8,128)(2,1)S(1)}, u32[]{:S(2)}, u32[]{:S(2)}) collective-permute-start(bf16[128,3584]{1,0:T(8,128)(2,1)S(1)} %slice.134), channel_id=1, source_target_pairs={{0,1},{1,0},{2,3},{3,2},{4,5},{5,4},{6,7},{7,6},{8,9},{9,8},{10,11... | collective-permute-start | bytes 2752520 | tf_op jit(solution)/shard_map/ppermute | solution.py:41
  227.8 19.4 %collective-permute-start.27 = (bf16[64,4608]{1,0:T(8,128)(2,1)S(1)}, bf16[64,4608]{1,0:T(8,128)(2,1)S(1)}, u32[]{:S(2)}, u32[]{:S(2)}) collective-permute-start(bf16[64,4608]{1,0:T(8,128)(2,1)S(1)} %pad_maximum_fusion.1), channel_id=1, source_target_pairs={{0,2},{1,3},{2,4},{3,5},{4,6},{5,7},{6,0},{7,1},{8,10},{9,11},{10,... | collective-permute-start | bytes 1769480 | tf_op jit(solution)/shard_map/ppermute | solution.py:41
  229.3 18.0 %collective-permute-start.29 = (bf16[64,4608]{1,0:T(8,128)(2,1)S(1)}, bf16[64,4608]{1,0:T(8,128)(2,1)S(1)}, u32[]{:S(2)}, u32[]{:S(2)}) collective-permute-start(bf16[64,4608]{1,0:T(8,128)(2,1)S(1)} %pad_maximum_fusion.2), channel_id=1, source_target_pairs={{0,6},{1,7},{2,0},{3,1},{4,2},{5,3},{6,4},{7,5},{8,14},{9,15},{10,... | collective-permute-start | bytes 1769480 | tf_op jit(solution)/shard_map/ppermute | solution.py:41
  247.5 8.3 %collective-permute-start.30 = (bf16[32,4608]{1,0:T(8,128)(2,1)S(1)}, bf16[32,4608]{1,0:T(8,128)(2,1)S(1)}, u32[]{:S(2)}, u32[]{:S(2)}) collective-permute-start(bf16[32,4608]{1,0:T(8,128)(2,1)S(1)} %slice.165), channel_id=1, source_target_pairs={{0,1},{1,0},{2,3},{3,2},{4,5},{5,4},{6,7},{7,6},{8,9},{9,8},{10,11... | collective-permute-start | bytes 884744 | tf_op jit(solution)/shard_map/ppermute | solution.py:41
  251.2 7.5 %collective-permute-start.33 = (bf16[32,3584]{1,0:T(8,128)(2,1)S(1)}, bf16[32,3584]{1,0:T(8,128)(2,1)S(1)}, u32[]{:S(2)}, u32[]{:S(2)}) collective-permute-start(bf16[32,3584]{1,0:T(8,128)(2,1)S(1)} %pad_maximum_fusion.3), channel_id=1, source_target_pairs={{0,2},{1,3},{2,4},{3,5},{4,6},{5,7},{6,0},{7,1},{8,10},{9,11},{10,... | collective-permute-start | bytes 688136 | tf_op jit(solution)/shard_map/ppermute | solution.py:41
  251.3 7.4 %collective-permute-start.35 = (bf16[32,3584]{1,0:T(8,128)(2,1)S(1)}, bf16[32,3584]{1,0:T(8,128)(2,1)S(1)}, u32[]{:S(2)}, u32[]{:S(2)}) collective-permute-start(bf16[32,3584]{1,0:T(8,128)(2,1)S(1)} %pad_maximum_fusion.4), channel_id=1, source_target_pairs={{0,6},{1,7},{2,0},{3,1},{4,2},{5,3},{6,4},{7,5},{8,14},{9,15},{10,... | collective-permute-start | bytes 688136 | tf_op jit(solution)/shard_map/ppermute | solution.py:41
  (16 other events, 156.9 us)

commit v3 on v2

--- a/solution.py
+++ b/solution.py
@@ -115,7 +115,7 @@
 def attend_chunks(chunks, q_ref, m_ref, o_ref, k_all, v_all, flag):
     keys = k_all.shape[0]
     queries = q_ref.shape[1]
-    step = keys if keys <= 2048 else max(d for d in (2048, 1536, 1024) if keys % d == 0)
+    step = keys if keys <= 2048 else max(d for d in (1536, 1024) if keys % d == 0)
     turns = queries // (2 * QUERY_BLOCK)
     at = 0
     for ref in chunks:
@@ -185,7 +185,7 @@
     q_ref[HEAD_DIM:, :] = split_rows(m_ref[0:1, :])
     q_out[...] = q_ref[...]
     start_out[...] = m_ref[...]
-    attend_chunks([kv_ref], q_ref, m_ref, o_ref, k_all, v_all, flag)
+    attend_chunks([kv_ref, swapped], q_ref, m_ref, o_ref, k_all, v_all, flag)
 
 
 def next_kernel(count, *refs):
@@ -204,19 +204,26 @@
     q_ref[...] = q_in[...]
     m_ref[...] = m_in[...]
     attend_chunks(chunks, q_ref, m_ref, o_ref, k_all, v_all, flag)
-    top = m_ref[0:1, :]
-    for t in tops:
-        top = jnp.maximum(top, t[0:1, :])
-    total = o_ref[...] * jnp.exp2(m_ref[0:1, :] - top)
-    for t, o in zip(tops, sums):
-        total = total + o[...] * jnp.exp2(t[0:1, :] - top)
-    half = total.shape[1] // 2
+    half = o_ref.shape[1] // 2
     for out_ref, lower in ((own_ref, 0), (swap_ref, half)):
-        for s in range(half // 128):
-            cols = slice(lower + s * 128, lower + (s + 1) * 128)
-            mass = total[HEAD_DIM : HEAD_DIM + 1, cols]
-            target = pl.ds(pl.multiple_of(place[s] * 128, 128), 128)
-            out_ref[:, target] = (total[:HEAD_DIM, cols] / mass).astype(BF)
+
+        def block(turn, carry, out_ref=out_ref, lower=lower):
+            for k in range(4):
+                slot = turn * 4 + k
+                cols = pl.ds(pl.multiple_of(lower + slot * 128, 128), 128)
+                own_top = m_ref[0:1, cols]
+                top = own_top
+                for t in tops:
+                    top = jnp.maximum(top, t[0:1, cols])
+                total = o_ref[:, cols] * jnp.exp2(own_top - top)
+                for t, o in zip(tops, sums):
+                    total = total + o[:, cols] * jnp.exp2(t[0:1, cols] - top)
+                target = pl.ds(pl.multiple_of(place[slot] * 128, 128), 128)
+                mass = total[HEAD_DIM : HEAD_DIM + 1]
+                out_ref[:, target] = (total[:HEAD_DIM] / mass).astype(BF)
+            return carry
+
+        lax.fori_loop(0, half // 512, block, 0)
 
 
 def add_heads(slots, pieces, col_ref, c, weight_ref, base_ref, out_ref):
@@ -238,15 +245,16 @@
 
 def mix_first_kernel(col_ref, place_ref, weight_ref, *refs):
     pieces, tiles, out_ref = refs[:4], refs[4:13], refs[13]
-    for slot in range(8):
-        row = col_ref[slot] * 128
-        if slot < 7:
-            spot = pl.ds(pl.multiple_of(row, 128), 128)
-            out_ref[spot, :] = tiles[slot][...].astype(F32)
-        else:
-            for k in range(2):
-                spot = pl.ds(pl.multiple_of(row + k * 64, 64), 64)
-                out_ref[spot, :] = tiles[7 + k][...].astype(F32)
+    starts = [col_ref[slot] * 128 for slot in range(8)] + [col_ref[7] * 128 + 64]
+    for tile, start in zip(tiles, starts):
+
+        def copy(i, carry, tile=tile, start=start):
+            rows = pl.ds(pl.multiple_of(i * 32, 32), 32)
+            spot = pl.ds(pl.multiple_of(start + i * 32, 32), 32)
+            out_ref[spot, :] = tile[rows, :].astype(F32)
+            return carry
+
+        lax.fori_loop(0, tile.shape[0] // 32, copy, 0)
     add_heads((0, 1, 2, 3), pieces, col_ref, place_ref[0], weight_ref, out_ref, out_ref)
 
 
@@ -382,9 +390,16 @@
     swap = pairs(lambda d: {"c": 1 - d["c"]})
     mirror_y = pairs(lambda d: {"zl": 1 - d["zl"]})
     swapped = send(other, swap)
-    kv = jnp.concatenate([kv_own, swapped[HEAD_DIM:]], axis=1)
-    chunks, _ = spread(kv, "y", mirror_y, 1)
-    groups = (chunks[1:4], chunks[4:7], chunks[7:])
+    forward, backward = shift("y", 1), shift("y", -1)
+    near = [send(kv_own, p) for p in (forward, backward, mirror_y)]
+    near += [send(swapped[HEAD_DIM:], p) for p in (forward, backward, mirror_y)]
+    near = lax.optimization_barrier(near)
+    plus = jnp.concatenate([near[0], near[3]], axis=1)
+    mirror = jnp.concatenate([near[2], near[5]], axis=1)
+    two, mirror_plus = send(plus, forward), send(plus, mirror_y)
+    mirror_minus = send(mirror, backward)
+    far = [send(mirror_plus[:, :band], forward), send(two[:, band:], mirror_y)]
+    groups = (near, [two, mirror_plus, mirror_minus], far)
     q_shape, m_shape, o_shape = sds((96, n), BF), sds((8, n), F32), sds((96, n), F32)
 
     def scratch(keys):
@@ -399,7 +414,7 @@
     q, start, top, part = call(
         first_kernel,
         (q_shape, m_shape, m_shape, o_shape),
-        [("v", q_own), ("v", swapped), ("v", kv)],
+        [("v", q_own), ("v", swapped), ("v", kv_own)],
         scratch(n),
         **work(n),
     )

time: 261 us -> 268 us (1.027)
  starting transfers between devices: 58 us -> 63.4 us
    ppermute x36 -> x39, starting transfers between devices: 58 us -> 63.4 us  [send(): return lax.ppermute(value, AXES, perm)]
    ppermute x36 -> x39, waiting for transfers between devices: 45.4 us -> 45.2 us  [send(): return lax.ppermute(value, AXES, perm)]
  transfers between devices with their start and end apart: 36 -> 39, of which waited for: 16 -> 14; matrix products, arithmetic and copies ran while one was open for 2% -> 2% of each run, Pallas kernels for 45% -> 45%
where the time goes in v3:
time: 268 us; the launch traced here: 267 us
  Pallas kernels  143 us (53%)
  starting transfers between devices  63.4 us (24%)
  waiting for transfers between devices  45.2 us (17%)
  local copies, waits for them, and re-layouts  6.68 us (2%)
  other arithmetic  3.96 us (1%)
  matrix products  3.68 us (1%)
    pallas_call x10, Pallas kernels, call(): pl.pallas_call(kernel, out_shape=outs, in_specs=specs, out_specs=jax.tree...  143 us
    ppermute x39, starting transfers between devices, send(): return lax.ppermute(value, AXES, perm)  63.4 us
    ppermute x39, waiting for transfers between devices, send(): return lax.ppermute(value, AXES, perm)  45.2 us
  transfers between devices with their start and end apart: 39, of which 14 were waited for; matrix products, arithmetic and copies ran while one was open for 2% of the time, Pallas kernels for 45%

profile of v3, /device:TPU:0, one launch (start us, length us, event | category | flops | bytes accessed | tf_op | source)
XLA Modules:
  0.0 266.8 jit_solution(6852916863122177537)
XLA Ops:
  3.2 4.0 %collective-permute-start.2 = (bf16[128,1280]{1,0:T(8,128)(2,1)}, bf16[128,1280]{1,0:T(8,128)(2,1)S(1)}, u32[]{:S(2)}, u32[]{:S(2)}) collective-permute-start(bf16[128,1280]{1,0:T(8,128)(2,1)} %bitcast.30), channel_id=1, source_target_pairs={{0,1},{1,0},{2,3},{3,2},{4,5},{5,4},{6,7},{7,6},{8,9},{9,8},{10,11... | collective-permute-start | bytes 983048 | tf_op jit(solution)/shard_map/ppermute | solution.py:41
  11.6 3.0 %collective-permute-done.2.refs_3_.refs_7_ = bf16[128,1280]{1,0:T(8,128)(2,1)S(1)} collective-permute-done((bf16[128,1280]{1,0:T(8,128)(2,1)}, bf16[128,1280]{1,0:T(8,128)(2,1)S(1)}, u32[]{:S(2)}, u32[]{:S(2)}) %collective-permute-start.2) | collective-permute-done | bytes 327712 | tf_op jit(solution)/shard_map/ppermute | solution.py:41
  14.6 3.2 %collective-permute-start.3 = (bf16[128,1280]{1,0:T(8,128)(2,1)S(1)}, bf16[128,1280]{1,0:T(8,128)(2,1)S(1)}, u32[]{:S(2)}, u32[]{:S(2)}) collective-permute-start(bf16[128,1280]{1,0:T(8,128)(2,1)S(1)} %collective-permute-done.refs_1_.refs_5_), channel_id=1, source_target_pairs={{0,1},{1,0},{2,3},{3,2},{4,5},{5,4},{6,7},{7,6},{8,9},{9,8},{10,11... | collective-permute-start | bytes 983048 | tf_op jit(solution)/shard_map/ppermute | solution.py:41
  18.1 3.0 %collective-permute-start.7 = (bf16[128,1280]{1,0:T(8,128)(2,1)S(1)}, bf16[128,1280]{1,0:T(8,128)(2,1)S(1)}, u32[]{:S(2)}, u32[]{:S(2)}) collective-permute-start(bf16[128,1280]{1,0:T(8,128)(2,1)S(1)} %collective-permute-done.2.refs_3_.refs_7_), channel_id=1, source_target_pairs={{0,6},{1,7},{2,0},{3,1},{4,2},{5,3},{6,4},{7,5},{8,14},{9,15},{10,... | collective-permute-start | bytes 983048 | tf_op jit(solution)/shard_map/ppermute | solution.py:41
  21.1 3.4 %collective-permute-done.3.refs_1_.refs_9_ = bf16[128,1280]{1,0:T(8,128)(2,1)S(1)} collective-permute-done((bf16[128,1280]{1,0:T(8,128)(2,1)S(1)}, bf16[128,1280]{1,0:T(8,128)(2,1)S(1)}, u32[]{:S(2)}, u32[]{:S(2)}) %collective-permute-start.3) | collective-permute-done | bytes 327712 | tf_op jit(solution)/shard_map/ppermute | solution.py:41
  24.8 2.6 collective-permute-done.5.refs_0_.refs_8_
  40.3 2.9 %collective-permute-start.13 = (bf16[160,1024]{1,0:T(8,128)(2,1)S(1)}, bf16[160,1024]{1,0:T(8,128)(2,1)S(1)}, u32[]{:S(2)}, u32[]{:S(2)}) collective-permute-start(bf16[160,1024]{1,0:T(8,128)(2,1)S(1)} %slice.131), channel_id=1, source_target_pairs={{0,96},{1,97},{2,98},{3,99},{4,100},{5,101},{6,102},{7,103},{8,104... | collective-permute-start | bytes 983048 | tf_op jit(solution)/shard_map/ppermute | solution.py:41
  43.2 2.4 collective-permute-done.10.refs_2_
  46.7 16.9 %shard_map.130 = (bf16[96,2048]{1,0:T(8,128)(2,1)S(1)}, f32[8,2048]{1,0:T(8,128)S(1)}, f32[8,2048]{1,0:T(8,128)S(1)}, f32[96,2048]{1,0:T(8,128)S(1)}) custom-call(bf16[80,1024]{1,0:T(8,128)(2,1)S(1)} %get-tuple-element.61.own_q, bf16[240,1024]{1,0:T(8,128)(2,1)S(1)} %collective-permute-done.11.swapped, bf16[160,1024]{1,0:T(8,128)(2,1)S(1)} %get-tuple-element.57.kv_ref), custom_call_target="tpu_custom_call" | custom-call | flops 4294967296 | bytes 786432 | tf_op jit(solution)/shard_map/pallas_call | solution.py:54
  66.3 1.9 collective-permute-start.19
  68.2 46.7 %shard_map.131 = (f32[8,2048]{1,0:T(8,128)S(1)}, f32[96,2048]{1,0:T(8,128)S(1)}) custom-call(bf16[160,1024]{1,0:T(8,128)(2,1)S(1)} %collective-permute-done.8.refs_0_, bf16[160,1024]{1,0:T(8,128)(2,1)S(1)} %collective-permute-done.9.refs_1_, bf16[160,1024]{1,0:T(8,128)(2,1)S(1)} %collective-permute-done.10.refs_2_, ...), custom_call_target="tpu_custom_call" | custom-call | flops 12884901888 | bytes 786432 | tf_op jit(solution)/shard_map/pallas_call | solution.py:54
  116.6 46.7 %shard_map.132 = (f32[8,2048]{1,0:T(8,128)S(1)}, f32[96,2048]{1,0:T(8,128)S(1)}) custom-call(bf16[160,2048]{1,0:T(8,128)(2,1)S(1)} %collective-permute-done.17.refs_0_, bf16[160,2048]{1,0:T(8,128)(2,1)S(1)} %collective-permute-done.15.refs_1_, bf16[160,2048]{1,0:T(8,128)(2,1)S(1)} %collective-permute-done.19.refs_2_, ...), custom_call_target="tpu_custom_call" | custom-call | flops 12884901888 | bytes 786432 | tf_op jit(solution)/shard_map/pallas_call | solution.py:54
  163.3 16.6 %shard_map.133 = (bf16[80,1024]{1,0:T(8,128)(2,1)S(1)}, bf16[80,1024]{1,0:T(8,128)(2,1)S(1)}) custom-call(s32[8]{0:T(128)S(1)} %get-tuple-element.86.place.col_ref, bf16[160,1024]{1,0:T(8,128)(2,1)S(1)} %collective-permute-done.16.refs_0_, bf16[160,1024]{1,0:T(8,128)(2,1)S(1)} %collective-permute-done.18.refs_1_, ...), custom_call_target="tpu_custom_call" | custom-call | flops 4294967296 | bytes 786432 | tf_op jit(solution)/shard_map/pallas_call | solution.py:54
  184.7 4.1 %collective-permute-start.23 = (bf16[160,1024]{1,0:T(8,128)(2,1)S(1)}, bf16[160,1024]{1,0:T(8,128)(2,1)S(1)}, u32[]{:S(2)}, u32[]{:S(2)}) collective-permute-start(bf16[160,1024]{1,0:T(8,128)(2,1)S(1)} %constant_dynamic-update-slice_fusion.2.refs_0_), channel_id=1, source_target_pairs={{0,1},{1,0},{2,3},{3,2},{4,5},{5,4},{6,7},{7,6},{8,9},{9,8},{10,11... | collective-permute-start | bytes 983048 | tf_op jit(solution)/shard_map/ppermute | solution.py:41
  188.8 3.6 %collective-permute-done.21.refs_1_ = bf16[160,1024]{1,0:T(8,128)(2,1)S(1)} collective-permute-done((bf16[160,1024]{1,0:T(8,128)(2,1)S(1)}, bf16[160,1024]{1,0:T(8,128)(2,1)S(1)}, u32[]{:S(2)}, u32[]{:S(2)}) %collective-permute-start.21) | collective-permute-done | bytes 327712 | tf_op jit(solution)/shard_map/ppermute | solution.py:41
  192.4 3.9 %collective-permute-done.23.refs_3_ = bf16[160,1024]{1,0:T(8,128)(2,1)S(1)} collective-permute-done((bf16[160,1024]{1,0:T(8,128)(2,1)S(1)}, bf16[160,1024]{1,0:T(8,128)(2,1)S(1)}, u32[]{:S(2)}, u32[]{:S(2)}) %collective-permute-start.23) | collective-permute-done | bytes 327712 | tf_op jit(solution)/shard_map/ppermute | solution.py:41
  196.3 3.2 %collective-permute-start.24 = (bf16[160,1024]{1,0:T(8,128)(2,1)S(1)}, bf16[160,1024]{1,0:T(8,128)(2,1)S(1)}, u32[]{:S(2)}, u32[]{:S(2)}) collective-permute-start(bf16[160,1024]{1,0:T(8,128)(2,1)S(1)} %collective-permute-done.21.refs_1_), channel_id=1, source_target_pairs={{0,1},{1,0},{2,3},{3,2},{4,5},{5,4},{6,7},{7,6},{8,9},{9,8},{10,11... | collective-permute-start | bytes 983048 | tf_op jit(solution)/shard_map/ppermute | solution.py:41
  199.5 3.2 %collective-permute-start.28 = (bf16[160,1024]{1,0:T(8,128)(2,1)S(1)}, bf16[160,1024]{1,0:T(8,128)(2,1)S(1)}, u32[]{:S(2)}, u32[]{:S(2)}) collective-permute-start(bf16[160,1024]{1,0:T(8,128)(2,1)S(1)} %collective-permute-done.23.refs_3_), channel_id=1, source_target_pairs={{0,6},{1,7},{2,0},{3,1},{4,2},{5,3},{6,4},{7,5},{8,14},{9,15},{10,... | collective-permute-start | bytes 983048 | tf_op jit(solution)/shard_map/ppermute | solution.py:41
  202.8 3.6 %collective-permute-done.24.refs_1_ = bf16[160,1024]{1,0:T(8,128)(2,1)S(1)} collective-permute-done((bf16[160,1024]{1,0:T(8,128)(2,1)S(1)}, bf16[160,1024]{1,0:T(8,128)(2,1)S(1)}, u32[]{:S(2)}, u32[]{:S(2)}) %collective-permute-start.24) | collective-permute-done | bytes 327712 | tf_op jit(solution)/shard_map/ppermute | solution.py:41
  206.5 2.6 collective-permute-done.26.refs_0_
  209.8 3.7 %shard_map.134.refs_3_ = f32[1024,1280]{1,0:T(8,128)S(1)} custom-call(s32[8]{0:T(128)S(1)} %get-tuple-element.86.place.col_ref, s32[3]{0:T(128)S(1)} %pad_add_fusion.place_ref, bf16[1280,1280]{1,0:T(8,128)(2,1)S(1)} %copy-done, bf16[160,1024]{1,0:T(8,128)(2,1)S(1)} %constant_dynamic-update-slice_fusion.2.refs_0_, ...), custom_call_target="tpu_custom_call" | custom-call | flops 1677721600 | tf_op jit(solution)/shard_map/pallas_call | solution.py:54
  213.6 2.7 %shard_map.135.refs_2_ = f32[1024,1280]{1,0:T(8,128)S(1)} custom-call(s32[8]{0:T(128)S(1)} %get-tuple-element.86.place.col_ref, s32[3]{0:T(128)S(1)} %pad_add_fusion.place_ref, bf16[1280,1280]{1,0:T(8,128)(2,1)S(1)} %copy-done, bf16[160,1024]{1,0:T(8,128)(2,1)S(1)} %collective-permute-done.26.refs_0_, ...), custom_call_target="tpu_custom_call", output_to_operand_aliasing={{}: (6, {})} | custom-call | flops 1258291200 | tf_op jit(solution)/shard_map/pallas_call | solution.py:54
  216.3 6.5 %shard_map.136 = (bf16[256,640]{1,0:T(8,128)(2,1)S(1)}, bf16[256,640]{1,0:T(8,128)(2,1)S(1)}) custom-call(s32[8]{0:T(128)S(1)} %get-tuple-element.86.place.col_ref, s32[3]{0:T(128)S(1)} %pad_add_fusion.place_ref, bf16[1280,1280]{1,0:T(8,128)(2,1)S(1)} %copy-done, bf16[80,1024]{1,0:T(8,128)(2,1)S(1)} %collective-permute-done.25.refs_0_, ...), custom_call_target="tpu_custom_call" | custom-call | flops 2097152000 | tf_op jit(solution)/shard_map/pallas_call | solution.py:54
  224.6 2.0 convolution_convert_fusion
  226.8 3.3 %collective-permute-start.31 = (bf16[64,2304]{1,0:T(8,128)(2,1)S(1)}, bf16[64,2304]{1,0:T(8,128)(2,1)S(1)}, u32[]{:S(2)}, u32[]{:S(2)}) collective-permute-start(bf16[64,2304]{1,0:T(8,128)(2,1)S(1)} %get-tuple-element.90), channel_id=1, source_target_pairs={{0,6},{1,7},{2,0},{3,1},{4,2},{5,3},{6,4},{7,5},{8,14},{9,15},{10,... | collective-permute-start | bytes 884744 | tf_op jit(solution)/shard_map/ppermute | solution.py:41
  230.1 3.1 %collective-permute-start.34 = (bf16[128,3584]{1,0:T(8,128)(2,1)S(1)}, bf16[128,3584]{1,0:T(8,128)(2,1)S(1)}, u32[]{:S(2)}, u32[]{:S(2)}) collective-permute-start(bf16[128,3584]{1,0:T(8,128)(2,1)S(1)} %slice.136), channel_id=1, source_target_pairs={{0,1},{1,0},{2,3},{3,2},{4,5},{5,4},{6,7},{7,6},{8,9},{9,8},{10,11... | collective-permute-start | bytes 2752520 | tf_op jit(solution)/shard_map/ppermute | solution.py:41
  236.5 2.0 collective-permute-start.32
  238.4 12.5 %collective-permute-done.34 = bf16[128,3584]{1,0:T(8,128)(2,1)S(1)} collective-permute-done((bf16[128,3584]{1,0:T(8,128)(2,1)S(1)}, bf16[128,3584]{1,0:T(8,128)(2,1)S(1)}, u32[]{:S(2)}, u32[]{:S(2)}) %collective-permute-start.34) | collective-permute-done | bytes 917536 | tf_op jit(solution)/shard_map/ppermute | solution.py:41
  251.2 3.2 %collective-permute-start.37 = (bf16[32,1792]{1,0:T(8,128)(2,1)S(1)}, bf16[32,1792]{1,0:T(8,128)(2,1)S(1)}, u32[]{:S(2)}, u32[]{:S(2)}) collective-permute-start(bf16[32,1792]{1,0:T(8,128)(2,1)S(1)} %get-tuple-element.96), channel_id=1, source_target_pairs={{0,6},{1,7},{2,0},{3,1},{4,2},{5,3},{6,4},{7,5},{8,14},{9,15},{10,... | collective-permute-start | bytes 344072 | tf_op jit(solution)/shard_map/ppermute | solution.py:41
  254.7 2.6 collective-permute-start.33
  258.4 3.5 %collective-permute-start.38 = (bf16[32,3584]{1,0:T(8,128)(2,1)S(1)}, bf16[32,3584]{1,0:T(8,128)(2,1)S(1)}, u32[]{:S(2)}, u32[]{:S(2)}) collective-permute-start(bf16[32,3584]{1,0:T(8,128)(2,1)S(1)} %pad_maximum_fusion.4), channel_id=1, source_target_pairs={{0,6},{1,7},{2,0},{3,1},{4,2},{5,3},{6,4},{7,5},{8,14},{9,15},{10,... | collective-permute-start | bytes 688136 | tf_op jit(solution)/shard_map/ppermute | solution.py:41
  263.1 2.7 %collective-permute-done.36 = bf16[32,3584]{1,0:T(8,128)(2,1)S(1)} collective-permute-done((bf16[32,3584]{1,0:T(8,128)(2,1)S(1)}, bf16[32,3584]{1,0:T(8,128)(2,1)S(1)}, u32[]{:S(2)}, u32[]{:S(2)}) %collective-permute-start.36) | collective-permute-done | bytes 229408 | tf_op jit(solution)/shard_map/ppermute | solution.py:41
  (124 shorter events, 41.0 us)
Async XLA Ops:
  0.0 11.6 %collective-permute-start = (bf16[128,1280]{1,0:T(8,128)(2,1)}, bf16[128,1280]{1,0:T(8,128)(2,1)S(1)}, u32[]{:S(2)}, u32[]{:S(2)}) collective-permute-start(bf16[128,1280]{1,0:T(8,128)(2,1)} %bitcast.28), channel_id=1, source_target_pairs={{0,2},{1,3},{2,4},{3,5},{4,6},{5,7},{6,0},{7,1},{8,10},{9,11},{10,... | collective-permute-start | bytes 983048 | tf_op jit(solution)/shard_map/ppermute | solution.py:41
  1.6 10.0 %collective-permute-start.1 = (bf16[128,1280]{1,0:T(8,128)(2,1)}, bf16[128,1280]{1,0:T(8,128)(2,1)S(1)}, u32[]{:S(2)}, u32[]{:S(2)}) collective-permute-start(bf16[128,1280]{1,0:T(8,128)(2,1)} %bitcast.29), channel_id=1, source_target_pairs={{0,6},{1,7},{2,0},{3,1},{4,2},{5,3},{6,4},{7,5},{8,14},{9,15},{10,... | collective-permute-start | bytes 983048 | tf_op jit(solution)/shard_map/ppermute | solution.py:41
  3.2 11.4 %collective-permute-start.2 = (bf16[128,1280]{1,0:T(8,128)(2,1)}, bf16[128,1280]{1,0:T(8,128)(2,1)S(1)}, u32[]{:S(2)}, u32[]{:S(2)}) collective-permute-start(bf16[128,1280]{1,0:T(8,128)(2,1)} %bitcast.30), channel_id=1, source_target_pairs={{0,1},{1,0},{2,3},{3,2},{4,5},{5,4},{6,7},{7,6},{8,9},{9,8},{10,11... | collective-permute-start | bytes 983048 | tf_op jit(solution)/shard_map/ppermute | solution.py:41
  14.6 9.8 %collective-permute-start.3 = (bf16[128,1280]{1,0:T(8,128)(2,1)S(1)}, bf16[128,1280]{1,0:T(8,128)(2,1)S(1)}, u32[]{:S(2)}, u32[]{:S(2)}) collective-permute-start(bf16[128,1280]{1,0:T(8,128)(2,1)S(1)} %collective-permute-done.refs_1_.refs_5_), channel_id=1, source_target_pairs={{0,1},{1,0},{2,3},{3,2},{4,5},{5,4},{6,7},{7,6},{8,9},{9,8},{10,11... | collective-permute-start | bytes 983048 | tf_op jit(solution)/shard_map/ppermute | solution.py:41
  17.8 9.6 %collective-permute-start.5 = (bf16[128,1280]{1,0:T(8,128)(2,1)S(1)}, bf16[128,1280]{1,0:T(8,128)(2,1)S(1)}, u32[]{:S(2)}, u32[]{:S(2)}) collective-permute-start(bf16[128,1280]{1,0:T(8,128)(2,1)S(1)} %collective-permute-done.refs_1_.refs_5_), channel_id=1, source_target_pairs={{0,2},{1,3},{2,4},{3,5},{4,6},{5,7},{6,0},{7,1},{8,10},{9,11},{10,... | collective-permute-start | bytes 983048 | tf_op jit(solution)/shard_map/ppermute | solution.py:41
  18.1 15.2 %collective-permute-start.7 = (bf16[128,1280]{1,0:T(8,128)(2,1)S(1)}, bf16[128,1280]{1,0:T(8,128)(2,1)S(1)}, u32[]{:S(2)}, u32[]{:S(2)}) collective-permute-start(bf16[128,1280]{1,0:T(8,128)(2,1)S(1)} %collective-permute-done.2.refs_3_.refs_7_), channel_id=1, source_target_pairs={{0,6},{1,7},{2,0},{3,1},{4,2},{5,3},{6,4},{7,5},{8,14},{9,15},{10,... | collective-permute-start | bytes 983048 | tf_op jit(solution)/shard_map/ppermute | solution.py:41
  24.5 10.2 %collective-permute-start.4 = (bf16[64,1280]{1,0:T(8,128)(2,1)S(1)}, bf16[64,1280]{1,0:T(8,128)(2,1)S(1)}, u32[]{:S(2)}, u32[]{:S(2)}) collective-permute-start(bf16[64,1280]{1,0:T(8,128)(2,1)S(1)} %slice.129), channel_id=1, source_target_pairs={{0,2},{1,3},{2,4},{3,5},{4,6},{5,7},{6,0},{7,1},{8,10},{9,11},{10,... | collective-permute-start | bytes 491528 | tf_op jit(solution)/shard_map/ppermute | solution.py:41
  35.5 10.1 %collective-permute-start.10 = (bf16[160,1024]{1,0:T(8,128)(2,1)S(1)}, bf16[160,1024]{1,0:T(8,128)(2,1)S(1)}, u32[]{:S(2)}, u32[]{:S(2)}) collective-permute-start(bf16[160,1024]{1,0:T(8,128)(2,1)S(1)} %get-tuple-element.57.kv_ref), channel_id=1, source_target_pairs={{0,16},{1,17},{2,18},{3,19},{4,20},{5,21},{6,22},{7,23},{8,24},{9,... | collective-permute-start | bytes 983048 | tf_op jit(solution)/shard_map/ppermute | solution.py:41
  36.6 26.9 %collective-permute-start.8 = (bf16[160,1024]{1,0:T(8,128)(2,1)S(1)}, bf16[160,1024]{1,0:T(8,128)(2,1)S(1)}, u32[]{:S(2)}, u32[]{:S(2)}) collective-permute-start(bf16[160,1024]{1,0:T(8,128)(2,1)S(1)} %get-tuple-element.57.kv_ref), channel_id=1, source_target_pairs={{0,32},{1,33},{2,34},{3,35},{4,36},{5,37},{6,38},{7,39},{8,40},{9,... | collective-permute-start | bytes 983048 | tf_op jit(solution)/shard_map/ppermute | solution.py:41
  38.2 25.3 %collective-permute-start.9 = (bf16[160,1024]{1,0:T(8,128)(2,1)S(1)}, bf16[160,1024]{1,0:T(8,128)(2,1)S(1)}, u32[]{:S(2)}, u32[]{:S(2)}) collective-permute-start(bf16[160,1024]{1,0:T(8,128)(2,1)S(1)} %get-tuple-element.57.kv_ref), channel_id=1, source_target_pairs={{0,96},{1,97},{2,98},{3,99},{4,100},{5,101},{6,102},{7,103},{8,104... | collective-permute-start | bytes 983048 | tf_op jit(solution)/shard_map/ppermute | solution.py:41
  39.9 23.7 %collective-permute-start.12 = (bf16[160,1024]{1,0:T(8,128)(2,1)S(1)}, bf16[160,1024]{1,0:T(8,128)(2,1)S(1)}, u32[]{:S(2)}, u32[]{:S(2)}) collective-permute-start(bf16[160,1024]{1,0:T(8,128)(2,1)S(1)} %slice.131), channel_id=1, source_target_pairs={{0,32},{1,33},{2,34},{3,35},{4,36},{5,37},{6,38},{7,39},{8,40},{9,... | collective-permute-start | bytes 983048 | tf_op jit(solution)/shard_map/ppermute | solution.py:41
  40.3 23.2 %collective-permute-start.13 = (bf16[160,1024]{1,0:T(8,128)(2,1)S(1)}, bf16[160,1024]{1,0:T(8,128)(2,1)S(1)}, u32[]{:S(2)}, u32[]{:S(2)}) collective-permute-start(bf16[160,1024]{1,0:T(8,128)(2,1)S(1)} %slice.131), channel_id=1, source_target_pairs={{0,96},{1,97},{2,98},{3,99},{4,100},{5,101},{6,102},{7,103},{8,104... | collective-permute-start | bytes 983048 | tf_op jit(solution)/shard_map/ppermute | solution.py:41
  45.6 18.0 %collective-permute-start.14 = (bf16[160,1024]{1,0:T(8,128)(2,1)S(1)}, bf16[160,1024]{1,0:T(8,128)(2,1)S(1)}, u32[]{:S(2)}, u32[]{:S(2)}) collective-permute-start(bf16[160,1024]{1,0:T(8,128)(2,1)S(1)} %slice.131), channel_id=1, source_target_pairs={{0,16},{1,17},{2,18},{3,19},{4,20},{5,21},{6,22},{7,23},{8,24},{9,... | collective-permute-start | bytes 983048 | tf_op jit(solution)/shard_map/ppermute | solution.py:41
  63.7 51.2 %collective-permute-start.15 = (bf16[160,2048]{1,0:T(8,128)(2,1)S(1)}, bf16[160,2048]{1,0:T(8,128)(2,1)S(1)}, u32[]{:S(2)}, u32[]{:S(2)}) collective-permute-start(bf16[160,2048]{1,0:T(8,128)(2,1)S(1)} %constant_dynamic-update-slice_fusion), channel_id=1, source_target_pairs={{0,16},{1,17},{2,18},{3,19},{4,20},{5,21},{6,22},{7,23},{8,24},{9,... | collective-permute-start | bytes 1966088 | tf_op jit(solution)/shard_map/ppermute | solution.py:41
  64.7 50.7 %collective-permute-start.17 = (bf16[160,2048]{1,0:T(8,128)(2,1)S(1)}, bf16[160,2048]{1,0:T(8,128)(2,1)S(1)}, u32[]{:S(2)}, u32[]{:S(2)}) collective-permute-start(bf16[160,2048]{1,0:T(8,128)(2,1)S(1)} %constant_dynamic-update-slice_fusion), channel_id=1, source_target_pairs={{0,32},{1,33},{2,34},{3,35},{4,36},{5,37},{6,38},{7,39},{8,40},{9,... | collective-permute-start | bytes 1966088 | tf_op jit(solution)/shard_map/ppermute | solution.py:41
  66.3 50.2 %collective-permute-start.19 = (bf16[160,2048]{1,0:T(8,128)(2,1)S(1)}, bf16[160,2048]{1,0:T(8,128)(2,1)S(1)}, u32[]{:S(2)}, u32[]{:S(2)}) collective-permute-start(bf16[160,2048]{1,0:T(8,128)(2,1)S(1)} %pad_maximum_fusion), channel_id=1, source_target_pairs={{0,96},{1,97},{2,98},{3,99},{4,100},{5,101},{6,102},{7,103},{8,104... | collective-permute-start | bytes 1966088 | tf_op jit(solution)/shard_map/ppermute | solution.py:41
  114.9 48.3 %collective-permute-start.16 = (bf16[160,1024]{1,0:T(8,128)(2,1)S(1)}, bf16[160,1024]{1,0:T(8,128)(2,1)S(1)}, u32[]{:S(2)}, u32[]{:S(2)}) collective-permute-start(bf16[160,1024]{1,0:T(8,128)(2,1)S(1)} %slice.132), channel_id=1, source_target_pairs={{0,32},{1,33},{2,34},{3,35},{4,36},{5,37},{6,38},{7,39},{8,40},{9,... | collective-permute-start | bytes 983048 | tf_op jit(solution)/shard_map/ppermute | solution.py:41
  115.4 47.8 %collective-permute-start.18 = (bf16[160,1024]{1,0:T(8,128)(2,1)S(1)}, bf16[160,1024]{1,0:T(8,128)(2,1)S(1)}, u32[]{:S(2)}, u32[]{:S(2)}) collective-permute-start(bf16[160,1024]{1,0:T(8,128)(2,1)S(1)} %slice.133), channel_id=1, source_target_pairs={{0,16},{1,17},{2,18},{3,19},{4,20},{5,21},{6,22},{7,23},{8,24},{9,... | collective-permute-start | bytes 983048 | tf_op jit(solution)/shard_map/ppermute | solution.py:41
  181.4 11.0 %collective-permute-start.21 = (bf16[160,1024]{1,0:T(8,128)(2,1)S(1)}, bf16[160,1024]{1,0:T(8,128)(2,1)S(1)}, u32[]{:S(2)}, u32[]{:S(2)}) collective-permute-start(bf16[160,1024]{1,0:T(8,128)(2,1)S(1)} %constant_dynamic-update-slice_fusion.2.refs_0_), channel_id=1, source_target_pairs={{0,2},{1,3},{2,4},{3,5},{4,6},{5,7},{6,0},{7,1},{8,10},{9,11},{10,... | collective-permute-start | bytes 983048 | tf_op jit(solution)/shard_map/ppermute | solution.py:41
  182.9 9.5 %collective-permute-start.22 = (bf16[160,1024]{1,0:T(8,128)(2,1)S(1)}, bf16[160,1024]{1,0:T(8,128)(2,1)S(1)}, u32[]{:S(2)}, u32[]{:S(2)}) collective-permute-start(bf16[160,1024]{1,0:T(8,128)(2,1)S(1)} %constant_dynamic-update-slice_fusion.2.refs_0_), channel_id=1, source_target_pairs={{0,6},{1,7},{2,0},{3,1},{4,2},{5,3},{6,4},{7,5},{8,14},{9,15},{10,... | collective-permute-start | bytes 983048 | tf_op jit(solution)/shard_map/ppermute | solution.py:41
  184.7 11.6 %collective-permute-start.23 = (bf16[160,1024]{1,0:T(8,128)(2,1)S(1)}, bf16[160,1024]{1,0:T(8,128)(2,1)S(1)}, u32[]{:S(2)}, u32[]{:S(2)}) collective-permute-start(bf16[160,1024]{1,0:T(8,128)(2,1)S(1)} %constant_dynamic-update-slice_fusion.2.refs_0_), channel_id=1, source_target_pairs={{0,1},{1,0},{2,3},{3,2},{4,5},{5,4},{6,7},{7,6},{8,9},{9,8},{10,11... | collective-permute-start | bytes 983048 | tf_op jit(solution)/shard_map/ppermute | solution.py:41
  196.3 10.1 %collective-permute-start.24 = (bf16[160,1024]{1,0:T(8,128)(2,1)S(1)}, bf16[160,1024]{1,0:T(8,128)(2,1)S(1)}, u32[]{:S(2)}, u32[]{:S(2)}) collective-permute-start(bf16[160,1024]{1,0:T(8,128)(2,1)S(1)} %collective-permute-done.21.refs_1_), channel_id=1, source_target_pairs={{0,1},{1,0},{2,3},{3,2},{4,5},{5,4},{6,7},{7,6},{8,9},{9,8},{10,11... | collective-permute-start | bytes 983048 | tf_op jit(solution)/shard_map/ppermute | solution.py:41
  199.5 9.6 %collective-permute-start.26 = (bf16[160,1024]{1,0:T(8,128)(2,1)S(1)}, bf16[160,1024]{1,0:T(8,128)(2,1)S(1)}, u32[]{:S(2)}, u32[]{:S(2)}) collective-permute-start(bf16[160,1024]{1,0:T(8,128)(2,1)S(1)} %collective-permute-done.21.refs_1_), channel_id=1, source_target_pairs={{0,2},{1,3},{2,4},{3,5},{4,6},{5,7},{6,0},{7,1},{8,10},{9,11},{10,... | collective-permute-start | bytes 983048 | tf_op jit(solution)/shard_map/ppermute | solution.py:41
  199.5 14.0 %collective-permute-start.28 = (bf16[160,1024]{1,0:T(8,128)(2,1)S(1)}, bf16[160,1024]{1,0:T(8,128)(2,1)S(1)}, u32[]{:S(2)}, u32[]{:S(2)}) collective-permute-start(bf16[160,1024]{1,0:T(8,128)(2,1)S(1)} %collective-permute-done.23.refs_3_), channel_id=1, source_target_pairs={{0,6},{1,7},{2,0},{3,1},{4,2},{5,3},{6,4},{7,5},{8,14},{9,15},{10,... | collective-permute-start | bytes 983048 | tf_op jit(solution)/shard_map/ppermute | solution.py:41
  206.4 9.9 %collective-permute-start.25 = (bf16[80,1024]{1,0:T(8,128)(2,1)S(1)}, bf16[80,1024]{1,0:T(8,128)(2,1)S(1)}, u32[]{:S(2)}, u32[]{:S(2)}) collective-permute-start(bf16[80,1024]{1,0:T(8,128)(2,1)S(1)} %slice.134), channel_id=1, source_target_pairs={{0,2},{1,3},{2,4},{3,5},{4,6},{5,7},{6,0},{7,1},{8,10},{9,11},{10,... | collective-permute-start | bytes 491528 | tf_op jit(solution)/shard_map/ppermute | solution.py:41
  226.7 8.0 %collective-permute-start.29 = (bf16[64,2304]{1,0:T(8,128)(2,1)S(1)}, bf16[64,2304]{1,0:T(8,128)(2,1)S(1)}, u32[]{:S(2)}, u32[]{:S(2)}) collective-permute-start(bf16[64,2304]{1,0:T(8,128)(2,1)S(1)} %get-tuple-element.89), channel_id=1, source_target_pairs={{0,2},{1,3},{2,4},{3,5},{4,6},{5,7},{6,0},{7,1},{8,10},{9,11},{10,... | collective-permute-start | bytes 884744 | tf_op jit(solution)/shard_map/ppermute | solution.py:41
  226.8 7.9 %collective-permute-start.31 = (bf16[64,2304]{1,0:T(8,128)(2,1)S(1)}, bf16[64,2304]{1,0:T(8,128)(2,1)S(1)}, u32[]{:S(2)}, u32[]{:S(2)}) collective-permute-start(bf16[64,2304]{1,0:T(8,128)(2,1)S(1)} %get-tuple-element.90), channel_id=1, source_target_pairs={{0,6},{1,7},{2,0},{3,1},{4,2},{5,3},{6,4},{7,5},{8,14},{9,15},{10,... | collective-permute-start | bytes 884744 | tf_op jit(solution)/shard_map/ppermute | solution.py:41
  230.1 20.8 %collective-permute-start.34 = (bf16[128,3584]{1,0:T(8,128)(2,1)S(1)}, bf16[128,3584]{1,0:T(8,128)(2,1)S(1)}, u32[]{:S(2)}, u32[]{:S(2)}) collective-permute-start(bf16[128,3584]{1,0:T(8,128)(2,1)S(1)} %slice.136), channel_id=1, source_target_pairs={{0,1},{1,0},{2,3},{3,2},{4,5},{5,4},{6,7},{7,6},{8,9},{9,8},{10,11... | collective-permute-start | bytes 2752520 | tf_op jit(solution)/shard_map/ppermute | solution.py:41
  235.0 19.5 %collective-permute-start.30 = (bf16[64,4608]{1,0:T(8,128)(2,1)S(1)}, bf16[64,4608]{1,0:T(8,128)(2,1)S(1)}, u32[]{:S(2)}, u32[]{:S(2)}) collective-permute-start(bf16[64,4608]{1,0:T(8,128)(2,1)S(1)} %pad_maximum_fusion.1), channel_id=1, source_target_pairs={{0,2},{1,3},{2,4},{3,5},{4,6},{5,7},{6,0},{7,1},{8,10},{9,11},{10,... | collective-permute-start | bytes 1769480 | tf_op jit(solution)/shard_map/ppermute | solution.py:41
  236.5 18.0 %collective-permute-start.32 = (bf16[64,4608]{1,0:T(8,128)(2,1)S(1)}, bf16[64,4608]{1,0:T(8,128)(2,1)S(1)}, u32[]{:S(2)}, u32[]{:S(2)}) collective-permute-start(bf16[64,4608]{1,0:T(8,128)(2,1)S(1)} %pad_maximum_fusion.2), channel_id=1, source_target_pairs={{0,6},{1,7},{2,0},{3,1},{4,2},{5,3},{6,4},{7,5},{8,14},{9,15},{10,... | collective-permute-start | bytes 1769480 | tf_op jit(solution)/shard_map/ppermute | solution.py:41
  254.7 8.3 %collective-permute-start.33 = (bf16[32,4608]{1,0:T(8,128)(2,1)S(1)}, bf16[32,4608]{1,0:T(8,128)(2,1)S(1)}, u32[]{:S(2)}, u32[]{:S(2)}) collective-permute-start(bf16[32,4608]{1,0:T(8,128)(2,1)S(1)} %slice.167), channel_id=1, source_target_pairs={{0,1},{1,0},{2,3},{3,2},{4,5},{5,4},{6,7},{7,6},{8,9},{9,8},{10,11... | collective-permute-start | bytes 884744 | tf_op jit(solution)/shard_map/ppermute | solution.py:41
  258.3 7.5 %collective-permute-start.36 = (bf16[32,3584]{1,0:T(8,128)(2,1)S(1)}, bf16[32,3584]{1,0:T(8,128)(2,1)S(1)}, u32[]{:S(2)}, u32[]{:S(2)}) collective-permute-start(bf16[32,3584]{1,0:T(8,128)(2,1)S(1)} %pad_maximum_fusion.3), channel_id=1, source_target_pairs={{0,2},{1,3},{2,4},{3,5},{4,6},{5,7},{6,0},{7,1},{8,10},{9,11},{10,... | collective-permute-start | bytes 688136 | tf_op jit(solution)/shard_map/ppermute | solution.py:41
  (19 other events, 181.0 us)

commit v4 on v3

--- a/solution.py
+++ b/solution.py
@@ -115,15 +115,22 @@
 def attend_chunks(chunks, q_ref, m_ref, o_ref, k_all, v_all, flag):
     keys = k_all.shape[0]
     queries = q_ref.shape[1]
-    step = keys if keys <= 2048 else max(d for d in (1536, 1024) if keys % d == 0)
-    turns = queries // (2 * QUERY_BLOCK)
+    step, unroll = (keys, 2) if keys <= 2048 else (keys // 2, 1)
+    turns = queries // (unroll * QUERY_BLOCK)
     at = 0
+    ones = jnp.ones((16, 512), BF)
     for ref in chunks:
-        n = ref.shape[1]
-        ones = jnp.ones((16, n), BF)
-        k_all[at : at + n, :] = jnp.concatenate([ref[-2 * HEAD_DIM : -HEAD_DIM, :], ones], axis=0).T
-        v_all[:, at : at + n] = jnp.concatenate([ref[-HEAD_DIM:, :], ones], axis=0)
-        at += n
+
+        def place(i, carry, ref=ref, at=at):
+            cols = pl.ds(pl.multiple_of(i * 512, 512), 512)
+            spot = pl.ds(pl.multiple_of(at + i * 512, 512), 512)
+            keys_part = ref[-2 * HEAD_DIM : -HEAD_DIM, cols]
+            k_all[spot, :] = jnp.concatenate([keys_part, ones], axis=0).T
+            v_all[:, spot] = jnp.concatenate([ref[-HEAD_DIM:, cols], ones], axis=0)
+            return carry
+
+        lax.fori_loop(0, ref.shape[1] // 512, place, 0)
+        at += ref.shape[1]
     flag[0] = 1
 
     def attempt(tries, carry):
@@ -133,8 +140,8 @@
 
             def block(t, carry):
                 rows = pl.ds(pl.multiple_of((t // turns) * step, step), step)
-                for i in range(2):
-                    col = (t % turns) * (2 * QUERY_BLOCK) + i * QUERY_BLOCK
+                for i in range(unroll):
+                    col = (t % turns) * (unroll * QUERY_BLOCK) + i * QUERY_BLOCK
                     cols = pl.ds(pl.multiple_of(col, QUERY_BLOCK), QUERY_BLOCK)
                     s = jnp.dot(k_all[rows, :], q_ref[:, cols], preferred_element_type=F32)
                     p = jnp.exp2(s).astype(BF)
@@ -173,7 +180,7 @@
     n = own_q.shape[1]
     q_ref[:HEAD_DIM, :n] = own_q[...]
     q_ref[:HEAD_DIM, n:] = swapped[:HEAD_DIM, :]
-    some = kv_ref[:HEAD_DIM, :512].T
+    some = kv_ref[:HEAD_DIM, :256].T
 
     def start(i, carry):
         cols = pl.ds(pl.multiple_of(i * QUERY_BLOCK, QUERY_BLOCK), QUERY_BLOCK)
@@ -226,7 +233,7 @@
         lax.fori_loop(0, half // 512, block, 0)
 
 
-def add_heads(slots, pieces, col_ref, c, weight_ref, base_ref, out_ref):
+def add_heads(slots, pieces, col_ref, c, weight_ref, base_ref, out_ref, rows_at_once=256):
     rows = []
     for slot in slots:
         for head in (c, 1 - c):
@@ -235,12 +242,12 @@
     weight = jnp.concatenate(rows, axis=0)
 
     def block(i, carry):
-        spot = pl.ds(pl.multiple_of(i * 512, 512), 512)
+        spot = pl.ds(pl.multiple_of(i * rows_at_once, rows_at_once), rows_at_once)
         lhs = jnp.concatenate([p[:, spot] for p in pieces], axis=0).T
         out_ref[spot, :] = base_ref[spot, :] + jnp.dot(lhs, weight, preferred_element_type=F32)
         return carry
 
-    lax.fori_loop(0, out_ref.shape[0] // 512, block, 0)
+    lax.fori_loop(0, out_ref.shape[0] // rows_at_once, block, 0)
 
 
 def mix_first_kernel(col_ref, place_ref, weight_ref, *refs):
@@ -268,7 +275,7 @@
     base_ref, gain_ref, up_weight, bias_ref, hidden_a, hidden_b, mixed_all, merged = rest
     c, x, zh = place_ref[0], place_ref[1], place_ref[2]
     width = out_weight.shape[1]
-    add_heads((7,), pieces, col_ref, c, out_weight, base_ref, mixed_all)
+    add_heads((7,), pieces, col_ref, c, out_weight, base_ref, mixed_all, 512)
     r = lax.broadcasted_iota(jnp.int32, (128, 128), 0)
     t = lax.broadcasted_iota(jnp.int32, (128, 128), 1)
     a, b, u, w = r >> 6, (r >> 5) & 1, (r >> 3) & 3, r & 7
@@ -426,6 +433,7 @@
             (m_shape, o_shape),
             [("v", t) for t in chunks] + [("v", q), ("v", start)],
             scratch(keys),
+            grant=12,
             **work(keys),
         )
         tops.append(top)
@@ -476,22 +484,30 @@
     return scatter_output(hidden_a, hidden_b, down_weight, down_bias, mirror_x)
 
 
-def ring(block, rows):
+def ring(block, rows, early):
     forward, backward = shift("x", 1), shift("x", -1)
     half = block.shape[1] // 2
     part = lambda k: block[k * rows : (k + 1) * rows]
     ahead, behind, far = part(1), part(3), part(2)
+    add = lambda p, q: (p.astype(F32) + q.astype(F32)).astype(BF)
     from_behind = send(far[:, :half], forward)
     from_ahead = send(far[:, half:], backward)
-    add = lambda p, q: (p.astype(F32) + q.astype(F32)).astype(BF)
-    onward = jnp.concatenate([add(ahead[:, :half], from_behind), ahead[:, half:]], axis=1)
-    back = jnp.concatenate([behind[:, :half], add(behind[:, half:], from_ahead)], axis=1)
-    got_behind, got_ahead = send(onward, forward), send(back, backward)
+    if early:
+        high_behind = send(ahead[:, half:], forward)
+        low_ahead = send(behind[:, :half], backward)
+        low_behind = send(add(ahead[:, :half], from_behind), forward)
+        high_ahead = send(add(behind[:, half:], from_ahead), backward)
+        got_behind = jnp.concatenate([low_behind, high_behind], axis=1)
+        got_ahead = jnp.concatenate([low_ahead, high_ahead], axis=1)
+    else:
+        onward = jnp.concatenate([add(ahead[:, :half], from_behind), ahead[:, half:]], axis=1)
+        back = jnp.concatenate([behind[:, :half], add(behind[:, half:], from_ahead)], axis=1)
+        got_behind, got_ahead = send(onward, forward), send(back, backward)
     return part(0).astype(F32) + got_behind.astype(F32) + got_ahead.astype(F32)
 
 
 def scatter_output(hidden_a, hidden_b, down_weight, down_bias, mirror):
-    split = 4608
+    split = 4864
     part_b = jnp.dot(
         hidden_b, down_weight[:, split:], preferred_element_type=F32
     ).astype(BF)
@@ -500,10 +516,10 @@
     part_a = jnp.dot(
         hidden_a, down_weight[:, :split], preferred_element_type=F32
     ).astype(BF)
-    total_a = ring(part_a, 64)
+    total_a = ring(part_a, 64, True)
     got_a = send(total_a[32:].astype(BF), mirror)
     block_b = (part_b[:128].astype(F32) + got_b.astype(F32)).astype(BF)
-    total_b = ring(block_b, 32)
+    total_b = ring(block_b, 32, True)
     total_a = total_a[:32] + got_a.astype(F32)
     return (jnp.concatenate([total_a, total_b], axis=1) + down_bias[None, :]).astype(BF)
 

time: 268 us -> 265 us (0.989)
  local copies, waits for them, and re-layouts: 6.68 us -> 3.7 us
    unnamed x26, local copies, waits for them, and re-layouts: 4.06 us -> 1.07 us
    ppermute x39 -> x43, waiting for transfers between devices: 45.2 us -> 44.3 us  [send(): return lax.ppermute(value, AXES, perm)]
    ppermute x39 -> x43, starting transfers between devices: 63.4 us -> 63.9 us  [send(): return lax.ppermute(value, AXES, perm)]
  transfers between devices with their start and end apart: 39 -> 43, of which waited for: 14 -> 14; matrix products, arithmetic and copies ran while one was open for 2% -> 2% of each run, Pallas kernels for 45% -> 46%
where the time goes in v4:
time: 265 us
  Pallas kernels  145 us (55%)
  starting transfers between devices  63.9 us (24%)
  waiting for transfers between devices  44.3 us (17%)
  other arithmetic  3.85 us (1%)
  local copies, waits for them, and re-layouts  3.7 us (1%)
  matrix products  3.6 us (1%)
    pallas_call x10, Pallas kernels, call(): pl.pallas_call(kernel, out_shape=outs, in_specs=specs, out_specs=jax.tree...  145 us
    ppermute x43, starting transfers between devices, send(): return lax.ppermute(value, AXES, perm)  63.9 us
    ppermute x43, waiting for transfers between devices, send(): return lax.ppermute(value, AXES, perm)  44.3 us
  transfers between devices with their start and end apart: 43, of which 14 were waited for; matrix products, arithmetic and copies ran while one was open for 2% of the time, Pallas kernels for 46%

profile of v4, /device:TPU:0, one launch (start us, length us, event | category | flops | bytes accessed | tf_op | source)
XLA Modules:
  0.0 264.8 jit_solution(10624658090751277188)
XLA Ops:
  3.2 4.1 %collective-permute-start.2 = (bf16[128,1280]{1,0:T(8,128)(2,1)}, bf16[128,1280]{1,0:T(8,128)(2,1)S(1)}, u32[]{:S(2)}, u32[]{:S(2)}) collective-permute-start(bf16[128,1280]{1,0:T(8,128)(2,1)} %bitcast.30), channel_id=1, source_target_pairs={{0,1},{1,0},{2,3},{3,2},{4,5},{5,4},{6,7},{7,6},{8,9},{9,8},{10,11... | collective-permute-start | bytes 983048 | tf_op jit(solution)/shard_map/ppermute | solution.py:41
  11.7 3.0 %collective-permute-done.2.refs_3_.refs_7_ = bf16[128,1280]{1,0:T(8,128)(2,1)S(1)} collective-permute-done((bf16[128,1280]{1,0:T(8,128)(2,1)}, bf16[128,1280]{1,0:T(8,128)(2,1)S(1)}, u32[]{:S(2)}, u32[]{:S(2)}) %collective-permute-start.2) | collective-permute-done | bytes 327712 | tf_op jit(solution)/shard_map/ppermute | solution.py:41
  14.7 3.2 %collective-permute-start.3 = (bf16[128,1280]{1,0:T(8,128)(2,1)S(1)}, bf16[128,1280]{1,0:T(8,128)(2,1)S(1)}, u32[]{:S(2)}, u32[]{:S(2)}) collective-permute-start(bf16[128,1280]{1,0:T(8,128)(2,1)S(1)} %collective-permute-done.refs_1_.refs_5_), channel_id=1, source_target_pairs={{0,1},{1,0},{2,3},{3,2},{4,5},{5,4},{6,7},{7,6},{8,9},{9,8},{10,11... | collective-permute-start | bytes 983048 | tf_op jit(solution)/shard_map/ppermute | solution.py:41
  18.2 3.0 %collective-permute-start.7 = (bf16[128,1280]{1,0:T(8,128)(2,1)S(1)}, bf16[128,1280]{1,0:T(8,128)(2,1)S(1)}, u32[]{:S(2)}, u32[]{:S(2)}) collective-permute-start(bf16[128,1280]{1,0:T(8,128)(2,1)S(1)} %collective-permute-done.2.refs_3_.refs_7_), channel_id=1, source_target_pairs={{0,6},{1,7},{2,0},{3,1},{4,2},{5,3},{6,4},{7,5},{8,14},{9,15},{10,... | collective-permute-start | bytes 983048 | tf_op jit(solution)/shard_map/ppermute | solution.py:41
  21.1 3.4 %collective-permute-done.3.refs_1_.refs_9_ = bf16[128,1280]{1,0:T(8,128)(2,1)S(1)} collective-permute-done((bf16[128,1280]{1,0:T(8,128)(2,1)S(1)}, bf16[128,1280]{1,0:T(8,128)(2,1)S(1)}, u32[]{:S(2)}, u32[]{:S(2)}) %collective-permute-start.3) | collective-permute-done | bytes 327712 | tf_op jit(solution)/shard_map/ppermute | solution.py:41
  24.9 2.6 collective-permute-done.5.refs_0_.refs_8_
  31.7 2.7 %collective-permute-done.6.refs_1_.refs_12_ = bf16[64,1280]{1,0:T(8,128)(2,1)S(1)} collective-permute-done((bf16[64,1280]{1,0:T(8,128)(2,1)S(1)}, bf16[64,1280]{1,0:T(8,128)(2,1)S(1)}, u32[]{:S(2)}, u32[]{:S(2)}) %collective-permute-start.6) | collective-permute-done | bytes 163872 | tf_op jit(solution)/shard_map/ppermute | solution.py:41
  40.4 2.9 %collective-permute-start.13 = (bf16[160,1024]{1,0:T(8,128)(2,1)S(1)}, bf16[160,1024]{1,0:T(8,128)(2,1)S(1)}, u32[]{:S(2)}, u32[]{:S(2)}) collective-permute-start(bf16[160,1024]{1,0:T(8,128)(2,1)S(1)} %slice.131), channel_id=1, source_target_pairs={{0,96},{1,97},{2,98},{3,99},{4,100},{5,101},{6,102},{7,103},{8,104... | collective-permute-start | bytes 983048 | tf_op jit(solution)/shard_map/ppermute | solution.py:41
  43.2 2.1 collective-permute-done.10.refs_2_
  46.7 16.8 %shard_map.130 = (bf16[96,2048]{1,0:T(8,128)(2,1)S(1)}, f32[8,2048]{1,0:T(8,128)S(1)}, f32[8,2048]{1,0:T(8,128)S(1)}, f32[96,2048]{1,0:T(8,128)S(1)}) custom-call(bf16[80,1024]{1,0:T(8,128)(2,1)S(1)} %get-tuple-element.61.own_q, bf16[240,1024]{1,0:T(8,128)(2,1)S(1)} %collective-permute-done.11.swapped, bf16[160,1024]{1,0:T(8,128)(2,1)S(1)} %get-tuple-element.57.kv_ref), custom_call_target="tpu_custom_call" | custom-call | flops 4294967296 | bytes 786432 | tf_op jit(solution)/shard_map/pallas_call | solution.py:54
  67.9 47.1 %shard_map.131 = (f32[8,2048]{1,0:T(8,128)S(1)}, f32[96,2048]{1,0:T(8,128)S(1)}) custom-call(bf16[160,1024]{1,0:T(8,128)(2,1)S(1)} %collective-permute-done.8.refs_0_, bf16[160,1024]{1,0:T(8,128)(2,1)S(1)} %collective-permute-done.9.refs_1_, bf16[160,1024]{1,0:T(8,128)(2,1)S(1)} %collective-permute-done.10.refs_2_, ...), custom_call_target="tpu_custom_call" | custom-call | flops 12884901888 | bytes 786432 | tf_op jit(solution)/shard_map/pallas_call | solution.py:54
  117.0 47.1 %shard_map.132 = (f32[8,2048]{1,0:T(8,128)S(1)}, f32[96,2048]{1,0:T(8,128)S(1)}) custom-call(bf16[160,2048]{1,0:T(8,128)(2,1)S(1)} %collective-permute-done.17.refs_0_, bf16[160,2048]{1,0:T(8,128)(2,1)S(1)} %collective-permute-done.15.refs_1_, bf16[160,2048]{1,0:T(8,128)(2,1)S(1)} %collective-permute-done.19.refs_2_, ...), custom_call_target="tpu_custom_call" | custom-call | flops 12884901888 | bytes 786432 | tf_op jit(solution)/shard_map/pallas_call | solution.py:54
  164.1 16.7 %shard_map.133 = (bf16[80,1024]{1,0:T(8,128)(2,1)S(1)}, bf16[80,1024]{1,0:T(8,128)(2,1)S(1)}) custom-call(s32[8]{0:T(128)S(1)} %get-tuple-element.86.place.col_ref, bf16[160,1024]{1,0:T(8,128)(2,1)S(1)} %collective-permute-done.16.refs_0_, bf16[160,1024]{1,0:T(8,128)(2,1)S(1)} %collective-permute-done.18.refs_1_, ...), custom_call_target="tpu_custom_call" | custom-call | flops 4294967296 | bytes 786432 | tf_op jit(solution)/shard_map/pallas_call | solution.py:54
  182.4 3.2 %collective-permute-start.22 = (bf16[160,1024]{1,0:T(8,128)(2,1)S(1)}, bf16[160,1024]{1,0:T(8,128)(2,1)S(1)}, u32[]{:S(2)}, u32[]{:S(2)}) collective-permute-start(bf16[160,1024]{1,0:T(8,128)(2,1)S(1)} %constant_dynamic-update-slice_fusion.2.refs_0_), channel_id=1, source_target_pairs={{0,6},{1,7},{2,0},{3,1},{4,2},{5,3},{6,4},{7,5},{8,14},{9,15},{10,... | collective-permute-start | bytes 983048 | tf_op jit(solution)/shard_map/ppermute | solution.py:41
  186.8 6.6 %collective-permute-done.21.refs_1_ = bf16[160,1024]{1,0:T(8,128)(2,1)S(1)} collective-permute-done((bf16[160,1024]{1,0:T(8,128)(2,1)S(1)}, bf16[160,1024]{1,0:T(8,128)(2,1)S(1)}, u32[]{:S(2)}, u32[]{:S(2)}) %collective-permute-start.21) | collective-permute-done | bytes 327712 | tf_op jit(solution)/shard_map/ppermute | solution.py:41
  193.4 3.0 %collective-permute-done.23.refs_3_ = bf16[160,1024]{1,0:T(8,128)(2,1)S(1)} collective-permute-done((bf16[160,1024]{1,0:T(8,128)(2,1)S(1)}, bf16[160,1024]{1,0:T(8,128)(2,1)S(1)}, u32[]{:S(2)}, u32[]{:S(2)}) %collective-permute-start.23) | collective-permute-done | bytes 327712 | tf_op jit(solution)/shard_map/ppermute | solution.py:41
  197.5 3.2 %collective-permute-start.28 = (bf16[160,1024]{1,0:T(8,128)(2,1)S(1)}, bf16[160,1024]{1,0:T(8,128)(2,1)S(1)}, u32[]{:S(2)}, u32[]{:S(2)}) collective-permute-start(bf16[160,1024]{1,0:T(8,128)(2,1)S(1)} %collective-permute-done.23.refs_3_), channel_id=1, source_target_pairs={{0,6},{1,7},{2,0},{3,1},{4,2},{5,3},{6,4},{7,5},{8,14},{9,15},{10,... | collective-permute-start | bytes 983048 | tf_op jit(solution)/shard_map/ppermute | solution.py:41
  200.8 5.4 %collective-permute-done.24.refs_1_ = bf16[160,1024]{1,0:T(8,128)(2,1)S(1)} collective-permute-done((bf16[160,1024]{1,0:T(8,128)(2,1)S(1)}, bf16[160,1024]{1,0:T(8,128)(2,1)S(1)}, u32[]{:S(2)}, u32[]{:S(2)}) %collective-permute-start.24) | collective-permute-done | bytes 327712 | tf_op jit(solution)/shard_map/ppermute | solution.py:41
  206.8 2.7 %collective-permute-start.27 = (bf16[80,1024]{1,0:T(8,128)(2,1)S(1)}, bf16[80,1024]{1,0:T(8,128)(2,1)S(1)}, u32[]{:S(2)}, u32[]{:S(2)}) collective-permute-start(bf16[80,1024]{1,0:T(8,128)(2,1)S(1)} %slice.135), channel_id=1, source_target_pairs={{0,1},{1,0},{2,3},{3,2},{4,5},{5,4},{6,7},{7,6},{8,9},{9,8},{10,11... | collective-permute-start | bytes 491528 | tf_op jit(solution)/shard_map/ppermute | solution.py:41
  209.5 4.1 %shard_map.134.refs_3_ = f32[1024,1280]{1,0:T(8,128)S(1)} custom-call(s32[8]{0:T(128)S(1)} %get-tuple-element.86.place.col_ref, s32[3]{0:T(128)S(1)} %pad_add_fusion.place_ref, bf16[1280,1280]{1,0:T(8,128)(2,1)S(1)} %copy-done, bf16[160,1024]{1,0:T(8,128)(2,1)S(1)} %constant_dynamic-update-slice_fusion.2.refs_0_, ...), custom_call_target="tpu_custom_call" | custom-call | flops 1677721600 | tf_op jit(solution)/shard_map/pallas_call | solution.py:54
  213.7 3.0 %shard_map.135.refs_2_ = f32[1024,1280]{1,0:T(8,128)S(1)} custom-call(s32[8]{0:T(128)S(1)} %get-tuple-element.86.place.col_ref, s32[3]{0:T(128)S(1)} %pad_add_fusion.place_ref, bf16[1280,1280]{1,0:T(8,128)(2,1)S(1)} %copy-done, bf16[160,1024]{1,0:T(8,128)(2,1)S(1)} %collective-permute-done.26.refs_0_, ...), custom_call_target="tpu_custom_call", output_to_operand_aliasing={{}: (6, {})} | custom-call | flops 1258291200 | tf_op jit(solution)/shard_map/pallas_call | solution.py:54
  216.7 6.5 %shard_map.136 = (bf16[256,640]{1,0:T(8,128)(2,1)S(1)}, bf16[256,640]{1,0:T(8,128)(2,1)S(1)}) custom-call(s32[8]{0:T(128)S(1)} %get-tuple-element.86.place.col_ref, s32[3]{0:T(128)S(1)} %pad_add_fusion.place_ref, bf16[1280,1280]{1,0:T(8,128)(2,1)S(1)} %copy-done, bf16[80,1024]{1,0:T(8,128)(2,1)S(1)} %collective-permute-done.25.refs_0_, ...), custom_call_target="tpu_custom_call" | custom-call | flops 2097152000 | tf_op jit(solution)/shard_map/pallas_call | solution.py:54
  224.8 2.1 convolution_convert_fusion
  227.1 3.2 %collective-permute-start.33 = (bf16[64,2432]{1,0:T(8,128)(2,1)S(1)}, bf16[64,2432]{1,0:T(8,128)(2,1)S(1)}, u32[]{:S(2)}, u32[]{:S(2)}) collective-permute-start(bf16[64,2432]{1,0:T(8,128)(2,1)S(1)} %get-tuple-element.88), channel_id=1, source_target_pairs={{0,6},{1,7},{2,0},{3,1},{4,2},{5,3},{6,4},{7,5},{8,14},{9,15},{10,... | collective-permute-start | bytes 933896 | tf_op jit(solution)/shard_map/ppermute | solution.py:41
  231.5 3.2 %collective-permute-start.32 = (bf16[64,2432]{1,0:T(8,128)(2,1)S(1)}, bf16[64,2432]{1,0:T(8,128)(2,1)S(1)}, u32[]{:S(2)}, u32[]{:S(2)}) collective-permute-start(bf16[64,2432]{1,0:T(8,128)(2,1)S(1)} %get-tuple-element.87), channel_id=1, source_target_pairs={{0,6},{1,7},{2,0},{3,1},{4,2},{5,3},{6,4},{7,5},{8,14},{9,15},{10,... | collective-permute-start | bytes 933896 | tf_op jit(solution)/shard_map/ppermute | solution.py:41
  234.8 3.8 %collective-permute-done.29 = bf16[64,2432]{1,0:T(8,128)(2,1)S(1)} collective-permute-done((bf16[64,2432]{1,0:T(8,128)(2,1)S(1)}, bf16[64,2432]{1,0:T(8,128)(2,1)S(1)}, u32[]{:S(2)}, u32[]{:S(2)}) %collective-permute-start.29) | collective-permute-done | bytes 311328 | tf_op jit(solution)/shard_map/ppermute | solution.py:41
  238.8 3.3 %collective-permute-start.34 = (bf16[64,2432]{1,0:T(8,128)(2,1)S(1)}, bf16[64,2432]{1,0:T(8,128)(2,1)S(1)}, u32[]{:S(2)}, u32[]{:S(2)}) collective-permute-start(bf16[64,2432]{1,0:T(8,128)(2,1)S(1)} %get-tuple-element.91), channel_id=1, source_target_pairs={{0,6},{1,7},{2,0},{3,1},{4,2},{5,3},{6,4},{7,5},{8,14},{9,15},{10,... | collective-permute-start | bytes 933896 | tf_op jit(solution)/shard_map/ppermute | solution.py:41
  242.1 7.4 %collective-permute-done.36 = bf16[128,3328]{1,0:T(8,128)(2,1)S(1)} collective-permute-done((bf16[128,3328]{1,0:T(8,128)(2,1)S(1)}, bf16[128,3328]{1,0:T(8,128)(2,1)S(1)}, u32[]{:S(2)}, u32[]{:S(2)}) %collective-permute-start.36) | collective-permute-done | bytes 852000 | tf_op jit(solution)/shard_map/ppermute | solution.py:41
  249.8 3.2 %collective-permute-start.41 = (bf16[32,1664]{1,0:T(8,128)(2,1)S(1)}, bf16[32,1664]{1,0:T(8,128)(2,1)S(1)}, u32[]{:S(2)}, u32[]{:S(2)}) collective-permute-start(bf16[32,1664]{1,0:T(8,128)(2,1)S(1)} %get-tuple-element.94), channel_id=1, source_target_pairs={{0,6},{1,7},{2,0},{3,1},{4,2},{5,3},{6,4},{7,5},{8,14},{9,15},{10,... | collective-permute-start | bytes 319496 | tf_op jit(solution)/shard_map/ppermute | solution.py:41
  254.5 3.2 %collective-permute-start.40 = (bf16[32,1664]{1,0:T(8,128)(2,1)S(1)}, bf16[32,1664]{1,0:T(8,128)(2,1)S(1)}, u32[]{:S(2)}, u32[]{:S(2)}) collective-permute-start(bf16[32,1664]{1,0:T(8,128)(2,1)S(1)} %get-tuple-element.93), channel_id=1, source_target_pairs={{0,6},{1,7},{2,0},{3,1},{4,2},{5,3},{6,4},{7,5},{8,14},{9,15},{10,... | collective-permute-start | bytes 319496 | tf_op jit(solution)/shard_map/ppermute | solution.py:41
  257.9 3.2 %collective-permute-start.42 = (bf16[32,1664]{1,0:T(8,128)(2,1)S(1)}, bf16[32,1664]{1,0:T(8,128)(2,1)S(1)}, u32[]{:S(2)}, u32[]{:S(2)}) collective-permute-start(bf16[32,1664]{1,0:T(8,128)(2,1)S(1)} %get-tuple-element.97), channel_id=1, source_target_pairs={{0,6},{1,7},{2,0},{3,1},{4,2},{5,3},{6,4},{7,5},{8,14},{9,15},{10,... | collective-permute-start | bytes 319496 | tf_op jit(solution)/shard_map/ppermute | solution.py:41
  261.9 1.9 collective-permute-done.38
  (128 shorter events, 37.4 us)
Async XLA Ops:
  0.0 11.7 %collective-permute-start = (bf16[128,1280]{1,0:T(8,128)(2,1)}, bf16[128,1280]{1,0:T(8,128)(2,1)S(1)}, u32[]{:S(2)}, u32[]{:S(2)}) collective-permute-start(bf16[128,1280]{1,0:T(8,128)(2,1)} %bitcast.28), channel_id=1, source_target_pairs={{0,2},{1,3},{2,4},{3,5},{4,6},{5,7},{6,0},{7,1},{8,10},{9,11},{10,... | collective-permute-start | bytes 983048 | tf_op jit(solution)/shard_map/ppermute | solution.py:41
  1.7 10.0 %collective-permute-start.1 = (bf16[128,1280]{1,0:T(8,128)(2,1)}, bf16[128,1280]{1,0:T(8,128)(2,1)S(1)}, u32[]{:S(2)}, u32[]{:S(2)}) collective-permute-start(bf16[128,1280]{1,0:T(8,128)(2,1)} %bitcast.29), channel_id=1, source_target_pairs={{0,6},{1,7},{2,0},{3,1},{4,2},{5,3},{6,4},{7,5},{8,14},{9,15},{10,... | collective-permute-start | bytes 983048 | tf_op jit(solution)/shard_map/ppermute | solution.py:41
  3.2 11.5 %collective-permute-start.2 = (bf16[128,1280]{1,0:T(8,128)(2,1)}, bf16[128,1280]{1,0:T(8,128)(2,1)S(1)}, u32[]{:S(2)}, u32[]{:S(2)}) collective-permute-start(bf16[128,1280]{1,0:T(8,128)(2,1)} %bitcast.30), channel_id=1, source_target_pairs={{0,1},{1,0},{2,3},{3,2},{4,5},{5,4},{6,7},{7,6},{8,9},{9,8},{10,11... | collective-permute-start | bytes 983048 | tf_op jit(solution)/shard_map/ppermute | solution.py:41
  14.7 9.8 %collective-permute-start.3 = (bf16[128,1280]{1,0:T(8,128)(2,1)S(1)}, bf16[128,1280]{1,0:T(8,128)(2,1)S(1)}, u32[]{:S(2)}, u32[]{:S(2)}) collective-permute-start(bf16[128,1280]{1,0:T(8,128)(2,1)S(1)} %collective-permute-done.refs_1_.refs_5_), channel_id=1, source_target_pairs={{0,1},{1,0},{2,3},{3,2},{4,5},{5,4},{6,7},{7,6},{8,9},{9,8},{10,11... | collective-permute-start | bytes 983048 | tf_op jit(solution)/shard_map/ppermute | solution.py:41
  17.9 9.6 %collective-permute-start.5 = (bf16[128,1280]{1,0:T(8,128)(2,1)S(1)}, bf16[128,1280]{1,0:T(8,128)(2,1)S(1)}, u32[]{:S(2)}, u32[]{:S(2)}) collective-permute-start(bf16[128,1280]{1,0:T(8,128)(2,1)S(1)} %collective-permute-done.refs_1_.refs_5_), channel_id=1, source_target_pairs={{0,2},{1,3},{2,4},{3,5},{4,6},{5,7},{6,0},{7,1},{8,10},{9,11},{10,... | collective-permute-start | bytes 983048 | tf_op jit(solution)/shard_map/ppermute | solution.py:41
  18.2 12.2 %collective-permute-start.7 = (bf16[128,1280]{1,0:T(8,128)(2,1)S(1)}, bf16[128,1280]{1,0:T(8,128)(2,1)S(1)}, u32[]{:S(2)}, u32[]{:S(2)}) collective-permute-start(bf16[128,1280]{1,0:T(8,128)(2,1)S(1)} %collective-permute-done.2.refs_3_.refs_7_), channel_id=1, source_target_pairs={{0,6},{1,7},{2,0},{3,1},{4,2},{5,3},{6,4},{7,5},{8,14},{9,15},{10,... | collective-permute-start | bytes 983048 | tf_op jit(solution)/shard_map/ppermute | solution.py:41
  35.2 10.1 %collective-permute-start.10 = (bf16[160,1024]{1,0:T(8,128)(2,1)S(1)}, bf16[160,1024]{1,0:T(8,128)(2,1)S(1)}, u32[]{:S(2)}, u32[]{:S(2)}) collective-permute-start(bf16[160,1024]{1,0:T(8,128)(2,1)S(1)} %get-tuple-element.57.kv_ref), channel_id=1, source_target_pairs={{0,16},{1,17},{2,18},{3,19},{4,20},{5,21},{6,22},{7,23},{8,24},{9,... | collective-permute-start | bytes 983048 | tf_op jit(solution)/shard_map/ppermute | solution.py:41
  36.7 26.8 %collective-permute-start.8 = (bf16[160,1024]{1,0:T(8,128)(2,1)S(1)}, bf16[160,1024]{1,0:T(8,128)(2,1)S(1)}, u32[]{:S(2)}, u32[]{:S(2)}) collective-permute-start(bf16[160,1024]{1,0:T(8,128)(2,1)S(1)} %get-tuple-element.57.kv_ref), channel_id=1, source_target_pairs={{0,32},{1,33},{2,34},{3,35},{4,36},{5,37},{6,38},{7,39},{8,40},{9,... | collective-permute-start | bytes 983048 | tf_op jit(solution)/shard_map/ppermute | solution.py:41
  38.2 25.2 %collective-permute-start.9 = (bf16[160,1024]{1,0:T(8,128)(2,1)S(1)}, bf16[160,1024]{1,0:T(8,128)(2,1)S(1)}, u32[]{:S(2)}, u32[]{:S(2)}) collective-permute-start(bf16[160,1024]{1,0:T(8,128)(2,1)S(1)} %get-tuple-element.57.kv_ref), channel_id=1, source_target_pairs={{0,96},{1,97},{2,98},{3,99},{4,100},{5,101},{6,102},{7,103},{8,104... | collective-permute-start | bytes 983048 | tf_op jit(solution)/shard_map/ppermute | solution.py:41
  39.9 23.6 %collective-permute-start.12 = (bf16[160,1024]{1,0:T(8,128)(2,1)S(1)}, bf16[160,1024]{1,0:T(8,128)(2,1)S(1)}, u32[]{:S(2)}, u32[]{:S(2)}) collective-permute-start(bf16[160,1024]{1,0:T(8,128)(2,1)S(1)} %slice.131), channel_id=1, source_target_pairs={{0,32},{1,33},{2,34},{3,35},{4,36},{5,37},{6,38},{7,39},{8,40},{9,... | collective-permute-start | bytes 983048 | tf_op jit(solution)/shard_map/ppermute | solution.py:41
  40.4 23.1 %collective-permute-start.13 = (bf16[160,1024]{1,0:T(8,128)(2,1)S(1)}, bf16[160,1024]{1,0:T(8,128)(2,1)S(1)}, u32[]{:S(2)}, u32[]{:S(2)}) collective-permute-start(bf16[160,1024]{1,0:T(8,128)(2,1)S(1)} %slice.131), channel_id=1, source_target_pairs={{0,96},{1,97},{2,98},{3,99},{4,100},{5,101},{6,102},{7,103},{8,104... | collective-permute-start | bytes 983048 | tf_op jit(solution)/shard_map/ppermute | solution.py:41
  45.3 18.2 %collective-permute-start.14 = (bf16[160,1024]{1,0:T(8,128)(2,1)S(1)}, bf16[160,1024]{1,0:T(8,128)(2,1)S(1)}, u32[]{:S(2)}, u32[]{:S(2)}) collective-permute-start(bf16[160,1024]{1,0:T(8,128)(2,1)S(1)} %slice.131), channel_id=1, source_target_pairs={{0,16},{1,17},{2,18},{3,19},{4,20},{5,21},{6,22},{7,23},{8,24},{9,... | collective-permute-start | bytes 983048 | tf_op jit(solution)/shard_map/ppermute | solution.py:41
  63.6 51.4 %collective-permute-start.15 = (bf16[160,2048]{1,0:T(8,128)(2,1)S(1)}, bf16[160,2048]{1,0:T(8,128)(2,1)S(1)}, u32[]{:S(2)}, u32[]{:S(2)}) collective-permute-start(bf16[160,2048]{1,0:T(8,128)(2,1)S(1)} %constant_dynamic-update-slice_fusion), channel_id=1, source_target_pairs={{0,16},{1,17},{2,18},{3,19},{4,20},{5,21},{6,22},{7,23},{8,24},{9,... | collective-permute-start | bytes 1966088 | tf_op jit(solution)/shard_map/ppermute | solution.py:41
  64.3 51.1 %collective-permute-start.17 = (bf16[160,2048]{1,0:T(8,128)(2,1)S(1)}, bf16[160,2048]{1,0:T(8,128)(2,1)S(1)}, u32[]{:S(2)}, u32[]{:S(2)}) collective-permute-start(bf16[160,2048]{1,0:T(8,128)(2,1)S(1)} %constant_dynamic-update-slice_fusion), channel_id=1, source_target_pairs={{0,32},{1,33},{2,34},{3,35},{4,36},{5,37},{6,38},{7,39},{8,40},{9,... | collective-permute-start | bytes 1966088 | tf_op jit(solution)/shard_map/ppermute | solution.py:41
  66.0 51.0 %collective-permute-start.19 = (bf16[160,2048]{1,0:T(8,128)(2,1)S(1)}, bf16[160,2048]{1,0:T(8,128)(2,1)S(1)}, u32[]{:S(2)}, u32[]{:S(2)}) collective-permute-start(bf16[160,2048]{1,0:T(8,128)(2,1)S(1)} %pad_maximum_fusion), channel_id=1, source_target_pairs={{0,96},{1,97},{2,98},{3,99},{4,100},{5,101},{6,102},{7,103},{8,104... | collective-permute-start | bytes 1966088 | tf_op jit(solution)/shard_map/ppermute | solution.py:41
  115.0 49.0 %collective-permute-start.16 = (bf16[160,1024]{1,0:T(8,128)(2,1)S(1)}, bf16[160,1024]{1,0:T(8,128)(2,1)S(1)}, u32[]{:S(2)}, u32[]{:S(2)}) collective-permute-start(bf16[160,1024]{1,0:T(8,128)(2,1)S(1)} %slice.132), channel_id=1, source_target_pairs={{0,32},{1,33},{2,34},{3,35},{4,36},{5,37},{6,38},{7,39},{8,40},{9,... | collective-permute-start | bytes 983048 | tf_op jit(solution)/shard_map/ppermute | solution.py:41
  115.5 48.6 %collective-permute-start.18 = (bf16[160,1024]{1,0:T(8,128)(2,1)S(1)}, bf16[160,1024]{1,0:T(8,128)(2,1)S(1)}, u32[]{:S(2)}, u32[]{:S(2)}) collective-permute-start(bf16[160,1024]{1,0:T(8,128)(2,1)S(1)} %slice.133), channel_id=1, source_target_pairs={{0,16},{1,17},{2,18},{3,19},{4,20},{5,21},{6,22},{7,23},{8,24},{9,... | collective-permute-start | bytes 983048 | tf_op jit(solution)/shard_map/ppermute | solution.py:41
  182.4 11.0 %collective-permute-start.21 = (bf16[160,1024]{1,0:T(8,128)(2,1)S(1)}, bf16[160,1024]{1,0:T(8,128)(2,1)S(1)}, u32[]{:S(2)}, u32[]{:S(2)}) collective-permute-start(bf16[160,1024]{1,0:T(8,128)(2,1)S(1)} %constant_dynamic-update-slice_fusion.2.refs_0_), channel_id=1, source_target_pairs={{0,2},{1,3},{2,4},{3,5},{4,6},{5,7},{6,0},{7,1},{8,10},{9,11},{10,... | collective-permute-start | bytes 983048 | tf_op jit(solution)/shard_map/ppermute | solution.py:41
  182.4 11.0 %collective-permute-start.22 = (bf16[160,1024]{1,0:T(8,128)(2,1)S(1)}, bf16[160,1024]{1,0:T(8,128)(2,1)S(1)}, u32[]{:S(2)}, u32[]{:S(2)}) collective-permute-start(bf16[160,1024]{1,0:T(8,128)(2,1)S(1)} %constant_dynamic-update-slice_fusion.2.refs_0_), channel_id=1, source_target_pairs={{0,6},{1,7},{2,0},{3,1},{4,2},{5,3},{6,4},{7,5},{8,14},{9,15},{10,... | collective-permute-start | bytes 983048 | tf_op jit(solution)/shard_map/ppermute | solution.py:41
  185.7 10.7 %collective-permute-start.23 = (bf16[160,1024]{1,0:T(8,128)(2,1)S(1)}, bf16[160,1024]{1,0:T(8,128)(2,1)S(1)}, u32[]{:S(2)}, u32[]{:S(2)}) collective-permute-start(bf16[160,1024]{1,0:T(8,128)(2,1)S(1)} %constant_dynamic-update-slice_fusion.2.refs_0_), channel_id=1, source_target_pairs={{0,1},{1,0},{2,3},{3,2},{4,5},{5,4},{6,7},{7,6},{8,9},{9,8},{10,11... | collective-permute-start | bytes 983048 | tf_op jit(solution)/shard_map/ppermute | solution.py:41
  196.4 9.8 %collective-permute-start.24 = (bf16[160,1024]{1,0:T(8,128)(2,1)S(1)}, bf16[160,1024]{1,0:T(8,128)(2,1)S(1)}, u32[]{:S(2)}, u32[]{:S(2)}) collective-permute-start(bf16[160,1024]{1,0:T(8,128)(2,1)S(1)} %collective-permute-done.21.refs_1_), channel_id=1, source_target_pairs={{0,1},{1,0},{2,3},{3,2},{4,5},{5,4},{6,7},{7,6},{8,9},{9,8},{10,11... | collective-permute-start | bytes 983048 | tf_op jit(solution)/shard_map/ppermute | solution.py:41
  197.5 9.3 %collective-permute-start.26 = (bf16[160,1024]{1,0:T(8,128)(2,1)S(1)}, bf16[160,1024]{1,0:T(8,128)(2,1)S(1)}, u32[]{:S(2)}, u32[]{:S(2)}) collective-permute-start(bf16[160,1024]{1,0:T(8,128)(2,1)S(1)} %collective-permute-done.21.refs_1_), channel_id=1, source_target_pairs={{0,2},{1,3},{2,4},{3,5},{4,6},{5,7},{6,0},{7,1},{8,10},{9,11},{10,... | collective-permute-start | bytes 983048 | tf_op jit(solution)/shard_map/ppermute | solution.py:41
  197.5 16.1 %collective-permute-start.28 = (bf16[160,1024]{1,0:T(8,128)(2,1)S(1)}, bf16[160,1024]{1,0:T(8,128)(2,1)S(1)}, u32[]{:S(2)}, u32[]{:S(2)}) collective-permute-start(bf16[160,1024]{1,0:T(8,128)(2,1)S(1)} %collective-permute-done.23.refs_3_), channel_id=1, source_target_pairs={{0,6},{1,7},{2,0},{3,1},{4,2},{5,3},{6,4},{7,5},{8,14},{9,15},{10,... | collective-permute-start | bytes 983048 | tf_op jit(solution)/shard_map/ppermute | solution.py:41
  206.2 10.5 %collective-permute-start.25 = (bf16[80,1024]{1,0:T(8,128)(2,1)S(1)}, bf16[80,1024]{1,0:T(8,128)(2,1)S(1)}, u32[]{:S(2)}, u32[]{:S(2)}) collective-permute-start(bf16[80,1024]{1,0:T(8,128)(2,1)S(1)} %slice.134), channel_id=1, source_target_pairs={{0,2},{1,3},{2,4},{3,5},{4,6},{5,7},{6,0},{7,1},{8,10},{9,11},{10,... | collective-permute-start | bytes 491528 | tf_op jit(solution)/shard_map/ppermute | solution.py:41
  206.8 9.9 %collective-permute-start.27 = (bf16[80,1024]{1,0:T(8,128)(2,1)S(1)}, bf16[80,1024]{1,0:T(8,128)(2,1)S(1)}, u32[]{:S(2)}, u32[]{:S(2)}) collective-permute-start(bf16[80,1024]{1,0:T(8,128)(2,1)S(1)} %slice.135), channel_id=1, source_target_pairs={{0,1},{1,0},{2,3},{3,2},{4,5},{5,4},{6,7},{7,6},{8,9},{9,8},{10,11... | collective-permute-start | bytes 491528 | tf_op jit(solution)/shard_map/ppermute | solution.py:41
  227.1 11.5 %collective-permute-start.29 = (bf16[64,2432]{1,0:T(8,128)(2,1)S(1)}, bf16[64,2432]{1,0:T(8,128)(2,1)S(1)}, u32[]{:S(2)}, u32[]{:S(2)}) collective-permute-start(bf16[64,2432]{1,0:T(8,128)(2,1)S(1)} %get-tuple-element.90), channel_id=1, source_target_pairs={{0,2},{1,3},{2,4},{3,5},{4,6},{5,7},{6,0},{7,1},{8,10},{9,11},{10,... | collective-permute-start | bytes 933896 | tf_op jit(solution)/shard_map/ppermute | solution.py:41
  227.1 11.4 %collective-permute-start.33 = (bf16[64,2432]{1,0:T(8,128)(2,1)S(1)}, bf16[64,2432]{1,0:T(8,128)(2,1)S(1)}, u32[]{:S(2)}, u32[]{:S(2)}) collective-permute-start(bf16[64,2432]{1,0:T(8,128)(2,1)S(1)} %get-tuple-element.88), channel_id=1, source_target_pairs={{0,6},{1,7},{2,0},{3,1},{4,2},{5,3},{6,4},{7,5},{8,14},{9,15},{10,... | collective-permute-start | bytes 933896 | tf_op jit(solution)/shard_map/ppermute | solution.py:41
  230.4 19.1 %collective-permute-start.36 = (bf16[128,3328]{1,0:T(8,128)(2,1)S(1)}, bf16[128,3328]{1,0:T(8,128)(2,1)S(1)}, u32[]{:S(2)}, u32[]{:S(2)}) collective-permute-start(bf16[128,3328]{1,0:T(8,128)(2,1)S(1)} %slice.136), channel_id=1, source_target_pairs={{0,1},{1,0},{2,3},{3,2},{4,5},{5,4},{6,7},{7,6},{8,9},{9,8},{10,11... | collective-permute-start | bytes 2555912 | tf_op jit(solution)/shard_map/ppermute | solution.py:41
  231.5 18.3 %collective-permute-start.31 = (bf16[64,2432]{1,0:T(8,128)(2,1)S(1)}, bf16[64,2432]{1,0:T(8,128)(2,1)S(1)}, u32[]{:S(2)}, u32[]{:S(2)}) collective-permute-start(bf16[64,2432]{1,0:T(8,128)(2,1)S(1)} %get-tuple-element.89), channel_id=1, source_target_pairs={{0,2},{1,3},{2,4},{3,5},{4,6},{5,7},{6,0},{7,1},{8,10},{9,11},{10,... | collective-permute-start | bytes 933896 | tf_op jit(solution)/shard_map/ppermute | solution.py:41
  231.5 21.5 %collective-permute-start.32 = (bf16[64,2432]{1,0:T(8,128)(2,1)S(1)}, bf16[64,2432]{1,0:T(8,128)(2,1)S(1)}, u32[]{:S(2)}, u32[]{:S(2)}) collective-permute-start(bf16[64,2432]{1,0:T(8,128)(2,1)S(1)} %get-tuple-element.87), channel_id=1, source_target_pairs={{0,6},{1,7},{2,0},{3,1},{4,2},{5,3},{6,4},{7,5},{8,14},{9,15},{10,... | collective-permute-start | bytes 933896 | tf_op jit(solution)/shard_map/ppermute | solution.py:41
  238.7 14.3 %collective-permute-start.30 = (bf16[64,2432]{1,0:T(8,128)(2,1)S(1)}, bf16[64,2432]{1,0:T(8,128)(2,1)S(1)}, u32[]{:S(2)}, u32[]{:S(2)}) collective-permute-start(bf16[64,2432]{1,0:T(8,128)(2,1)S(1)} %get-tuple-element.92), channel_id=1, source_target_pairs={{0,2},{1,3},{2,4},{3,5},{4,6},{5,7},{6,0},{7,1},{8,10},{9,11},{10,... | collective-permute-start | bytes 933896 | tf_op jit(solution)/shard_map/ppermute | solution.py:41
  238.8 14.2 %collective-permute-start.34 = (bf16[64,2432]{1,0:T(8,128)(2,1)S(1)}, bf16[64,2432]{1,0:T(8,128)(2,1)S(1)}, u32[]{:S(2)}, u32[]{:S(2)}) collective-permute-start(bf16[64,2432]{1,0:T(8,128)(2,1)S(1)} %get-tuple-element.91), channel_id=1, source_target_pairs={{0,6},{1,7},{2,0},{3,1},{4,2},{5,3},{6,4},{7,5},{8,14},{9,15},{10,... | collective-permute-start | bytes 933896 | tf_op jit(solution)/shard_map/ppermute | solution.py:41
  (23 other events, 293.5 us)

commit v5 on v4

--- a/solution.py
+++ b/solution.py
@@ -115,22 +115,15 @@
 def attend_chunks(chunks, q_ref, m_ref, o_ref, k_all, v_all, flag):
     keys = k_all.shape[0]
     queries = q_ref.shape[1]
-    step, unroll = (keys, 2) if keys <= 2048 else (keys // 2, 1)
-    turns = queries // (unroll * QUERY_BLOCK)
+    step = keys if keys <= 2048 else max(d for d in (1536, 1024) if keys % d == 0)
+    turns = queries // (2 * QUERY_BLOCK)
     at = 0
-    ones = jnp.ones((16, 512), BF)
     for ref in chunks:
-
-        def place(i, carry, ref=ref, at=at):
-            cols = pl.ds(pl.multiple_of(i * 512, 512), 512)
-            spot = pl.ds(pl.multiple_of(at + i * 512, 512), 512)
-            keys_part = ref[-2 * HEAD_DIM : -HEAD_DIM, cols]
-            k_all[spot, :] = jnp.concatenate([keys_part, ones], axis=0).T
-            v_all[:, spot] = jnp.concatenate([ref[-HEAD_DIM:, cols], ones], axis=0)
-            return carry
-
-        lax.fori_loop(0, ref.shape[1] // 512, place, 0)
-        at += ref.shape[1]
+        n = ref.shape[1]
+        ones = jnp.ones((16, n), BF)
+        k_all[at : at + n, :] = jnp.concatenate([ref[-2 * HEAD_DIM : -HEAD_DIM, :], ones], axis=0).T
+        v_all[:, at : at + n] = jnp.concatenate([ref[-HEAD_DIM:, :], ones], axis=0)
+        at += n
     flag[0] = 1
 
     def attempt(tries, carry):
@@ -140,8 +133,8 @@
 
             def block(t, carry):
                 rows = pl.ds(pl.multiple_of((t // turns) * step, step), step)
-                for i in range(unroll):
-                    col = (t % turns) * (unroll * QUERY_BLOCK) + i * QUERY_BLOCK
+                for i in range(2):
+                    col = (t % turns) * (2 * QUERY_BLOCK) + i * QUERY_BLOCK
                     cols = pl.ds(pl.multiple_of(col, QUERY_BLOCK), QUERY_BLOCK)
                     s = jnp.dot(k_all[rows, :], q_ref[:, cols], preferred_element_type=F32)
                     p = jnp.exp2(s).astype(BF)
@@ -433,7 +426,6 @@
             (m_shape, o_shape),
             [("v", t) for t in chunks] + [("v", q), ("v", start)],
             scratch(keys),
-            grant=12,
             **work(keys),
         )
         tops.append(top)
@@ -507,7 +499,7 @@
 
 
 def scatter_output(hidden_a, hidden_b, down_weight, down_bias, mirror):
-    split = 4864
+    split = 4608
     part_b = jnp.dot(
         hidden_b, down_weight[:, split:], preferred_element_type=F32
     ).astype(BF)
@@ -519,7 +511,7 @@
     total_a = ring(part_a, 64, True)
     got_a = send(total_a[32:].astype(BF), mirror)
     block_b = (part_b[:128].astype(F32) + got_b.astype(F32)).astype(BF)
-    total_b = ring(block_b, 32, True)
+    total_b = ring(block_b, 32, False)
     total_a = total_a[:32] + got_a.astype(F32)
     return (jnp.concatenate([total_a, total_b], axis=1) + down_bias[None, :]).astype(BF)
 

time: 265 us -> 268 us (1.011)
  starting transfers between devices: 63.9 us -> 66.9 us
  local copies, waits for them, and re-layouts: 3.7 us -> 6.68 us
    unnamed x26, local copies, waits for them, and re-layouts: 1.07 us -> 4.06 us
    ppermute x43 -> x41, starting transfers between devices: 63.9 us -> 66.9 us  [send(): return lax.ppermute(value, AXES, perm)]
    ppermute x43 -> x41, waiting for transfers between devices: 44.3 us -> 41.8 us  [send(): return lax.ppermute(value, AXES, perm)]
  transfers between devices with their start and end apart: 43 -> 41, of which waited for: 14 -> 13; matrix products, arithmetic and copies ran while one was open for 2% -> 2% of each run, Pallas kernels for 46% -> 45%
where the time goes in v5:
time: 268 us; the launch traced here: 267 us
  Pallas kernels  144 us (54%)
  starting transfers between devices  66.9 us (25%)
  waiting for transfers between devices  41.8 us (16%)
  local copies, waits for them, and re-layouts  6.68 us (2%)
  other arithmetic  3.89 us (1%)
  matrix products  3.68 us (1%)
    pallas_call x10, Pallas kernels, call(): pl.pallas_call(kernel, out_shape=outs, in_specs=specs, out_specs=jax.tree...  144 us
    ppermute x41, starting transfers between devices, send(): return lax.ppermute(value, AXES, perm)  66.9 us
    ppermute x41, waiting for transfers between devices, send(): return lax.ppermute(value, AXES, perm)  41.8 us
  transfers between devices with their start and end apart: 41, of which 13 were waited for; matrix products, arithmetic and copies ran while one was open for 2% of the time, Pallas kernels for 45%

profile of v5, /device:TPU:0, one launch (start us, length us, event | category | flops | bytes accessed | tf_op | source)
XLA Modules:
  0.0 267.2 jit_solution(14006347441248292493)
XLA Ops:
  3.2 4.0 %collective-permute-start.2 = (bf16[128,1280]{1,0:T(8,128)(2,1)}, bf16[128,1280]{1,0:T(8,128)(2,1)S(1)}, u32[]{:S(2)}, u32[]{:S(2)}) collective-permute-start(bf16[128,1280]{1,0:T(8,128)(2,1)} %bitcast.30), channel_id=1, source_target_pairs={{0,1},{1,0},{2,3},{3,2},{4,5},{5,4},{6,7},{7,6},{8,9},{9,8},{10,11... | collective-permute-start | bytes 983048 | tf_op jit(solution)/shard_map/ppermute | solution.py:41
  11.6 3.0 %collective-permute-done.2.refs_3_.refs_7_ = bf16[128,1280]{1,0:T(8,128)(2,1)S(1)} collective-permute-done((bf16[128,1280]{1,0:T(8,128)(2,1)}, bf16[128,1280]{1,0:T(8,128)(2,1)S(1)}, u32[]{:S(2)}, u32[]{:S(2)}) %collective-permute-start.2) | collective-permute-done | bytes 327712 | tf_op jit(solution)/shard_map/ppermute | solution.py:41
  14.6 3.2 %collective-permute-start.3 = (bf16[128,1280]{1,0:T(8,128)(2,1)S(1)}, bf16[128,1280]{1,0:T(8,128)(2,1)S(1)}, u32[]{:S(2)}, u32[]{:S(2)}) collective-permute-start(bf16[128,1280]{1,0:T(8,128)(2,1)S(1)} %collective-permute-done.refs_1_.refs_5_), channel_id=1, source_target_pairs={{0,1},{1,0},{2,3},{3,2},{4,5},{5,4},{6,7},{7,6},{8,9},{9,8},{10,11... | collective-permute-start | bytes 983048 | tf_op jit(solution)/shard_map/ppermute | solution.py:41
  18.1 3.0 %collective-permute-start.7 = (bf16[128,1280]{1,0:T(8,128)(2,1)S(1)}, bf16[128,1280]{1,0:T(8,128)(2,1)S(1)}, u32[]{:S(2)}, u32[]{:S(2)}) collective-permute-start(bf16[128,1280]{1,0:T(8,128)(2,1)S(1)} %collective-permute-done.2.refs_3_.refs_7_), channel_id=1, source_target_pairs={{0,6},{1,7},{2,0},{3,1},{4,2},{5,3},{6,4},{7,5},{8,14},{9,15},{10,... | collective-permute-start | bytes 983048 | tf_op jit(solution)/shard_map/ppermute | solution.py:41
  21.1 3.4 %collective-permute-done.3.refs_1_.refs_9_ = bf16[128,1280]{1,0:T(8,128)(2,1)S(1)} collective-permute-done((bf16[128,1280]{1,0:T(8,128)(2,1)S(1)}, bf16[128,1280]{1,0:T(8,128)(2,1)S(1)}, u32[]{:S(2)}, u32[]{:S(2)}) %collective-permute-start.3) | collective-permute-done | bytes 327712 | tf_op jit(solution)/shard_map/ppermute | solution.py:41
  24.8 2.6 collective-permute-done.5.refs_0_.refs_8_
  40.3 2.9 %collective-permute-start.13 = (bf16[160,1024]{1,0:T(8,128)(2,1)S(1)}, bf16[160,1024]{1,0:T(8,128)(2,1)S(1)}, u32[]{:S(2)}, u32[]{:S(2)}) collective-permute-start(bf16[160,1024]{1,0:T(8,128)(2,1)S(1)} %slice.131), channel_id=1, source_target_pairs={{0,96},{1,97},{2,98},{3,99},{4,100},{5,101},{6,102},{7,103},{8,104... | collective-permute-start | bytes 983048 | tf_op jit(solution)/shard_map/ppermute | solution.py:41
  43.2 2.4 collective-permute-done.10.refs_2_
  46.7 16.6 %shard_map.130 = (bf16[96,2048]{1,0:T(8,128)(2,1)S(1)}, f32[8,2048]{1,0:T(8,128)S(1)}, f32[8,2048]{1,0:T(8,128)S(1)}, f32[96,2048]{1,0:T(8,128)S(1)}) custom-call(bf16[80,1024]{1,0:T(8,128)(2,1)S(1)} %get-tuple-element.61.own_q, bf16[240,1024]{1,0:T(8,128)(2,1)S(1)} %collective-permute-done.11.swapped, bf16[160,1024]{1,0:T(8,128)(2,1)S(1)} %get-tuple-element.57.kv_ref), custom_call_target="tpu_custom_call" | custom-call | flops 4294967296 | bytes 786432 | tf_op jit(solution)/shard_map/pallas_call | solution.py:54
  68.0 46.7 %shard_map.131 = (f32[8,2048]{1,0:T(8,128)S(1)}, f32[96,2048]{1,0:T(8,128)S(1)}) custom-call(bf16[160,1024]{1,0:T(8,128)(2,1)S(1)} %collective-permute-done.8.refs_0_, bf16[160,1024]{1,0:T(8,128)(2,1)S(1)} %collective-permute-done.9.refs_1_, bf16[160,1024]{1,0:T(8,128)(2,1)S(1)} %collective-permute-done.10.refs_2_, ...), custom_call_target="tpu_custom_call" | custom-call | flops 12884901888 | bytes 786432 | tf_op jit(solution)/shard_map/pallas_call | solution.py:54
  116.3 46.7 %shard_map.132 = (f32[8,2048]{1,0:T(8,128)S(1)}, f32[96,2048]{1,0:T(8,128)S(1)}) custom-call(bf16[160,2048]{1,0:T(8,128)(2,1)S(1)} %collective-permute-done.17.refs_0_, bf16[160,2048]{1,0:T(8,128)(2,1)S(1)} %collective-permute-done.15.refs_1_, bf16[160,2048]{1,0:T(8,128)(2,1)S(1)} %collective-permute-done.19.refs_2_, ...), custom_call_target="tpu_custom_call" | custom-call | flops 12884901888 | bytes 786432 | tf_op jit(solution)/shard_map/pallas_call | solution.py:54
  163.0 16.6 %shard_map.133 = (bf16[80,1024]{1,0:T(8,128)(2,1)S(1)}, bf16[80,1024]{1,0:T(8,128)(2,1)S(1)}) custom-call(s32[8]{0:T(128)S(1)} %get-tuple-element.86.place.col_ref, bf16[160,1024]{1,0:T(8,128)(2,1)S(1)} %collective-permute-done.16.refs_0_, bf16[160,1024]{1,0:T(8,128)(2,1)S(1)} %collective-permute-done.18.refs_1_, ...), custom_call_target="tpu_custom_call" | custom-call | flops 4294967296 | bytes 786432 | tf_op jit(solution)/shard_map/pallas_call | solution.py:54
  184.4 4.1 %collective-permute-start.23 = (bf16[160,1024]{1,0:T(8,128)(2,1)S(1)}, bf16[160,1024]{1,0:T(8,128)(2,1)S(1)}, u32[]{:S(2)}, u32[]{:S(2)}) collective-permute-start(bf16[160,1024]{1,0:T(8,128)(2,1)S(1)} %constant_dynamic-update-slice_fusion.2.refs_0_), channel_id=1, source_target_pairs={{0,1},{1,0},{2,3},{3,2},{4,5},{5,4},{6,7},{7,6},{8,9},{9,8},{10,11... | collective-permute-start | bytes 983048 | tf_op jit(solution)/shard_map/ppermute | solution.py:41
  188.5 3.6 %collective-permute-done.21.refs_1_ = bf16[160,1024]{1,0:T(8,128)(2,1)S(1)} collective-permute-done((bf16[160,1024]{1,0:T(8,128)(2,1)S(1)}, bf16[160,1024]{1,0:T(8,128)(2,1)S(1)}, u32[]{:S(2)}, u32[]{:S(2)}) %collective-permute-start.21) | collective-permute-done | bytes 327712 | tf_op jit(solution)/shard_map/ppermute | solution.py:41
  192.1 3.9 %collective-permute-done.23.refs_3_ = bf16[160,1024]{1,0:T(8,128)(2,1)S(1)} collective-permute-done((bf16[160,1024]{1,0:T(8,128)(2,1)S(1)}, bf16[160,1024]{1,0:T(8,128)(2,1)S(1)}, u32[]{:S(2)}, u32[]{:S(2)}) %collective-permute-start.23) | collective-permute-done | bytes 327712 | tf_op jit(solution)/shard_map/ppermute | solution.py:41
  196.0 3.2 %collective-permute-start.24 = (bf16[160,1024]{1,0:T(8,128)(2,1)S(1)}, bf16[160,1024]{1,0:T(8,128)(2,1)S(1)}, u32[]{:S(2)}, u32[]{:S(2)}) collective-permute-start(bf16[160,1024]{1,0:T(8,128)(2,1)S(1)} %collective-permute-done.21.refs_1_), channel_id=1, source_target_pairs={{0,1},{1,0},{2,3},{3,2},{4,5},{5,4},{6,7},{7,6},{8,9},{9,8},{10,11... | collective-permute-start | bytes 983048 | tf_op jit(solution)/shard_map/ppermute | solution.py:41
  199.2 3.2 %collective-permute-start.28 = (bf16[160,1024]{1,0:T(8,128)(2,1)S(1)}, bf16[160,1024]{1,0:T(8,128)(2,1)S(1)}, u32[]{:S(2)}, u32[]{:S(2)}) collective-permute-start(bf16[160,1024]{1,0:T(8,128)(2,1)S(1)} %collective-permute-done.23.refs_3_), channel_id=1, source_target_pairs={{0,6},{1,7},{2,0},{3,1},{4,2},{5,3},{6,4},{7,5},{8,14},{9,15},{10,... | collective-permute-start | bytes 983048 | tf_op jit(solution)/shard_map/ppermute | solution.py:41
  202.5 3.6 %collective-permute-done.24.refs_1_ = bf16[160,1024]{1,0:T(8,128)(2,1)S(1)} collective-permute-done((bf16[160,1024]{1,0:T(8,128)(2,1)S(1)}, bf16[160,1024]{1,0:T(8,128)(2,1)S(1)}, u32[]{:S(2)}, u32[]{:S(2)}) %collective-permute-start.24) | collective-permute-done | bytes 327712 | tf_op jit(solution)/shard_map/ppermute | solution.py:41
  206.2 2.6 collective-permute-done.26.refs_0_
  209.5 4.1 %shard_map.134.refs_3_ = f32[1024,1280]{1,0:T(8,128)S(1)} custom-call(s32[8]{0:T(128)S(1)} %get-tuple-element.86.place.col_ref, s32[3]{0:T(128)S(1)} %pad_add_fusion.place_ref, bf16[1280,1280]{1,0:T(8,128)(2,1)S(1)} %copy-done, bf16[160,1024]{1,0:T(8,128)(2,1)S(1)} %constant_dynamic-update-slice_fusion.2.refs_0_, ...), custom_call_target="tpu_custom_call" | custom-call | flops 1677721600 | tf_op jit(solution)/shard_map/pallas_call | solution.py:54
  213.7 3.0 %shard_map.135.refs_2_ = f32[1024,1280]{1,0:T(8,128)S(1)} custom-call(s32[8]{0:T(128)S(1)} %get-tuple-element.86.place.col_ref, s32[3]{0:T(128)S(1)} %pad_add_fusion.place_ref, bf16[1280,1280]{1,0:T(8,128)(2,1)S(1)} %copy-done, bf16[160,1024]{1,0:T(8,128)(2,1)S(1)} %collective-permute-done.26.refs_0_, ...), custom_call_target="tpu_custom_call", output_to_operand_aliasing={{}: (6, {})} | custom-call | flops 1258291200 | tf_op jit(solution)/shard_map/pallas_call | solution.py:54
  216.7 6.5 %shard_map.136 = (bf16[256,640]{1,0:T(8,128)(2,1)S(1)}, bf16[256,640]{1,0:T(8,128)(2,1)S(1)}) custom-call(s32[8]{0:T(128)S(1)} %get-tuple-element.86.place.col_ref, s32[3]{0:T(128)S(1)} %pad_add_fusion.place_ref, bf16[1280,1280]{1,0:T(8,128)(2,1)S(1)} %copy-done, bf16[80,1024]{1,0:T(8,128)(2,1)S(1)} %collective-permute-done.25.refs_0_, ...), custom_call_target="tpu_custom_call" | custom-call | flops 2097152000 | tf_op jit(solution)/shard_map/pallas_call | solution.py:54
  225.0 2.0 convolution_convert_fusion
  227.2 3.3 %collective-permute-start.33 = (bf16[64,2304]{1,0:T(8,128)(2,1)S(1)}, bf16[64,2304]{1,0:T(8,128)(2,1)S(1)}, u32[]{:S(2)}, u32[]{:S(2)}) collective-permute-start(bf16[64,2304]{1,0:T(8,128)(2,1)S(1)} %get-tuple-element.88), channel_id=1, source_target_pairs={{0,6},{1,7},{2,0},{3,1},{4,2},{5,3},{6,4},{7,5},{8,14},{9,15},{10,... | collective-permute-start | bytes 884744 | tf_op jit(solution)/shard_map/ppermute | solution.py:41
  230.5 3.1 %collective-permute-start.36 = (bf16[128,3584]{1,0:T(8,128)(2,1)S(1)}, bf16[128,3584]{1,0:T(8,128)(2,1)S(1)}, u32[]{:S(2)}, u32[]{:S(2)}) collective-permute-start(bf16[128,3584]{1,0:T(8,128)(2,1)S(1)} %slice.136), channel_id=1, source_target_pairs={{0,1},{1,0},{2,3},{3,2},{4,5},{5,4},{6,7},{7,6},{8,9},{9,8},{10,11... | collective-permute-start | bytes 2752520 | tf_op jit(solution)/shard_map/ppermute | solution.py:41
  233.6 3.2 %collective-permute-start.32 = (bf16[64,2304]{1,0:T(8,128)(2,1)S(1)}, bf16[64,2304]{1,0:T(8,128)(2,1)S(1)}, u32[]{:S(2)}, u32[]{:S(2)}) collective-permute-start(bf16[64,2304]{1,0:T(8,128)(2,1)S(1)} %get-tuple-element.87), channel_id=1, source_target_pairs={{0,6},{1,7},{2,0},{3,1},{4,2},{5,3},{6,4},{7,5},{8,14},{9,15},{10,... | collective-permute-start | bytes 884744 | tf_op jit(solution)/shard_map/ppermute | solution.py:41
  237.0 2.9 %collective-permute-start.30 = (bf16[64,2304]{1,0:T(8,128)(2,1)S(1)}, bf16[64,2304]{1,0:T(8,128)(2,1)S(1)}, u32[]{:S(2)}, u32[]{:S(2)}) collective-permute-start(bf16[64,2304]{1,0:T(8,128)(2,1)S(1)} %get-tuple-element.92), channel_id=1, source_target_pairs={{0,2},{1,3},{2,4},{3,5},{4,6},{5,7},{6,0},{7,1},{8,10},{9,11},{10,... | collective-permute-start | bytes 884744 | tf_op jit(solution)/shard_map/ppermute | solution.py:41
  240.6 10.6 %collective-permute-done.36 = bf16[128,3584]{1,0:T(8,128)(2,1)S(1)} collective-permute-done((bf16[128,3584]{1,0:T(8,128)(2,1)S(1)}, bf16[128,3584]{1,0:T(8,128)(2,1)S(1)}, u32[]{:S(2)}, u32[]{:S(2)}) %collective-permute-start.36) | collective-permute-done | bytes 917536 | tf_op jit(solution)/shard_map/ppermute | solution.py:41
  251.6 3.2 %collective-permute-start.39 = (bf16[32,1792]{1,0:T(8,128)(2,1)S(1)}, bf16[32,1792]{1,0:T(8,128)(2,1)S(1)}, u32[]{:S(2)}, u32[]{:S(2)}) collective-permute-start(bf16[32,1792]{1,0:T(8,128)(2,1)S(1)} %get-tuple-element.96), channel_id=1, source_target_pairs={{0,6},{1,7},{2,0},{3,1},{4,2},{5,3},{6,4},{7,5},{8,14},{9,15},{10,... | collective-permute-start | bytes 344072 | tf_op jit(solution)/shard_map/ppermute | solution.py:41
  255.1 2.6 collective-permute-start.35
  258.8 3.5 %collective-permute-start.40 = (bf16[32,3584]{1,0:T(8,128)(2,1)S(1)}, bf16[32,3584]{1,0:T(8,128)(2,1)S(1)}, u32[]{:S(2)}, u32[]{:S(2)}) collective-permute-start(bf16[32,3584]{1,0:T(8,128)(2,1)S(1)} %pad_maximum_fusion.2), channel_id=1, source_target_pairs={{0,6},{1,7},{2,0},{3,1},{4,2},{5,3},{6,4},{7,5},{8,14},{9,15},{10,... | collective-permute-start | bytes 688136 | tf_op jit(solution)/shard_map/ppermute | solution.py:41
  263.5 2.7 %collective-permute-done.38 = bf16[32,3584]{1,0:T(8,128)(2,1)S(1)} collective-permute-done((bf16[32,3584]{1,0:T(8,128)(2,1)S(1)}, bf16[32,3584]{1,0:T(8,128)(2,1)S(1)}, u32[]{:S(2)}, u32[]{:S(2)}) %collective-permute-start.38) | collective-permute-done | bytes 229408 | tf_op jit(solution)/shard_map/ppermute | solution.py:41
  (126 shorter events, 40.6 us)
Async XLA Ops:
  0.0 11.6 %collective-permute-start = (bf16[128,1280]{1,0:T(8,128)(2,1)}, bf16[128,1280]{1,0:T(8,128)(2,1)S(1)}, u32[]{:S(2)}, u32[]{:S(2)}) collective-permute-start(bf16[128,1280]{1,0:T(8,128)(2,1)} %bitcast.28), channel_id=1, source_target_pairs={{0,2},{1,3},{2,4},{3,5},{4,6},{5,7},{6,0},{7,1},{8,10},{9,11},{10,... | collective-permute-start | bytes 983048 | tf_op jit(solution)/shard_map/ppermute | solution.py:41
  1.6 10.0 %collective-permute-start.1 = (bf16[128,1280]{1,0:T(8,128)(2,1)}, bf16[128,1280]{1,0:T(8,128)(2,1)S(1)}, u32[]{:S(2)}, u32[]{:S(2)}) collective-permute-start(bf16[128,1280]{1,0:T(8,128)(2,1)} %bitcast.29), channel_id=1, source_target_pairs={{0,6},{1,7},{2,0},{3,1},{4,2},{5,3},{6,4},{7,5},{8,14},{9,15},{10,... | collective-permute-start | bytes 983048 | tf_op jit(solution)/shard_map/ppermute | solution.py:41
  3.2 11.4 %collective-permute-start.2 = (bf16[128,1280]{1,0:T(8,128)(2,1)}, bf16[128,1280]{1,0:T(8,128)(2,1)S(1)}, u32[]{:S(2)}, u32[]{:S(2)}) collective-permute-start(bf16[128,1280]{1,0:T(8,128)(2,1)} %bitcast.30), channel_id=1, source_target_pairs={{0,1},{1,0},{2,3},{3,2},{4,5},{5,4},{6,7},{7,6},{8,9},{9,8},{10,11... | collective-permute-start | bytes 983048 | tf_op jit(solution)/shard_map/ppermute | solution.py:41
  14.6 9.8 %collective-permute-start.3 = (bf16[128,1280]{1,0:T(8,128)(2,1)S(1)}, bf16[128,1280]{1,0:T(8,128)(2,1)S(1)}, u32[]{:S(2)}, u32[]{:S(2)}) collective-permute-start(bf16[128,1280]{1,0:T(8,128)(2,1)S(1)} %collective-permute-done.refs_1_.refs_5_), channel_id=1, source_target_pairs={{0,1},{1,0},{2,3},{3,2},{4,5},{5,4},{6,7},{7,6},{8,9},{9,8},{10,11... | collective-permute-start | bytes 983048 | tf_op jit(solution)/shard_map/ppermute | solution.py:41
  17.8 9.6 %collective-permute-start.5 = (bf16[128,1280]{1,0:T(8,128)(2,1)S(1)}, bf16[128,1280]{1,0:T(8,128)(2,1)S(1)}, u32[]{:S(2)}, u32[]{:S(2)}) collective-permute-start(bf16[128,1280]{1,0:T(8,128)(2,1)S(1)} %collective-permute-done.refs_1_.refs_5_), channel_id=1, source_target_pairs={{0,2},{1,3},{2,4},{3,5},{4,6},{5,7},{6,0},{7,1},{8,10},{9,11},{10,... | collective-permute-start | bytes 983048 | tf_op jit(solution)/shard_map/ppermute | solution.py:41
  18.1 15.2 %collective-permute-start.7 = (bf16[128,1280]{1,0:T(8,128)(2,1)S(1)}, bf16[128,1280]{1,0:T(8,128)(2,1)S(1)}, u32[]{:S(2)}, u32[]{:S(2)}) collective-permute-start(bf16[128,1280]{1,0:T(8,128)(2,1)S(1)} %collective-permute-done.2.refs_3_.refs_7_), channel_id=1, source_target_pairs={{0,6},{1,7},{2,0},{3,1},{4,2},{5,3},{6,4},{7,5},{8,14},{9,15},{10,... | collective-permute-start | bytes 983048 | tf_op jit(solution)/shard_map/ppermute | solution.py:41
  24.5 10.2 %collective-permute-start.4 = (bf16[64,1280]{1,0:T(8,128)(2,1)S(1)}, bf16[64,1280]{1,0:T(8,128)(2,1)S(1)}, u32[]{:S(2)}, u32[]{:S(2)}) collective-permute-start(bf16[64,1280]{1,0:T(8,128)(2,1)S(1)} %slice.129), channel_id=1, source_target_pairs={{0,2},{1,3},{2,4},{3,5},{4,6},{5,7},{6,0},{7,1},{8,10},{9,11},{10,... | collective-permute-start | bytes 491528 | tf_op jit(solution)/shard_map/ppermute | solution.py:41
  35.5 10.1 %collective-permute-start.10 = (bf16[160,1024]{1,0:T(8,128)(2,1)S(1)}, bf16[160,1024]{1,0:T(8,128)(2,1)S(1)}, u32[]{:S(2)}, u32[]{:S(2)}) collective-permute-start(bf16[160,1024]{1,0:T(8,128)(2,1)S(1)} %get-tuple-element.57.kv_ref), channel_id=1, source_target_pairs={{0,16},{1,17},{2,18},{3,19},{4,20},{5,21},{6,22},{7,23},{8,24},{9,... | collective-permute-start | bytes 983048 | tf_op jit(solution)/shard_map/ppermute | solution.py:41
  36.6 26.6 %collective-permute-start.8 = (bf16[160,1024]{1,0:T(8,128)(2,1)S(1)}, bf16[160,1024]{1,0:T(8,128)(2,1)S(1)}, u32[]{:S(2)}, u32[]{:S(2)}) collective-permute-start(bf16[160,1024]{1,0:T(8,128)(2,1)S(1)} %get-tuple-element.57.kv_ref), channel_id=1, source_target_pairs={{0,32},{1,33},{2,34},{3,35},{4,36},{5,37},{6,38},{7,39},{8,40},{9,... | collective-permute-start | bytes 983048 | tf_op jit(solution)/shard_map/ppermute | solution.py:41
  38.2 25.1 %collective-permute-start.9 = (bf16[160,1024]{1,0:T(8,128)(2,1)S(1)}, bf16[160,1024]{1,0:T(8,128)(2,1)S(1)}, u32[]{:S(2)}, u32[]{:S(2)}) collective-permute-start(bf16[160,1024]{1,0:T(8,128)(2,1)S(1)} %get-tuple-element.57.kv_ref), channel_id=1, source_target_pairs={{0,96},{1,97},{2,98},{3,99},{4,100},{5,101},{6,102},{7,103},{8,104... | collective-permute-start | bytes 983048 | tf_op jit(solution)/shard_map/ppermute | solution.py:41
  39.9 23.4 %collective-permute-start.12 = (bf16[160,1024]{1,0:T(8,128)(2,1)S(1)}, bf16[160,1024]{1,0:T(8,128)(2,1)S(1)}, u32[]{:S(2)}, u32[]{:S(2)}) collective-permute-start(bf16[160,1024]{1,0:T(8,128)(2,1)S(1)} %slice.131), channel_id=1, source_target_pairs={{0,32},{1,33},{2,34},{3,35},{4,36},{5,37},{6,38},{7,39},{8,40},{9,... | collective-permute-start | bytes 983048 | tf_op jit(solution)/shard_map/ppermute | solution.py:41
  40.3 23.0 %collective-permute-start.13 = (bf16[160,1024]{1,0:T(8,128)(2,1)S(1)}, bf16[160,1024]{1,0:T(8,128)(2,1)S(1)}, u32[]{:S(2)}, u32[]{:S(2)}) collective-permute-start(bf16[160,1024]{1,0:T(8,128)(2,1)S(1)} %slice.131), channel_id=1, source_target_pairs={{0,96},{1,97},{2,98},{3,99},{4,100},{5,101},{6,102},{7,103},{8,104... | collective-permute-start | bytes 983048 | tf_op jit(solution)/shard_map/ppermute | solution.py:41
  45.6 17.7 %collective-permute-start.14 = (bf16[160,1024]{1,0:T(8,128)(2,1)S(1)}, bf16[160,1024]{1,0:T(8,128)(2,1)S(1)}, u32[]{:S(2)}, u32[]{:S(2)}) collective-permute-start(bf16[160,1024]{1,0:T(8,128)(2,1)S(1)} %slice.131), channel_id=1, source_target_pairs={{0,16},{1,17},{2,18},{3,19},{4,20},{5,21},{6,22},{7,23},{8,24},{9,... | collective-permute-start | bytes 983048 | tf_op jit(solution)/shard_map/ppermute | solution.py:41
  63.4 51.3 %collective-permute-start.15 = (bf16[160,2048]{1,0:T(8,128)(2,1)S(1)}, bf16[160,2048]{1,0:T(8,128)(2,1)S(1)}, u32[]{:S(2)}, u32[]{:S(2)}) collective-permute-start(bf16[160,2048]{1,0:T(8,128)(2,1)S(1)} %constant_dynamic-update-slice_fusion), channel_id=1, source_target_pairs={{0,16},{1,17},{2,18},{3,19},{4,20},{5,21},{6,22},{7,23},{8,24},{9,... | collective-permute-start | bytes 1966088 | tf_op jit(solution)/shard_map/ppermute | solution.py:41
  64.4 50.7 %collective-permute-start.17 = (bf16[160,2048]{1,0:T(8,128)(2,1)S(1)}, bf16[160,2048]{1,0:T(8,128)(2,1)S(1)}, u32[]{:S(2)}, u32[]{:S(2)}) collective-permute-start(bf16[160,2048]{1,0:T(8,128)(2,1)S(1)} %constant_dynamic-update-slice_fusion), channel_id=1, source_target_pairs={{0,32},{1,33},{2,34},{3,35},{4,36},{5,37},{6,38},{7,39},{8,40},{9,... | collective-permute-start | bytes 1966088 | tf_op jit(solution)/shard_map/ppermute | solution.py:41
  66.0 50.2 %collective-permute-start.19 = (bf16[160,2048]{1,0:T(8,128)(2,1)S(1)}, bf16[160,2048]{1,0:T(8,128)(2,1)S(1)}, u32[]{:S(2)}, u32[]{:S(2)}) collective-permute-start(bf16[160,2048]{1,0:T(8,128)(2,1)S(1)} %pad_maximum_fusion), channel_id=1, source_target_pairs={{0,96},{1,97},{2,98},{3,99},{4,100},{5,101},{6,102},{7,103},{8,104... | collective-permute-start | bytes 1966088 | tf_op jit(solution)/shard_map/ppermute | solution.py:41
  114.7 48.3 %collective-permute-start.16 = (bf16[160,1024]{1,0:T(8,128)(2,1)S(1)}, bf16[160,1024]{1,0:T(8,128)(2,1)S(1)}, u32[]{:S(2)}, u32[]{:S(2)}) collective-permute-start(bf16[160,1024]{1,0:T(8,128)(2,1)S(1)} %slice.132), channel_id=1, source_target_pairs={{0,32},{1,33},{2,34},{3,35},{4,36},{5,37},{6,38},{7,39},{8,40},{9,... | collective-permute-start | bytes 983048 | tf_op jit(solution)/shard_map/ppermute | solution.py:41
  115.1 47.9 %collective-permute-start.18 = (bf16[160,1024]{1,0:T(8,128)(2,1)S(1)}, bf16[160,1024]{1,0:T(8,128)(2,1)S(1)}, u32[]{:S(2)}, u32[]{:S(2)}) collective-permute-start(bf16[160,1024]{1,0:T(8,128)(2,1)S(1)} %slice.133), channel_id=1, source_target_pairs={{0,16},{1,17},{2,18},{3,19},{4,20},{5,21},{6,22},{7,23},{8,24},{9,... | collective-permute-start | bytes 983048 | tf_op jit(solution)/shard_map/ppermute | solution.py:41
  181.1 11.0 %collective-permute-start.21 = (bf16[160,1024]{1,0:T(8,128)(2,1)S(1)}, bf16[160,1024]{1,0:T(8,128)(2,1)S(1)}, u32[]{:S(2)}, u32[]{:S(2)}) collective-permute-start(bf16[160,1024]{1,0:T(8,128)(2,1)S(1)} %constant_dynamic-update-slice_fusion.2.refs_0_), channel_id=1, source_target_pairs={{0,2},{1,3},{2,4},{3,5},{4,6},{5,7},{6,0},{7,1},{8,10},{9,11},{10,... | collective-permute-start | bytes 983048 | tf_op jit(solution)/shard_map/ppermute | solution.py:41
  182.6 9.5 %collective-permute-start.22 = (bf16[160,1024]{1,0:T(8,128)(2,1)S(1)}, bf16[160,1024]{1,0:T(8,128)(2,1)S(1)}, u32[]{:S(2)}, u32[]{:S(2)}) collective-permute-start(bf16[160,1024]{1,0:T(8,128)(2,1)S(1)} %constant_dynamic-update-slice_fusion.2.refs_0_), channel_id=1, source_target_pairs={{0,6},{1,7},{2,0},{3,1},{4,2},{5,3},{6,4},{7,5},{8,14},{9,15},{10,... | collective-permute-start | bytes 983048 | tf_op jit(solution)/shard_map/ppermute | solution.py:41
  184.4 11.6 %collective-permute-start.23 = (bf16[160,1024]{1,0:T(8,128)(2,1)S(1)}, bf16[160,1024]{1,0:T(8,128)(2,1)S(1)}, u32[]{:S(2)}, u32[]{:S(2)}) collective-permute-start(bf16[160,1024]{1,0:T(8,128)(2,1)S(1)} %constant_dynamic-update-slice_fusion.2.refs_0_), channel_id=1, source_target_pairs={{0,1},{1,0},{2,3},{3,2},{4,5},{5,4},{6,7},{7,6},{8,9},{9,8},{10,11... | collective-permute-start | bytes 983048 | tf_op jit(solution)/shard_map/ppermute | solution.py:41
  196.0 10.1 %collective-permute-start.24 = (bf16[160,1024]{1,0:T(8,128)(2,1)S(1)}, bf16[160,1024]{1,0:T(8,128)(2,1)S(1)}, u32[]{:S(2)}, u32[]{:S(2)}) collective-permute-start(bf16[160,1024]{1,0:T(8,128)(2,1)S(1)} %collective-permute-done.21.refs_1_), channel_id=1, source_target_pairs={{0,1},{1,0},{2,3},{3,2},{4,5},{5,4},{6,7},{7,6},{8,9},{9,8},{10,11... | collective-permute-start | bytes 983048 | tf_op jit(solution)/shard_map/ppermute | solution.py:41
  199.2 9.6 %collective-permute-start.26 = (bf16[160,1024]{1,0:T(8,128)(2,1)S(1)}, bf16[160,1024]{1,0:T(8,128)(2,1)S(1)}, u32[]{:S(2)}, u32[]{:S(2)}) collective-permute-start(bf16[160,1024]{1,0:T(8,128)(2,1)S(1)} %collective-permute-done.21.refs_1_), channel_id=1, source_target_pairs={{0,2},{1,3},{2,4},{3,5},{4,6},{5,7},{6,0},{7,1},{8,10},{9,11},{10,... | collective-permute-start | bytes 983048 | tf_op jit(solution)/shard_map/ppermute | solution.py:41
  199.2 14.4 %collective-permute-start.28 = (bf16[160,1024]{1,0:T(8,128)(2,1)S(1)}, bf16[160,1024]{1,0:T(8,128)(2,1)S(1)}, u32[]{:S(2)}, u32[]{:S(2)}) collective-permute-start(bf16[160,1024]{1,0:T(8,128)(2,1)S(1)} %collective-permute-done.23.refs_3_), channel_id=1, source_target_pairs={{0,6},{1,7},{2,0},{3,1},{4,2},{5,3},{6,4},{7,5},{8,14},{9,15},{10,... | collective-permute-start | bytes 983048 | tf_op jit(solution)/shard_map/ppermute | solution.py:41
  206.1 10.6 %collective-permute-start.25 = (bf16[80,1024]{1,0:T(8,128)(2,1)S(1)}, bf16[80,1024]{1,0:T(8,128)(2,1)S(1)}, u32[]{:S(2)}, u32[]{:S(2)}) collective-permute-start(bf16[80,1024]{1,0:T(8,128)(2,1)S(1)} %slice.134), channel_id=1, source_target_pairs={{0,2},{1,3},{2,4},{3,5},{4,6},{5,7},{6,0},{7,1},{8,10},{9,11},{10,... | collective-permute-start | bytes 491528 | tf_op jit(solution)/shard_map/ppermute | solution.py:41
  227.1 9.7 %collective-permute-start.29 = (bf16[64,2304]{1,0:T(8,128)(2,1)S(1)}, bf16[64,2304]{1,0:T(8,128)(2,1)S(1)}, u32[]{:S(2)}, u32[]{:S(2)}) collective-permute-start(bf16[64,2304]{1,0:T(8,128)(2,1)S(1)} %get-tuple-element.90), channel_id=1, source_target_pairs={{0,2},{1,3},{2,4},{3,5},{4,6},{5,7},{6,0},{7,1},{8,10},{9,11},{10,... | collective-permute-start | bytes 884744 | tf_op jit(solution)/shard_map/ppermute | solution.py:41
  227.2 9.6 %collective-permute-start.33 = (bf16[64,2304]{1,0:T(8,128)(2,1)S(1)}, bf16[64,2304]{1,0:T(8,128)(2,1)S(1)}, u32[]{:S(2)}, u32[]{:S(2)}) collective-permute-start(bf16[64,2304]{1,0:T(8,128)(2,1)S(1)} %get-tuple-element.88), channel_id=1, source_target_pairs={{0,6},{1,7},{2,0},{3,1},{4,2},{5,3},{6,4},{7,5},{8,14},{9,15},{10,... | collective-permute-start | bytes 884744 | tf_op jit(solution)/shard_map/ppermute | solution.py:41
  230.5 20.8 %collective-permute-start.36 = (bf16[128,3584]{1,0:T(8,128)(2,1)S(1)}, bf16[128,3584]{1,0:T(8,128)(2,1)S(1)}, u32[]{:S(2)}, u32[]{:S(2)}) collective-permute-start(bf16[128,3584]{1,0:T(8,128)(2,1)S(1)} %slice.136), channel_id=1, source_target_pairs={{0,1},{1,0},{2,3},{3,2},{4,5},{5,4},{6,7},{7,6},{8,9},{9,8},{10,11... | collective-permute-start | bytes 2752520 | tf_op jit(solution)/shard_map/ppermute | solution.py:41
  233.6 18.0 %collective-permute-start.31 = (bf16[64,2304]{1,0:T(8,128)(2,1)S(1)}, bf16[64,2304]{1,0:T(8,128)(2,1)S(1)}, u32[]{:S(2)}, u32[]{:S(2)}) collective-permute-start(bf16[64,2304]{1,0:T(8,128)(2,1)S(1)} %get-tuple-element.89), channel_id=1, source_target_pairs={{0,2},{1,3},{2,4},{3,5},{4,6},{5,7},{6,0},{7,1},{8,10},{9,11},{10,... | collective-permute-start | bytes 884744 | tf_op jit(solution)/shard_map/ppermute | solution.py:41
  233.6 21.2 %collective-permute-start.32 = (bf16[64,2304]{1,0:T(8,128)(2,1)S(1)}, bf16[64,2304]{1,0:T(8,128)(2,1)S(1)}, u32[]{:S(2)}, u32[]{:S(2)}) collective-permute-start(bf16[64,2304]{1,0:T(8,128)(2,1)S(1)} %get-tuple-element.87), channel_id=1, source_target_pairs={{0,6},{1,7},{2,0},{3,1},{4,2},{5,3},{6,4},{7,5},{8,14},{9,15},{10,... | collective-permute-start | bytes 884744 | tf_op jit(solution)/shard_map/ppermute | solution.py:41
  237.0 17.8 %collective-permute-start.30 = (bf16[64,2304]{1,0:T(8,128)(2,1)S(1)}, bf16[64,2304]{1,0:T(8,128)(2,1)S(1)}, u32[]{:S(2)}, u32[]{:S(2)}) collective-permute-start(bf16[64,2304]{1,0:T(8,128)(2,1)S(1)} %get-tuple-element.92), channel_id=1, source_target_pairs={{0,2},{1,3},{2,4},{3,5},{4,6},{5,7},{6,0},{7,1},{8,10},{9,11},{10,... | collective-permute-start | bytes 884744 | tf_op jit(solution)/shard_map/ppermute | solution.py:41
  239.9 14.9 %collective-permute-start.34 = (bf16[64,2304]{1,0:T(8,128)(2,1)S(1)}, bf16[64,2304]{1,0:T(8,128)(2,1)S(1)}, u32[]{:S(2)}, u32[]{:S(2)}) collective-permute-start(bf16[64,2304]{1,0:T(8,128)(2,1)S(1)} %get-tuple-element.91), channel_id=1, source_target_pairs={{0,6},{1,7},{2,0},{3,1},{4,2},{5,3},{6,4},{7,5},{8,14},{9,15},{10,... | collective-permute-start | bytes 884744 | tf_op jit(solution)/shard_map/ppermute | solution.py:41
  (21 other events, 198.9 us)
